TPU v7x, 32 devices: a whole 2x2x4 slice. The times are simulated.
32 devices in a mesh: wide: 8 (over y, x, core), narrow: 4 (over z).
Axes of the slice: x: 2, y: 2, z: 4, core: 2. Of those that a mesh axis runs over, the one named last changes fastest.
Arguments:
- tokens: bfloat16 [4096, 4096], P(('wide', 'narrow')), may hold values from -6 to 6
- cotangent: bfloat16 [4096, 4096], P(('wide', 'narrow')), may hold values from -6 to 6
- weights: bfloat16 [32, 6, 256, 256], P(('wide', 'narrow')), may hold values from -0.1875 to 0.1875
- block_index: int32 [32, 6], P(('wide', 'narrow')), may hold values from 0 to 15, as said below
- block_counts: int32 [32], P(('wide', 'narrow')), may hold values from 1 to 6, as said below
Outputs:
- mixed: bfloat16 [4096, 4096], P(('wide', 'narrow'))
- grad_tokens: bfloat16 [4096, 4096], P(('wide', 'narrow'))
Inputs may be any that keep to these rules, and one draw needn't show every extreme that they name: `block_index`: each row lists 6 distinct blocks. `block_counts`: slots at or beyond a row's count are unused.
All inputs are finite; a program needn't handle non-finite values.
Results may differ from a plain program's by a relative error of at most 0.008.
Values may be sent and summed in bfloat16 or wider, within the bound.
No kernel may reach another device: no remote copies, remote signals or barrier semaphores. Data moves between devices by JAX's collectives and lax.ppermute only.
A program may use at most 192 MiB of HBM per device.

v0:
```python
import jax
import jax.numpy as jnp
from jax import lax
from jax.sharding import PartitionSpec as P


def from_root(block, axis, source):
    block = jnp.where(lax.axis_index(axis) == source, block, jnp.zeros_like(block))
    return lax.psum(block, axis)


def activate(values):
    return jax.nn.gelu(values, approximate=True)


def body(tokens, cotangent, weights, block_index, block_counts):
    rows_tok, rows_cot = (
        lax.all_gather(tokens, "narrow", axis=0, tiled=True),
        lax.all_gather(cotangent, "narrow", axis=0, tiled=True),
    )
    wide_count = lax.axis_size("wide")

    def receive(section_num, buffers):
        received = (
            from_root(weights, "wide", section_num),
            from_root(block_index, "wide", section_num),
            from_root(block_counts, "wide", section_num),
        )
        return tuple(
            (
                lax.dynamic_update_index_in_dim(buffer, piece[0], section_num, 0)
                for buffer, piece in zip(buffers, received)
            )
        )

    initial = (
        jnp.zeros((wide_count,) + weights.shape[1:], weights.dtype),
        jnp.zeros((wide_count, block_index.shape[1]), jnp.int32),
        jnp.zeros((wide_count,), jnp.int32),
    )
    blocks_all, indices_all, counts_all = lax.fori_loop(0, wide_count, receive, initial)
    half_wide = wide_count // 2
    num_slots = blocks_all.shape[1]
    block_width = blocks_all.shape[2]
    live_mask = (jnp.arange(num_slots)[None, :] < counts_all[:, None]).astype(jnp.bfloat16)
    kept_blocks = blocks_all * live_mask[:, :, None, None]
    num_rows = rows_tok.shape[0]
    num_blocks = rows_tok.shape[1] // block_width
    tok_blocks = rows_tok.reshape(num_rows, num_blocks, block_width)
    cot_blocks = rows_cot.reshape(num_rows, num_blocks, block_width)
    panel_items = (
        kept_blocks[:half_wide],
        indices_all[:half_wide],
        kept_blocks[half_wide:],
        indices_all[half_wide:],
    )
    zeros_acc = jnp.zeros((num_rows, num_blocks, block_width), jnp.float32)

    def forward(running, panel_item):
        w_first, idx_first, w_second, idx_second = panel_item
        picked = jnp.take(tok_blocks, idx_first, axis=1)
        pre_act = jnp.einsum("tjd,jdh->th", picked, w_first, preferred_element_type=jnp.float32)
        act_out = activate(pre_act).astype(jnp.bfloat16)
        running = running.at[:, idx_second].add(
            jnp.einsum("th,jhd->tjd", act_out, w_second, preferred_element_type=jnp.float32)
        )
        return (running, pre_act)

    def backward(running, panel_item):
        w_first, idx_first, w_second, idx_second, pre_act = panel_item
        cot_picked = jnp.take(cot_blocks, idx_second, axis=1)
        grad_act = jnp.einsum(
            "tjd,jhd->th", cot_picked, w_second, preferred_element_type=jnp.float32
        )
        grad_pre = jax.vjp(activate, pre_act)[1](grad_act)[0].astype(jnp.bfloat16)
        running = running.at[:, idx_first].add(
            jnp.einsum("th,jdh->tjd", grad_pre, w_first, preferred_element_type=jnp.float32)
        )
        return (running, None)

    out_acc, pre_stack = lax.scan(forward, zeros_acc, panel_items)
    grad_acc, _ = lax.scan(backward, zeros_acc, panel_items + (pre_stack,))
    out_part = out_acc.reshape(num_rows, -1).astype(jnp.bfloat16)
    grad_part = grad_acc.reshape(num_rows, -1).astype(jnp.bfloat16)
    mixed, grad_tokens = (
        lax.psum_scatter(out_part, "narrow", scatter_dimension=0, tiled=True).astype(jnp.float32),
        lax.psum_scatter(grad_part, "narrow", scatter_dimension=0, tiled=True).astype(jnp.float32),
    )
    return (mixed.astype(jnp.bfloat16), grad_tokens.astype(jnp.bfloat16))


def solution(mesh):
    placed = (
        P(("wide", "narrow"), None),
        P(("wide", "narrow"), None),
        P(("wide", "narrow"), None, None, None),
        P(("wide", "narrow"), None),
        P(("wide", "narrow")),
    )
    return jax.shard_map(
        body,
        mesh=mesh,
        in_specs=placed,
        out_specs=(P(("wide", "narrow"), None), P(("wide", "narrow"), None)),
        check_vma=False,
    )
```

profile of v0, /device:TPU:0, one launch (start us, length us, event | category | flops | bytes accessed | tf_op | source)
XLA Modules:
  0.0 832.8 jit_solution(13676505129722302704)
XLA Ops:
  10.3 494.1 %while.41 = (s32[]{:T(128)}, bf16[8,6,256,256]{3,2,1,0:T(8,128)(2,1)}, s32[8,6]{1,0:T(8,128)S(1)}, s32[8]{0:T(128)S(1)}, bf16[1,6,256,256]{3,2,1,0:T(8,128)(2,1)...) while((s32[]{:T(128)}, ...), condition=%wide.region_4.5_spmd, body=%wide.region_0.4_spmd.sunk | while | flops 786452 | bytes 7864713 | solution.py:41
  13.8 8.2 all-reduce.2
  22.7 50.4 %all-reduce.5.cloned.1.call-done = bf16[1,6,256,256]{3,2,1,0:T(8,128)(2,1)} async-done(((bf16[1,6,256,256]{3,2,1,0:T(8,128)(2,1)}), bf16[1,6,256,256]{3,2,1,0:T(8,128)(2,1)}) %all-reduce.5.cloned.1.call-update) | async-done | bytes 786448 | tf_op jit(solution)/shard_map/while/body/eval_jaxpr/psum | solution.py:9
  76.8 7.2 all-reduce.2
  84.7 49.8 %all-reduce.5.cloned.1.call-done = bf16[1,6,256,256]{3,2,1,0:T(8,128)(2,1)} async-done(((bf16[1,6,256,256]{3,2,1,0:T(8,128)(2,1)}), bf16[1,6,256,256]{3,2,1,0:T(8,128)(2,1)}) %all-reduce.5.cloned.1.call-update) | async-done | bytes 786448 | tf_op jit(solution)/shard_map/while/body/eval_jaxpr/psum | solution.py:9
  138.3 7.8 all-reduce.2
  146.8 49.1 %all-reduce.5.cloned.1.call-done = bf16[1,6,256,256]{3,2,1,0:T(8,128)(2,1)} async-done(((bf16[1,6,256,256]{3,2,1,0:T(8,128)(2,1)}), bf16[1,6,256,256]{3,2,1,0:T(8,128)(2,1)}) %all-reduce.5.cloned.1.call-update) | async-done | bytes 786448 | tf_op jit(solution)/shard_map/while/body/eval_jaxpr/psum | solution.py:9
  199.7 7.2 all-reduce.2
  207.6 49.5 %all-reduce.5.cloned.1.call-done = bf16[1,6,256,256]{3,2,1,0:T(8,128)(2,1)} async-done(((bf16[1,6,256,256]{3,2,1,0:T(8,128)(2,1)}), bf16[1,6,256,256]{3,2,1,0:T(8,128)(2,1)}) %all-reduce.5.cloned.1.call-update) | async-done | bytes 786448 | tf_op jit(solution)/shard_map/while/body/eval_jaxpr/psum | solution.py:9
  260.8 8.9 %all-reduce.2 = (s32[1,6]{1,0:T(1,128)S(1)}, s32[1]{0:T(128)}) all-reduce(s32[1,6]{1,0:T(1,128)S(1)} %broadcast_select_fusion.5, s32[1]{0:T(128)S(6)} %select_n.151), channel_id=1, replica_groups=mesh['wide'=8,'narrow'=4] {'wide'}, use_global_device_ids=true, to_apply=%region_2.2 | all-reduce | flops 7 | bytes 56 | tf_op jit(solution)/shard_map/while/body/eval_jaxpr/psum | solution.py:9
  270.5 47.7 %all-reduce.5.cloned.1.call-done = bf16[1,6,256,256]{3,2,1,0:T(8,128)(2,1)} async-done(((bf16[1,6,256,256]{3,2,1,0:T(8,128)(2,1)}), bf16[1,6,256,256]{3,2,1,0:T(8,128)(2,1)}) %all-reduce.5.cloned.1.call-update) | async-done | bytes 786448 | tf_op jit(solution)/shard_map/while/body/eval_jaxpr/psum | solution.py:9
  322.0 7.2 all-reduce.2
  329.9 49.5 %all-reduce.5.cloned.1.call-done = bf16[1,6,256,256]{3,2,1,0:T(8,128)(2,1)} async-done(((bf16[1,6,256,256]{3,2,1,0:T(8,128)(2,1)}), bf16[1,6,256,256]{3,2,1,0:T(8,128)(2,1)}) %all-reduce.5.cloned.1.call-update) | async-done | bytes 786448 | tf_op jit(solution)/shard_map/while/body/eval_jaxpr/psum | solution.py:9
  383.1 8.5 %all-reduce.2 = (s32[1,6]{1,0:T(1,128)S(1)}, s32[1]{0:T(128)}) all-reduce(s32[1,6]{1,0:T(1,128)S(1)} %broadcast_select_fusion.5, s32[1]{0:T(128)S(6)} %select_n.151), channel_id=1, replica_groups=mesh['wide'=8,'narrow'=4] {'wide'}, use_global_device_ids=true, to_apply=%region_2.2 | all-reduce | flops 7 | bytes 56 | tf_op jit(solution)/shard_map/while/body/eval_jaxpr/psum | solution.py:9
  392.4 48.5 %all-reduce.5.cloned.1.call-done = bf16[1,6,256,256]{3,2,1,0:T(8,128)(2,1)} async-done(((bf16[1,6,256,256]{3,2,1,0:T(8,128)(2,1)}), bf16[1,6,256,256]{3,2,1,0:T(8,128)(2,1)}) %all-reduce.5.cloned.1.call-update) | async-done | bytes 786448 | tf_op jit(solution)/shard_map/while/body/eval_jaxpr/psum | solution.py:9
  444.5 7.2 all-reduce.2
  452.4 49.8 %all-reduce.5.cloned.1.call-done = bf16[1,6,256,256]{3,2,1,0:T(8,128)(2,1)} async-done(((bf16[1,6,256,256]{3,2,1,0:T(8,128)(2,1)}), bf16[1,6,256,256]{3,2,1,0:T(8,128)(2,1)}) %all-reduce.5.cloned.1.call-update) | async-done | bytes 786448 | tf_op jit(solution)/shard_map/while/body/eval_jaxpr/psum | solution.py:9
  506.5 3.3 broadcast_multiply_fusion
  509.7 3.1 fusion.90
  512.8 73.8 %all-gather.3.cloned.1.call-done = bf16[512,4096]{0,1:T(8,128)(2,1)} async-done(((bf16[128,4096]{0,1:T(8,128)(2,1)}), bf16[512,4096]{0,1:T(8,128)(2,1)}) %all-gather.3.cloned.1.call-update) | async-done | bytes 4194320 | tf_op jit(solution)/shard_map/all_gather | solution.py:18
  586.6 6.4 copy.14
  593.1 4.1 broadcast_in_dim.36.clone
  597.1 59.4 %while.42 = (s32[]{:T(128)}, f32[512,16,256]{2,0,1:T(8,128)}, f32[4,512,256]{2,1,0:T(8,128)}, s32[4,6]{1,0:T(4,128)S(1)}, s32[4,6]{1,0:T(4,128)S(1)}, /*index=5*...) while((s32[]{:T(128)}, f32[512,16,256]{2,0,1:T(8,128)}, ...), condition=%wide.region_7.9_spmd, body=%wide.region_5.8_spmd.sunk | while | flops 808059968 | bytes 20452644 | solution.py:81
  597.2 2.9 gather_fusion
  604.4 7.7 scatter_fusion
  612.1 2.9 gather_fusion
  619.3 7.6 scatter_fusion
  634.1 7.6 scatter_fusion
  648.9 7.7 scatter_fusion
  656.6 3.9 convert_bitcast_fusion.1
  663.1 4.2 all-gather.5.cloned.1.call-done
  667.3 6.3 copy.17
  673.6 4.1 broadcast_in_dim.36
  677.7 63.3 %while.43 = (s32[]{:T(128)}, f32[512,16,256]{2,0,1:T(8,128)}, s32[4,6]{1,0:T(4,128)S(1)}, s32[4,6]{1,0:T(4,128)S(1)}, bf16[512,16,256]{2,0,1:T(8,128)(2,1)}, /*i...) while((s32[]{:T(128)}, f32[512,16,256]{2,0,1:T(8,128)}, ...), condition=%wide.region_11.13_spmd, body=%wide.region_9.12_spmd.sunk | while | flops 809501760 | bytes 19404576 | solution.py:82
  677.7 4.1 gather_fusion.1
  681.8 4.0 convolution_bitcast_fusion.5
  685.8 7.6 scatter_fusion.1
  693.5 4.2 gather_fusion.1
  697.6 4.0 convolution_bitcast_fusion.5
  701.6 7.8 scatter_fusion.1
  709.5 4.1 gather_fusion.1
  713.6 4.1 convolution_bitcast_fusion.5
  717.6 7.6 scatter_fusion.1
  725.2 4.1 gather_fusion.1
  729.3 4.0 convolution_bitcast_fusion.5
  733.3 7.7 scatter_fusion.1
  741.0 3.9 convert_bitcast_fusion
  747.5 77.7 %reduce-scatter.5.cloned.1.call-done = bf16[128,4096]{1,0:T(8,128)(2,1)} async-done(((bf16[512,4096]{1,0:T(8,128)(2,1)}), bf16[128,4096]{1,0:T(8,128)(2,1)}) %reduce-scatter.5.cloned.1.call-update) | async-done | bytes 1048592 | tf_op jit(solution)/shard_map/reduce_scatter | solution.py:87
  (111 shorter events, 64.8 us)
Async XLA Ops:
  10.3 494.7 %copy-start = (bf16[128,4096]{1,0:T(8,128)(2,1)S(1)}, bf16[128,4096]{1,0:T(8,128)(2,1)}, u32[]{:S(2)}) copy-start(bf16[128,4096]{1,0:T(8,128)(2,1)} %param.14) | copy-start | bytes 3145732
  10.3 62.8 %all-reduce.5.cloned.1.call-start = ((), (), s32[]{:S(2)}) async-start(), calls=%async_computation.6 | async-start | bytes 1572864 | tf_op jit(solution)/shard_map/while/body/eval_jaxpr/psum | solution.py:9
  75.2 59.4 %all-reduce.5.cloned.1.call-start = ((), (), s32[]{:S(2)}) async-start(), calls=%async_computation.6 | async-start | bytes 1572864 | tf_op jit(solution)/shard_map/while/body/eval_jaxpr/psum | solution.py:9
  136.6 59.4 %all-reduce.5.cloned.1.call-start = ((), (), s32[]{:S(2)}) async-start(), calls=%async_computation.6 | async-start | bytes 1572864 | tf_op jit(solution)/shard_map/while/body/eval_jaxpr/psum | solution.py:9
  198.1 59.1 %all-reduce.5.cloned.1.call-start = ((), (), s32[]{:S(2)}) async-start(), calls=%async_computation.6 | async-start | bytes 1572864 | tf_op jit(solution)/shard_map/while/body/eval_jaxpr/psum | solution.py:9
  259.2 59.1 %all-reduce.5.cloned.1.call-start = ((), (), s32[]{:S(2)}) async-start(), calls=%async_computation.6 | async-start | bytes 1572864 | tf_op jit(solution)/shard_map/while/body/eval_jaxpr/psum | solution.py:9
  320.3 59.1 %all-reduce.5.cloned.1.call-start = ((), (), s32[]{:S(2)}) async-start(), calls=%async_computation.6 | async-start | bytes 1572864 | tf_op jit(solution)/shard_map/while/body/eval_jaxpr/psum | solution.py:9
  381.5 59.4 %all-reduce.5.cloned.1.call-start = ((), (), s32[]{:S(2)}) async-start(), calls=%async_computation.6 | async-start | bytes 1572864 | tf_op jit(solution)/shard_map/while/body/eval_jaxpr/psum | solution.py:9
  442.9 59.4 %all-reduce.5.cloned.1.call-start = ((), (), s32[]{:S(2)}) async-start(), calls=%async_computation.6 | async-start | bytes 1572864 | tf_op jit(solution)/shard_map/while/body/eval_jaxpr/psum | solution.py:9
  504.4 82.3 %all-gather.3.cloned.1.call-start = ((), (), s32[]{:S(2)}) async-start(), calls=%async_computation.2 | async-start | bytes 5242880 | tf_op jit(solution)/shard_map/all_gather | solution.py:18
  504.9 162.3 %all-gather.5.cloned.1.call-start = ((), (), s32[]{:S(2)}) async-start(), calls=%async_computation.4 | async-start | bytes 5242880 | tf_op jit(solution)/shard_map/all_gather | solution.py:19
  506.3 241.2 %reduce-scatter.3.cloned.1.call-start = ((), (), s32[]{:S(2)}) async-start(), calls=%async_computation.3 | async-start | bytes 5242880 | tf_op jit(solution)/shard_map/reduce_scatter | solution.py:86
  663.0 162.2 %reduce-scatter.5.cloned.1.call-start = ((), (), s32[]{:S(2)}) async-start(), calls=%async_computation.5 | async-start | bytes 5242880 | tf_op jit(solution)/shard_map/reduce_scatter | solution.py:87
Sparse Core Ops, SparseCore 0:
  14.8 58.2 all-reduce.4
  79.7 54.7 all-reduce.4
  141.2 54.7 all-reduce.4
  202.3 54.7 all-reduce.4
  263.4 54.7 all-reduce.4
  324.6 54.7 all-reduce.4
  386.0 54.7 all-reduce.4
  447.4 54.7 all-reduce.4
Sparse Core Ops, SparseCore 1:
  507.0 79.6 all-gather.2
  588.6 78.6 all-gather.4
  670.0 74.9 reduce-scatter.2
  748.0 77.2 reduce-scatter.4
where the time goes:
time: 835 us; the launch traced here: 833 us
  waiting for transfers between devices  551 us (66%)
  local copies, waits for them, and re-layouts  83.2 us (10%)
  other arithmetic  82.1 us (10%)
  blocking collectives  62.1 us (7%)
  matrix products  33.1 us (4%)
  between operations  15.7 us (2%)
    psum x8, waiting for transfers between devices, from_root(): return lax.psum(block, axis)  394 us
    reduce_scatter x1, waiting for transfers between devices, body(): lax.psum_scatter(grad_part, 'narrow', scatter_dimension=0, tiled=True)  77.7 us
    all_gather x1, waiting for transfers between devices, body(): lax.all_gather(tokens, 'narrow', axis=0, tiled=True)  73.8 us
    psum x8, blocking collectives, from_root(): return lax.psum(block, axis)  62.1 us
    scatter-add x4, other arithmetic, backward(): running.at[:, idx_first]  30.8 us
    scatter-add x4, other arithmetic, forward(): running.at[:, idx_second]  30.6 us
    dynamic_update_slice x24, local copies, waits for them, and re-layouts, receive(): lax.dynamic_update_index_in_dim(buffer, piece[0], section_num, 0)  22.7 us
  transfers between devices with their start and end apart: 12, of which 11 were waited for; matrix products, arithmetic and copies ran while one was open for 21% of the time, Pallas kernels for 0%

commit v1 on v0

v1 whole, which is shorter than its diff:
```python
import functools

import jax
import jax.numpy as jnp
from jax import lax
from jax.experimental import pallas as pl
from jax.experimental.pallas import tpu as pltpu
from jax.sharding import PartitionSpec as P

ROOT_2_OVER_PI = 0.7978845608028654
CUBIC = 0.044715
BOTH = ("wide", "narrow")
VMEM_LIMIT = 32 * 1024 * 1024
PAIRS_VMEM_LIMIT = 16 * 1024 * 1024

ENDS = [(0, 1), (1, 0), (2, 3), (3, 2)]
MIDDLE = [(1, 2), (2, 1)]
OUTWARD = [(1, 0), (2, 3)]


def gelu_and_slope(v):
    inner = ROOT_2_OVER_PI * (v + CUBIC * (v * v * v))
    t = jnp.tanh(inner)
    cdf = 0.5 * (1.0 + t)
    slope = cdf + (0.5 * v) * (1.0 - t * t) * (ROOT_2_OVER_PI * (1.0 + (3.0 * CUBIC) * (v * v)))
    return v * cdf, slope


def dot_plain(a, b):
    return lax.dot_general(a, b, (((1,), (0,)), ((), ())), preferred_element_type=jnp.float32)


def dot_turned(a, b):
    return lax.dot_general(a, b, (((1,), (1,)), ((), ())), preferred_element_type=jnp.float32)


def lanes(index, width):
    return pl.ds(pl.multiple_of(index * width, width), width)


def run_panel(meta, row1, row2, slots, width, toks, cots, w1, w2, out_accs, grad_accs):
    count1, count2 = meta[row1, slots], meta[row2, slots]

    def kept(parts, row, count, j):
        at = lanes(meta[row, j], width)
        value = jnp.concatenate([part[:, at] for part in parts], axis=0)
        return value if j == 0 else jnp.where(j < count, value, jnp.zeros_like(value))

    pre = dot_plain(kept(toks, row1, count1, 0), w1(0))
    gact = dot_turned(kept(cots, row2, count2, 0), w2(0))
    for j in range(1, slots):
        pre = pre + dot_plain(kept(toks, row1, count1, j), w1(j))
    for j in range(1, slots):
        gact = gact + dot_turned(kept(cots, row2, count2, j), w2(j))
    act, slope = gelu_and_slope(pre)
    act = act.astype(jnp.bfloat16)
    gpre = (gact * slope).astype(jnp.bfloat16)
    zero = jnp.zeros_like(act)

    def add(accs, block, value):
        at = 0
        for acc in accs:
            rows = acc.shape[0]
            acc[:, lanes(block, width)] += value[at : at + rows]
            at += rows

    for j in range(slots):
        add(out_accs, meta[row2, j], dot_plain(jnp.where(j < count2, act, zero), w2(j)))
    for j in range(slots):
        add(grad_accs, meta[row1, j], dot_turned(jnp.where(j < count1, gpre, zero), w1(j)))


def pairs_kernel(plan, *refs):
    pairs, spans, starts, rounds, slots, width = (
        plan["pairs"], plan["spans"], plan["starts"], plan["rounds"], plan["slots"], plan["width"],
    )
    n, parts = len(pairs), len(spans)
    refs = list(refs)

    def take(count):
        taken = refs[:count]
        del refs[:count]
        return taken

    pos, meta = take(2)
    fed = take(3 if starts else 2)
    held = [[take(k) for k in counts] for _, _, counts in pairs]
    if starts:
        tok, cot = take(2)
    else:
        tok, cot = fed
        take(2 * parts)
    sums = take(2 * parts)
    rounded = take(2 * parts if rounds else 0)
    blocks, block_sem = take(2)
    low, z = pos[0], pos[1]
    middle = (z == 1) | (z == 2)

    feeding = []
    if starts:
        own_tok, own_cot, other = fed
        rows = own_tok.shape[0]
        first, second = pl.ds(0, rows), pl.ds(rows, rows)
        feeding = [
            pltpu.make_async_copy(src, dst, refs[0].at[k])
            for k, (src, dst) in enumerate((
                (own_tok, tok.at[first]), (other.at[first], tok.at[second]),
                (own_cot, cot.at[first]), (other.at[second], cot.at[second]),
            ))
        ]
    for copy in feeding:
        copy.start()

    def block_copy(k, side, source):
        return pltpu.make_async_copy(source.at[0], blocks.at[k, side], block_sem.at[k, side])

    def begin(k, side):
        for which in range(2):
            choice = held[k][which]
            here = low == (1 if which == side else 0)
            for pick, source in enumerate(choice):
                wanted = here
                if len(choice) == 2:
                    wanted = here & (middle if pick == 0 else jnp.logical_not(middle))
                pl.when(wanted)(lambda source=source: block_copy(k, side, source).start())

    for k in range(n):
        begin(k, 0)
        begin(k, 1)
    if starts:
        for total in sums:
            total[...] = jnp.zeros_like(total)
    for copy in feeding:
        copy.wait()
    toks = [tok.at[pl.ds(at, size)] for at, size in spans]
    cots = [cot.at[pl.ds(at, size)] for at, size in spans]
    for k, (flip, kind, _) in enumerate(pairs):
        there = {
            "own": z,
            "near": z ^ 1,
            "third": jnp.where(z < 2, 2, 1),
            "last": jnp.where(z < 2, 3, 0),
        }[kind]
        for side in range(2):
            block_copy(k, side, held[k][side][0]).wait()
        at = (z ^ there) * 4 + 2 * flip
        run_panel(
            meta, at + 1 - low, at + low, slots, width, toks, cots,
            lambda j, k=k: blocks[k, 0, j], lambda j, k=k: blocks[k, 1, j],
            sums[:parts], sums[parts:],
        )
    for total, out in zip(sums, rounded):
        out[...] = total[...].astype(out.dtype)


def run_pairs(pos, meta, fed, items, spans, accs, rounds, sizes):
    slots, width = sizes
    parts, n = len(spans), len(items)
    starts = accs is None
    model = fed[0].shape[1]
    plan = dict(
        pairs=[(flip, kind, (len(first), len(second))) for flip, kind, first, second in items],
        spans=spans, starts=starts, rounds=rounds, slots=slots, width=width,
    )
    smem = pl.BlockSpec(memory_space=pltpu.SMEM)
    vmem = pl.BlockSpec(memory_space=pltpu.VMEM)
    hbm = pl.BlockSpec(memory_space=pl.ANY)

    def off_chip(value):
        return pltpu.with_memory_space_constraint(value, pltpu.HBM)

    blocks = [off_chip(a) for item in items for choice in item[2:] for a in choice]
    if starts:
        fed = [off_chip(value) for value in fed]
    operands = [pos, meta, *fed, *blocks, *(accs or [])]
    first_acc = len(operands) - 2 * parts
    out_shape = [jax.ShapeDtypeStruct((size, model), jnp.float32) for _, size in spans] * 2
    if rounds:
        out_shape += [jax.ShapeDtypeStruct((size, model), jnp.bfloat16) for _, size in spans] * 2
    rows = sum(size for _, size in spans)
    scratch = [pltpu.VMEM((n, 2, slots, width, width), jnp.bfloat16), pltpu.SemaphoreType.DMA((n, 2))]
    if starts:
        out_shape = [jax.ShapeDtypeStruct((rows, model), jnp.bfloat16)] * 2 + out_shape
        scratch += [pltpu.SemaphoreType.DMA((4,))]
    outs = pl.pallas_call(
        functools.partial(pairs_kernel, plan),
        out_shape=out_shape,
        in_specs=[smem, smem] + [hbm if starts else vmem] * len(fed) + [hbm] * len(blocks) + [vmem] * len(accs or []),
        out_specs=[vmem] * len(out_shape),
        scratch_shapes=scratch,
        input_output_aliases={} if starts else {first_acc + i: i for i in range(2 * parts)},
        compiler_params=pltpu.CompilerParams(vmem_limit_bytes=PAIRS_VMEM_LIMIT),
        cost_estimate=pl.CostEstimate(
            flops=n * 4 * slots * 2 * rows * width * width,
            transcendentals=n * rows * width,
            bytes_accessed=2 * n * slots * width * width * 2,
        ),
    )(*operands)
    return (outs[:2] if starts else fed), outs[-2 * parts :]


def all_panels_kernel(slots, width, half, meta, tok, cot, held, out, grad, blocks, out_acc, grad_acc, sem):
    def copies(p, buf):
        return [
            pltpu.make_async_copy(held.at[p], blocks.at[buf, 0], sem.at[buf, 0]),
            pltpu.make_async_copy(held.at[half + p], blocks.at[buf, 1], sem.at[buf, 1]),
        ]

    out_acc[...] = jnp.zeros_like(out_acc)
    grad_acc[...] = jnp.zeros_like(grad_acc)
    for copy in copies(0, 0):
        copy.start()

    def step(p, _):
        buf = lax.rem(p, 2)

        @pl.when(p + 1 < half)
        def _():
            for copy in copies(p + 1, 1 - buf):
                copy.start()

        for copy in copies(p, buf):
            copy.wait()
        run_panel(
            meta, p, half + p, slots, width, [tok], [cot],
            lambda j: blocks[buf, 0, j], lambda j: blocks[buf, 1, j], [out_acc], [grad_acc],
        )
        return 0

    lax.fori_loop(0, half, step, 0)
    out[...] = out_acc[...].astype(out.dtype)
    grad[...] = grad_acc[...].astype(grad.dtype)


def run_all(meta, tokens, cotangent, gathered):
    count, slots, width, _ = gathered.shape
    rows, model = tokens.shape
    vmem = pl.BlockSpec(memory_space=pltpu.VMEM)
    return pl.pallas_call(
        functools.partial(all_panels_kernel, slots, width, count // 2),
        out_shape=[jax.ShapeDtypeStruct((rows, model), jnp.bfloat16)] * 2,
        in_specs=[pl.BlockSpec(memory_space=pltpu.SMEM), vmem, vmem, pl.BlockSpec(memory_space=pl.ANY)],
        out_specs=[vmem] * 2,
        scratch_shapes=[
            pltpu.VMEM((2, 2, slots, width, width), jnp.bfloat16),
            pltpu.VMEM((rows, model), jnp.float32),
            pltpu.VMEM((rows, model), jnp.float32),
            pltpu.SemaphoreType.DMA((2, 2)),
        ],
        compiler_params=pltpu.CompilerParams(vmem_limit_bytes=VMEM_LIMIT),
    )(meta, tokens, cotangent, gathered)


def together(*values):
    return lax.optimization_barrier(values)


def exchange_plan(wide, narrow):
    return wide == 8 and narrow == 4


def body(tokens, cotangent, weights, block_index, block_counts):
    wide, narrow = lax.axis_size("wide"), lax.axis_size("narrow")
    slots, width = weights.shape[1], weights.shape[2]
    own_meta = jnp.concatenate([block_index, block_counts[:, None]], axis=1)
    if not exchange_plan(wide, narrow):
        meta = lax.all_gather(own_meta, BOTH, axis=0, tiled=True)
        gathered = lax.all_gather(weights, BOTH, axis=0, tiled=True)
        return tuple(run_all(meta, tokens, cotangent, gathered))

    def across(value, bit):
        return lax.ppermute(value, "wide", [(i, i ^ bit) for i in range(wide)])

    core, x, y = (functools.partial(across, bit=bit) for bit in (1, 2, 4))

    def line(value, pairs):
        return lax.ppermute(value, "narrow", pairs)

    w, z = lax.axis_index("wide"), lax.axis_index("narrow")
    pos = jnp.stack([(w < wide // 2).astype(jnp.int32), z.astype(jnp.int32)])
    mid = (z == 1) | (z == 2)
    run = functools.partial(run_pairs, sizes=(slots, width))

    def doubled(table, moved):
        return jnp.concatenate([table, moved], axis=0)

    own = weights
    x_own, y_own, near, beyond = x(own), y(own), line(own, ENDS), line(own, MIDDLE)
    meta = doubled(own_meta, y(own_meta))
    both = jnp.concatenate([tokens, cotangent], axis=0)

    x_own, y_own, near, beyond, meta, both = together(x_own, y_own, near, beyond, meta, both)
    x_near, y_near, out1, in1 = x(near), y(near), line(beyond, OUTWARD), line(near, MIDDLE)
    meta = doubled(meta, x(meta))

    x_near, y_near, out1, in1, y_own, meta, both = together(x_near, y_near, out1, in1, y_own, meta, both)
    third = jnp.where(mid, beyond, out1)
    xy_own, y_third, out2 = x(y_own), y(third), line(in1, OUTWARD)
    meta = doubled(meta, line(meta, ENDS))
    both_other = core(both)

    xy_own, y_third, out2, meta, both_other = together(xy_own, y_third, out2, meta, both_other)
    last = jnp.where(mid, in1, out2)
    x_last, y_last, xy_near, xy_beyond = x(last), y(last), line(xy_own, ENDS), line(xy_own, MIDDLE)
    meta = doubled(meta, line(meta, [(i, i ^ 2) for i in range(narrow)]))

    x_last, y_last, xy_near, xy_beyond, third, meta = together(x_last, y_last, xy_near, xy_beyond, third, meta)
    x_third, xy_last, out3 = x(third), y(x_last), line(xy_beyond, OUTWARD)
    rows = tokens.shape[0]
    mine, others = (0, rows), (rows, rows)
    fed, accs = run(pos, meta, [tokens, cotangent, both_other], [
        (0, "own", [own], [y_own]), (0, "near", [near], [y_near]), (1, "own", [x_own], [xy_own]),
    ], [mine, others], None, False)
    fed, accs = run(pos, meta, fed, [
        (0, "third", [third], [y_third]), (1, "near", [x_near], [xy_near]), (0, "last", [last], [y_last]),
    ], [mine, others], accs, False)

    ending = [(1, "last", [x_last], [xy_last]), (1, "third", [x_third], [xy_beyond, out3])]
    _, sent = run(pos, meta, fed, ending, [others], [accs[1], accs[3]], True)
    got = [core(part) for part in sent]
    _, kept = run(pos, meta, fed, ending, [mine], [accs[0], accs[2]], False)
    return tuple(
        (total + other.astype(jnp.float32)).astype(jnp.bfloat16) for total, other in zip(kept, got)
    )


def solution(mesh):
    rows = P(BOTH, None)
    return jax.shard_map(
        body,
        mesh=mesh,
        in_specs=(rows, rows, P(BOTH, None, None, None), rows, P(BOTH)),
        out_specs=(rows, rows),
        check_vma=False,
    )
```

time: 835 us -> 129 us (0.15)
  waiting for transfers between devices: 551 us -> 66.8 us
  local copies, waits for them, and re-layouts: 83.2 us -> 1.76 us
  other arithmetic: 82.1 us -> 6.36 us
  blocking collectives: 62.1 us -> 0 us
  matrix products: 33.1 us -> 0 us
  starting transfers between devices: 0.15 us -> 30.7 us
  Pallas kernels: 0 us -> 21.9 us
  between operations: 15.7 us -> 1.64 us
    psum x8 -> x0, waiting for transfers between devices: 394 us -> none  [from_root(): return lax.psum(block, axis)]
    all_gather x2 -> x0, waiting for transfers between devices: 78 us -> none  [the longest x1 73.8 us: body(): lax.all_gather(tokens, 'narrow', axis=0, tiled=True)]
    reduce_scatter x2 -> x0, waiting for transfers between devices: 77.7 us -> none  [the longest x1 77.7 us: body(): lax.psum_scatter(grad_part, 'narrow', scatter_dimension=0, tiled=True)]
    ppermute x0 -> x25, waiting for transfers between devices: none -> 66.8 us  [the longest x10 41.5 us: line(): return lax.ppermute(value, 'narrow', pairs)]
    psum x8 -> x0, blocking collectives: 62.1 us -> none  [from_root(): return lax.psum(block, axis)]
    scatter-add x8 -> x0, other arithmetic: 61.3 us -> none  [the longest x4 30.8 us: backward(): running.at[:, idx_first]]
    dot_general x12 -> x0, matrix products: 33.1 us -> none  [the longest x4 16 us: backward(): jnp.einsum('th,jdh->tjd', grad_pre, w_first, preferred_element_type=jnp.f...]
    ppermute x0 -> x25, starting transfers between devices: none -> 30.7 us  [the longest x15 15.5 us: across(): return lax.ppermute(value, 'wide', [(i, i ^ bit) for i in range(wide)])]
  transfers between devices with their start and end apart: 12 -> 25, of which waited for: 11 -> 8; matrix products, arithmetic and copies ran while one was open for 21% -> 4% of each run, Pallas kernels for 0% -> 14%
where the time goes in v1:
time: 129 us
  waiting for transfers between devices  66.8 us (52%)
  starting transfers between devices  30.7 us (24%)
  Pallas kernels  21.9 us (17%)
  other arithmetic  6.36 us (5%)
  local copies, waits for them, and re-layouts  1.76 us (1%)
  between operations  1.64 us (1%)
    ppermute x10, waiting for transfers between devices, line(): return lax.ppermute(value, 'narrow', pairs)  41.5 us
    ppermute x15, waiting for transfers between devices, across(): return lax.ppermute(value, 'wide', [(i, i ^ bit) for i in range(wide)])  25.4 us
    pallas_call x4, Pallas kernels, run_pairs(): pl.pallas_call(functools.partial(pairs_kernel, plan), out_shape=out_shape...  21.9 us
    ppermute x15, starting transfers between devices, across(): return lax.ppermute(value, 'wide', [(i, i ^ bit) for i in range(wide)])  15.5 us
    ppermute x10, starting transfers between devices, line(): return lax.ppermute(value, 'narrow', pairs)  15.2 us
  transfers between devices with their start and end apart: 25, of which 8 were waited for; matrix products, arithmetic and copies ran while one was open for 4% of the time, Pallas kernels for 14%

profile of v1, /device:TPU:0, one launch (start us, length us, event | category | flops | bytes accessed | tf_op | source)
XLA Modules:
  0.0 129.2 jit_solution(16758651139618280152)
XLA Ops:
  0.6 3.0 %collective-permute-start = (bf16[1,6,256,256]{3,2,1,0:T(8,128)(2,1)}, bf16[1,6,256,256]{3,2,1,0:T(8,128)(2,1)S(1)}, u32[]{:S(2)}, u32[]{:S(2)}) collective-permute-start(bf16[1,6,256,256]{3,2,1,0:T(8,128)(2,1)} %refs_5_.1), channel_id=1, source_target_pairs={{0,8},{4,12},{8,0},{12,4},{16,24},{20,28},{24,16},{28,20},{1,9},{5... | collective-permute-start | bytes 2359304 | tf_op jit(solution)/shard_map/ppermute | solution.py:272
  3.6 1.5 %collective-permute-start.1 = (bf16[1,6,256,256]{3,2,1,0:T(8,128)(2,1)}, bf16[1,6,256,256]{3,2,1,0:T(8,128)(2,1)S(1)}, u32[]{:S(2)}, u32[]{:S(2)}) collective-permute-start(bf16[1,6,256,256]{3,2,1,0:T(8,128)(2,1)} %refs_5_.1), channel_id=1, source_target_pairs={{0,16},{4,20},{8,24},{12,28},{16,0},{20,4},{24,8},{28,12},{1,17},{... | collective-permute-start | bytes 2359304 | tf_op jit(solution)/shard_map/ppermute | solution.py:272
  5.2 1.6 %collective-permute-start.2 = (bf16[1,6,256,256]{3,2,1,0:T(8,128)(2,1)}, bf16[1,6,256,256]{3,2,1,0:T(8,128)(2,1)S(1)}, u32[]{:S(2)}, u32[]{:S(2)}) collective-permute-start(bf16[1,6,256,256]{3,2,1,0:T(8,128)(2,1)} %refs_5_.1), channel_id=1, source_target_pairs={{0,1},{1,0},{2,3},{3,2},{4,5},{5,4},{6,7},{7,6},{8,9},{9,8},{10,11... | collective-permute-start | bytes 2359304 | tf_op jit(solution)/shard_map/ppermute | solution.py:277
  6.7 0.7 collective-permute-start.3
  8.1 0.7 pad_add_fusion.5
  8.8 0.5 collective-permute-start.4
  9.3 1.7 %pad_maximum_fusion = bf16[256,4096]{1,0:T(8,128)(2,1)S(1)} fusion(bf16[128,4096]{1,0:T(8,128)(2,1)} %refs_3_.1, bf16[128,4096]{1,0:T(8,128)(2,1)} %refs_2_.1), kind=kLoop, calls=%fused_computation | loop fusion | flops 4194304 | bytes 4194304 | tf_op jit(solution)/shard_map/concatenate | solution.py:290
  11.0 11.9 %collective-permute-done.4 = s32[1,7]{1,0:T(1,128)S(1)} collective-permute-done((s32[1,7]{1,0:T(1,128)S(1)}, s32[1,7]{1,0:T(1,128)S(1)}, u32[]{:S(2)}, u32[]{:S(2)}) %collective-permute-start.4) | collective-permute-done | bytes 60 | tf_op jit(solution)/shard_map/ppermute | solution.py:272
  22.9 0.1 pad_add_fusion.3
  23.0 0.0 collective-permute-done.refs_9_
  23.0 0.0 collective-permute-done.1.refs_6_
  23.0 0.0 copy-start.14
  23.0 1.1 collective-permute-done.2.refs_7_
  24.1 0.6 collective-permute-start.5
  24.7 0.5 collective-permute-start.6
  25.2 0.7 collective-permute-start.8
  25.9 1.3 %collective-permute-start.7 = (bf16[1,6,256,256]{3,2,1,0:T(8,128)(2,1)S(1)}, bf16[1,6,256,256]{3,2,1,0:T(8,128)(2,1)S(1)}, u32[]{:S(2)}, u32[]{:S(2)}) collective-permute-start(bf16[1,6,256,256]{3,2,1,0:T(8,128)(2,1)S(1)} %collective-permute-done.3), channel_id=1, source_target_pairs={{1,0},{2,3},{5,4},{6,7},{9,8},{10,11},{13,12},{14,15},{17,16},{18,... | collective-permute-start | bytes 2359304 | tf_op jit(solution)/shard_map/ppermute | solution.py:277
  27.2 1.6 %collective-permute-start.9 = (s32[2,7]{1,0:T(2,128)S(1)}, s32[2,7]{1,0:T(2,128)S(1)}, u32[]{:S(2)}, u32[]{:S(2)}) collective-permute-start(s32[2,7]{1,0:T(2,128)S(1)} %pad_add_fusion.3), channel_id=1, source_target_pairs={{0,8},{4,12},{8,0},{12,4},{16,24},{20,28},{24,16},{28,20},{1,9},{5... | collective-permute-start | bytes 176 | tf_op jit(solution)/shard_map/ppermute | solution.py:272
  28.8 13.2 %collective-permute-done.9 = s32[2,7]{1,0:T(2,128)S(1)} collective-permute-done((s32[2,7]{1,0:T(2,128)S(1)}, s32[2,7]{1,0:T(2,128)S(1)}, u32[]{:S(2)}, u32[]{:S(2)}) %collective-permute-start.9) | collective-permute-done | bytes 88 | tf_op jit(solution)/shard_map/ppermute | solution.py:272
  42.0 0.2 collective-permute-done.6.refs_8_
  42.2 7.4 %collective-permute-done.7 = bf16[1,6,256,256]{3,2,1,0:T(8,128)(2,1)S(1)} collective-permute-done((bf16[1,6,256,256]{3,2,1,0:T(8,128)(2,1)S(1)}, bf16[1,6,256,256]{3,2,1,0:T(8,128)(2,1)S(1)}, u32[]{:S(2)}, u32[]{:S(2)}) %collective-permute-start.7) | collective-permute-done | bytes 786464 | tf_op jit(solution)/shard_map/ppermute | solution.py:277
  49.6 0.8 copy-done.11
  50.5 1.3 %broadcast_select_fusion.1.refs_4_ = bf16[1,6,256,256]{3,2,1,0:T(8,128)(2,1)S(1)} fusion(bf16[1,6,256,256]{3,2,1,0:T(8,128)(2,1)} %copy-done.8, bf16[1,6,256,256]{3,2,1,0:T(8,128)(2,1)} %copy-done.11, pred[]{:T(512)S(6)} %or.3), kind=kLoop, calls=%fused_computation.4 | loop fusion | flops 393216 | bytes 2359297 | tf_op jit(solution)/shard_map/jit(_where)/select_n | solution.py:297
  51.8 1.6 %collective-permute-start.11 = (bf16[1,6,256,256]{3,2,1,0:T(8,128)(2,1)S(1)}, bf16[1,6,256,256]{3,2,1,0:T(8,128)(2,1)S(1)}, u32[]{:S(2)}, u32[]{:S(2)}) collective-permute-start(bf16[1,6,256,256]{3,2,1,0:T(8,128)(2,1)S(1)} %broadcast_select_fusion.1.refs_4_), channel_id=1, source_target_pairs={{0,16},{4,20},{8,24},{12,28},{16,0},{20,4},{24,8},{28,12},{1,17},{... | collective-permute-start | bytes 2359304 | tf_op jit(solution)/shard_map/ppermute | solution.py:272
  53.4 1.5 %collective-permute-start.10 = (bf16[1,6,256,256]{3,2,1,0:T(8,128)(2,1)S(1)}, bf16[1,6,256,256]{3,2,1,0:T(8,128)(2,1)S(1)}, u32[]{:S(2)}, u32[]{:S(2)}) collective-permute-start(bf16[1,6,256,256]{3,2,1,0:T(8,128)(2,1)S(1)} %copy-done.15), channel_id=1, source_target_pairs={{0,8},{4,12},{8,0},{12,4},{16,24},{20,28},{24,16},{28,20},{1,9},{5... | collective-permute-start | bytes 2359304 | tf_op jit(solution)/shard_map/ppermute | solution.py:272
  54.9 1.3 collective-permute-start.12
  56.2 2.8 %collective-permute-start.13 = (s32[4,7]{1,0:T(4,128)S(1)}, s32[4,7]{1,0:T(4,128)S(1)}, u32[]{:S(2)}, u32[]{:S(2)}) collective-permute-start(s32[4,7]{1,0:T(4,128)S(1)} %pad_add_fusion.2), channel_id=1, source_target_pairs={{0,1},{1,0},{2,3},{3,2},{4,5},{5,4},{6,7},{7,6},{8,9},{9,8},{10,11... | collective-permute-start | bytes 344 | tf_op jit(solution)/shard_map/ppermute | solution.py:277
  59.0 16.5 %collective-permute-done.13 = s32[4,7]{1,0:T(4,128)S(1)} collective-permute-done((s32[4,7]{1,0:T(4,128)S(1)}, s32[4,7]{1,0:T(4,128)S(1)}, u32[]{:S(2)}, u32[]{:S(2)}) %collective-permute-start.13) | collective-permute-done | bytes 144 | tf_op jit(solution)/shard_map/ppermute | solution.py:277
  75.5 0.9 copy-done.5
  76.3 0.1 broadcast_select_fusion.refs_8_
  76.4 0.6 collective-permute-start.15
  77.0 0.5 collective-permute-start.16
  77.5 0.7 collective-permute-start.18
  78.3 4.7 %collective-permute-start.19 = (s32[8,7]{1,0:T(8,128)S(1)}, s32[8,7]{1,0:T(8,128)S(1)}, u32[]{:S(2)}, u32[]{:S(2)}) collective-permute-start(s32[8,7]{1,0:T(8,128)S(1)} %pad_add_fusion.1), channel_id=1, source_target_pairs={{0,2},{1,3},{2,0},{3,1},{4,6},{5,7},{6,4},{7,5},{8,10},{9,11},{10,... | collective-permute-start | bytes 680 | tf_op jit(solution)/shard_map/ppermute | solution.py:277
  83.0 14.9 %collective-permute-done.19 = s32[8,7]{1,0:T(8,128)S(1)} collective-permute-done((s32[8,7]{1,0:T(8,128)S(1)}, s32[8,7]{1,0:T(8,128)S(1)}, u32[]{:S(2)}, u32[]{:S(2)}) %collective-permute-start.19) | collective-permute-done | bytes 256 | tf_op jit(solution)/shard_map/ppermute | solution.py:277
  98.0 1.6 %collective-permute-start.20 = (bf16[1,6,256,256]{3,2,1,0:T(8,128)(2,1)S(1)}, bf16[1,6,256,256]{3,2,1,0:T(8,128)(2,1)}, u32[]{:S(2)}, u32[]{:S(2)}) collective-permute-start(bf16[1,6,256,256]{3,2,1,0:T(8,128)(2,1)S(1)} %collective-permute-done.15.refs_4_), channel_id=1, source_target_pairs={{0,16},{4,20},{8,24},{12,28},{16,0},{20,4},{24,8},{28,12},{1,17},{... | collective-permute-start | bytes 2359304 | tf_op jit(solution)/shard_map/ppermute | solution.py:272
  99.6 1.5 %collective-permute-start.21 = (bf16[1,6,256,256]{3,2,1,0:T(8,128)(2,1)S(1)}, bf16[1,6,256,256]{3,2,1,0:T(8,128)(2,1)}, u32[]{:S(2)}, u32[]{:S(2)}) collective-permute-start(bf16[1,6,256,256]{3,2,1,0:T(8,128)(2,1)S(1)} %broadcast_select_fusion.1.refs_4_), channel_id=1, source_target_pairs={{0,8},{4,12},{8,0},{12,4},{16,24},{20,28},{24,16},{28,20},{1,9},{5... | collective-permute-start | bytes 2359304 | tf_op jit(solution)/shard_map/ppermute | solution.py:272
  101.1 1.5 %collective-permute-start.22 = (bf16[1,6,256,256]{3,2,1,0:T(8,128)(2,1)S(1)}, bf16[1,6,256,256]{3,2,1,0:T(8,128)(2,1)}, u32[]{:S(2)}, u32[]{:S(2)}) collective-permute-start(bf16[1,6,256,256]{3,2,1,0:T(8,128)(2,1)S(1)} %collective-permute-done.18.refs_7_), channel_id=1, source_target_pairs={{1,0},{2,3},{5,4},{6,7},{9,8},{10,11},{13,12},{14,15},{17,16},{18,... | collective-permute-start | bytes 2359304 | tf_op jit(solution)/shard_map/ppermute | solution.py:277
  102.5 0.1 pad_add_fusion.4.refs_0_
  102.6 7.9 %shard_map.68 = (bf16[256,4096]{1,0:T(8,128)(2,1)S(1)}, bf16[256,4096]{1,0:T(8,128)(2,1)S(1)}, f32[128,4096]{1,0:T(8,128)S(1)}, f32[128,4096]{1,0:T(8,128)S(1)},...) custom-call(s32[2]{0:T(128)S(1)} %pad_add_fusion.4.refs_0_, s32[16,7]{1,0:T(8,128)S(1)} %pad_add_fusion.refs_1_, ...), custom_call_target="tpu_custom_call" | custom-call | flops 2415919104 | bytes 4718592 | tf_op jit(solution)/shard_map/pallas_call | solution.py:185
  110.5 5.8 %shard_map.69 = (f32[128,4096]{1,0:T(8,128)S(1)}, f32[128,4096]{1,0:T(8,128)S(1)}, f32[128,4096]{1,0:T(8,128)S(1)}, f32[128,4096]{1,0:T(8,128)S(1)}) custom-call(s32[2]{0:T(128)S(1)} %pad_add_fusion.4.refs_0_, s32[16,7]{1,0:T(8,128)S(1)} %pad_add_fusion.refs_1_, ...), custom_call_target="tpu_custom_call", output_to_operand_aliasing={{0}: (10, {}), {1}: (11, {}), {2}: (12, {}), {3}: (13, {})} | custom-call | flops 2415919104 | bytes 4718592 | tf_op jit(solution)/shard_map/pallas_call | solution.py:185
  116.4 1.7 %collective-permute-done.22.refs_8_ = bf16[1,6,256,256]{3,2,1,0:T(8,128)(2,1)} collective-permute-done((bf16[1,6,256,256]{3,2,1,0:T(8,128)(2,1)S(1)}, bf16[1,6,256,256]{3,2,1,0:T(8,128)(2,1)}, u32[]{:S(2)}, u32[]{:S(2)}) %collective-permute-start.22) | collective-permute-done | bytes 786464 | tf_op jit(solution)/shard_map/ppermute | solution.py:277
  118.1 4.2 %shard_map.71 = (f32[128,4096]{1,0:T(8,128)S(1)}, f32[128,4096]{1,0:T(8,128)S(1)}, bf16[128,4096]{1,0:T(8,128)(2,1)S(1)}, bf16[128,4096]{1,0:T(8,128)(2,1)S(1)}) custom-call(s32[2]{0:T(128)S(1)} %pad_add_fusion.4.refs_0_, s32[16,7]{1,0:T(8,128)S(1)} %pad_add_fusion.refs_1_, ...), custom_call_target="tpu_custom_call", output_to_operand_aliasing={{0}: (9, {}), {1}: (10, {})} | custom-call | flops 805306368 | bytes 3145728 | tf_op jit(solution)/shard_map/pallas_call | solution.py:185
  122.3 0.1 collective-permute-start.24
  122.3 0.5 collective-permute-start.23
  122.8 4.0 %shard_map.70 = (f32[128,4096]{1,0:T(8,128)S(1)}, f32[128,4096]{1,0:T(8,128)S(1)}) custom-call(s32[2]{0:T(128)S(1)} %pad_add_fusion.4.refs_0_, s32[16,7]{1,0:T(8,128)S(1)} %pad_add_fusion.refs_1_, bf16[256,4096]{1,0:T(8,128)(2,1)S(1)} %get-tuple-element.57.refs_2_, ...), custom_call_target="tpu_custom_call", output_to_operand_aliasing={{0}: (9, {}), {1}: (10, {})} | custom-call | flops 805306368 | bytes 3145728 | tf_op jit(solution)/shard_map/pallas_call | solution.py:185
  126.8 1.2 add_convert_fusion
  128.0 1.2 add_convert_fusion.1
  (55 shorter events, 0.1 us)
Async XLA Ops:
  0.6 22.4 %collective-permute-start = (bf16[1,6,256,256]{3,2,1,0:T(8,128)(2,1)}, bf16[1,6,256,256]{3,2,1,0:T(8,128)(2,1)S(1)}, u32[]{:S(2)}, u32[]{:S(2)}) collective-permute-start(bf16[1,6,256,256]{3,2,1,0:T(8,128)(2,1)} %refs_5_.1), channel_id=1, source_target_pairs={{0,8},{4,12},{8,0},{12,4},{16,24},{20,28},{24,16},{28,20},{1,9},{5... | collective-permute-start | bytes 2359304 | tf_op jit(solution)/shard_map/ppermute | solution.py:272
  3.6 19.4 %collective-permute-start.1 = (bf16[1,6,256,256]{3,2,1,0:T(8,128)(2,1)}, bf16[1,6,256,256]{3,2,1,0:T(8,128)(2,1)S(1)}, u32[]{:S(2)}, u32[]{:S(2)}) collective-permute-start(bf16[1,6,256,256]{3,2,1,0:T(8,128)(2,1)} %refs_5_.1), channel_id=1, source_target_pairs={{0,16},{4,20},{8,24},{12,28},{16,0},{20,4},{24,8},{28,12},{1,17},{... | collective-permute-start | bytes 2359304 | tf_op jit(solution)/shard_map/ppermute | solution.py:272
  5.2 18.9 %collective-permute-start.2 = (bf16[1,6,256,256]{3,2,1,0:T(8,128)(2,1)}, bf16[1,6,256,256]{3,2,1,0:T(8,128)(2,1)S(1)}, u32[]{:S(2)}, u32[]{:S(2)}) collective-permute-start(bf16[1,6,256,256]{3,2,1,0:T(8,128)(2,1)} %refs_5_.1), channel_id=1, source_target_pairs={{0,1},{1,0},{2,3},{3,2},{4,5},{5,4},{6,7},{7,6},{8,9},{9,8},{10,11... | collective-permute-start | bytes 2359304 | tf_op jit(solution)/shard_map/ppermute | solution.py:277
  6.7 17.4 %collective-permute-start.3 = (bf16[1,6,256,256]{3,2,1,0:T(8,128)(2,1)}, bf16[1,6,256,256]{3,2,1,0:T(8,128)(2,1)S(1)}, u32[]{:S(2)}, u32[]{:S(2)}) collective-permute-start(bf16[1,6,256,256]{3,2,1,0:T(8,128)(2,1)} %refs_5_.1), channel_id=1, source_target_pairs={{1,2},{2,1},{5,6},{6,5},{9,10},{10,9},{13,14},{14,13},{17,18},{18,... | collective-permute-start | bytes 2359304 | tf_op jit(solution)/shard_map/ppermute | solution.py:277
  8.8 14.1 %copy-start.12 = (s32[1,6]{1,0:T(1,128)S(1)}, s32[1,6]{1,0:T(1,128)}, u32[]{:S(2)}) copy-start(s32[1,6]{1,0:T(1,128)} %param.8) | copy-start | bytes 76
  8.8 14.1 %collective-permute-start.4 = (s32[1,7]{1,0:T(1,128)S(1)}, s32[1,7]{1,0:T(1,128)S(1)}, u32[]{:S(2)}, u32[]{:S(2)}) collective-permute-start(s32[1,7]{1,0:T(1,128)S(1)} %pad_add_fusion.5), channel_id=1, source_target_pairs={{0,16},{4,20},{8,24},{12,28},{16,0},{20,4},{24,8},{28,12},{1,17},{... | collective-permute-start | bytes 92 | tf_op jit(solution)/shard_map/ppermute | solution.py:272
  23.0 26.6 %copy-start.13 = (bf16[1,6,256,256]{3,2,1,0:T(8,128)(2,1)}, bf16[1,6,256,256]{3,2,1,0:T(8,128)(2,1)S(1)}, u32[]{:S(2)}) copy-start(bf16[1,6,256,256]{3,2,1,0:T(8,128)(2,1)S(1)} %collective-permute-done.refs_9_) | copy-start | bytes 2359300
  23.0 26.6 %copy-start.14 = (bf16[1,6,256,256]{3,2,1,0:T(8,128)(2,1)}, bf16[1,6,256,256]{3,2,1,0:T(8,128)(2,1)S(1)}, u32[]{:S(2)}) copy-start(bf16[1,6,256,256]{3,2,1,0:T(8,128)(2,1)S(1)} %collective-permute-done.1.refs_6_) | copy-start | bytes 2359300
  24.1 25.5 %copy-start.16 = (bf16[1,6,256,256]{3,2,1,0:T(8,128)(2,1)}, bf16[1,6,256,256]{3,2,1,0:T(8,128)(2,1)S(1)}, u32[]{:S(2)}) copy-start(bf16[1,6,256,256]{3,2,1,0:T(8,128)(2,1)S(1)} %collective-permute-done.2.refs_7_) | copy-start | bytes 2359300
  24.1 25.5 %copy-start.8 = (bf16[1,6,256,256]{3,2,1,0:T(8,128)(2,1)}, bf16[1,6,256,256]{3,2,1,0:T(8,128)(2,1)S(1)}, u32[]{:S(2)}) copy-start(bf16[1,6,256,256]{3,2,1,0:T(8,128)(2,1)S(1)} %collective-permute-done.3) | copy-start | bytes 2359300
  24.1 17.9 %collective-permute-start.5 = (bf16[1,6,256,256]{3,2,1,0:T(8,128)(2,1)S(1)}, bf16[1,6,256,256]{3,2,1,0:T(8,128)(2,1)S(1)}, u32[]{:S(2)}, u32[]{:S(2)}) collective-permute-start(bf16[1,6,256,256]{3,2,1,0:T(8,128)(2,1)S(1)} %collective-permute-done.2.refs_7_), channel_id=1, source_target_pairs={{0,8},{4,12},{8,0},{12,4},{16,24},{20,28},{24,16},{28,20},{1,9},{5... | collective-permute-start | bytes 2359304 | tf_op jit(solution)/shard_map/ppermute | solution.py:272
  24.7 17.5 %collective-permute-start.6 = (bf16[1,6,256,256]{3,2,1,0:T(8,128)(2,1)S(1)}, bf16[1,6,256,256]{3,2,1,0:T(8,128)(2,1)S(1)}, u32[]{:S(2)}, u32[]{:S(2)}) collective-permute-start(bf16[1,6,256,256]{3,2,1,0:T(8,128)(2,1)S(1)} %collective-permute-done.2.refs_7_), channel_id=1, source_target_pairs={{0,16},{4,20},{8,24},{12,28},{16,0},{20,4},{24,8},{28,12},{1,17},{... | collective-permute-start | bytes 2359304 | tf_op jit(solution)/shard_map/ppermute | solution.py:272
  25.2 17.0 %collective-permute-start.8 = (bf16[1,6,256,256]{3,2,1,0:T(8,128)(2,1)S(1)}, bf16[1,6,256,256]{3,2,1,0:T(8,128)(2,1)S(1)}, u32[]{:S(2)}, u32[]{:S(2)}) collective-permute-start(bf16[1,6,256,256]{3,2,1,0:T(8,128)(2,1)S(1)} %collective-permute-done.2.refs_7_), channel_id=1, source_target_pairs={{1,2},{2,1},{5,6},{6,5},{9,10},{10,9},{13,14},{14,13},{17,18},{18,... | collective-permute-start | bytes 2359304 | tf_op jit(solution)/shard_map/ppermute | solution.py:277
  25.9 23.7 %collective-permute-start.7 = (bf16[1,6,256,256]{3,2,1,0:T(8,128)(2,1)S(1)}, bf16[1,6,256,256]{3,2,1,0:T(8,128)(2,1)S(1)}, u32[]{:S(2)}, u32[]{:S(2)}) collective-permute-start(bf16[1,6,256,256]{3,2,1,0:T(8,128)(2,1)S(1)} %collective-permute-done.3), channel_id=1, source_target_pairs={{1,0},{2,3},{5,4},{6,7},{9,8},{10,11},{13,12},{14,15},{17,16},{18,... | collective-permute-start | bytes 2359304 | tf_op jit(solution)/shard_map/ppermute | solution.py:277
  27.2 14.8 %collective-permute-start.9 = (s32[2,7]{1,0:T(2,128)S(1)}, s32[2,7]{1,0:T(2,128)S(1)}, u32[]{:S(2)}, u32[]{:S(2)}) collective-permute-start(s32[2,7]{1,0:T(2,128)S(1)} %pad_add_fusion.3), channel_id=1, source_target_pairs={{0,8},{4,12},{8,0},{12,4},{16,24},{20,28},{24,16},{28,20},{1,9},{5... | collective-permute-start | bytes 176 | tf_op jit(solution)/shard_map/ppermute | solution.py:272
  42.0 7.6 %copy-start.4 = (bf16[1,6,256,256]{3,2,1,0:T(8,128)(2,1)}, bf16[1,6,256,256]{3,2,1,0:T(8,128)(2,1)S(1)}, u32[]{:S(2)}) copy-start(bf16[1,6,256,256]{3,2,1,0:T(8,128)(2,1)S(1)} %collective-permute-done.5.refs_6_) | copy-start | bytes 2359300
  42.2 7.4 %copy-start.17 = (bf16[1,6,256,256]{3,2,1,0:T(8,128)(2,1)}, bf16[1,6,256,256]{3,2,1,0:T(8,128)(2,1)S(1)}, u32[]{:S(2)}) copy-start(bf16[1,6,256,256]{3,2,1,0:T(8,128)(2,1)S(1)} %collective-permute-done.6.refs_8_) | copy-start | bytes 2359300
  42.2 7.4 %copy-start.9 = (bf16[1,6,256,256]{3,2,1,0:T(8,128)(2,1)}, bf16[1,6,256,256]{3,2,1,0:T(8,128)(2,1)S(1)}, u32[]{:S(2)}) copy-start(bf16[1,6,256,256]{3,2,1,0:T(8,128)(2,1)S(1)} %collective-permute-done.8) | copy-start | bytes 2359300
  49.6 0.9 copy-start.11
  49.6 26.8 %collective-permute-start.14 = (bf16[256,4096]{1,0:T(8,128)(2,1)S(1)}, bf16[256,4096]{1,0:T(8,128)(2,1)}, u32[]{:S(2)}, u32[]{:S(2)}) collective-permute-start(bf16[256,4096]{1,0:T(8,128)(2,1)S(1)} %pad_maximum_fusion), channel_id=1, source_target_pairs={{0,4},{4,0},{8,12},{12,8},{16,20},{20,16},{24,28},{28,24},{1,5},{5... | collective-permute-start | bytes 6291464 | tf_op jit(solution)/shard_map/ppermute | solution.py:272
  50.5 2.9 %copy-start.15 = (bf16[1,6,256,256]{3,2,1,0:T(8,128)(2,1)S(1)}, bf16[1,6,256,256]{3,2,1,0:T(8,128)(2,1)}, u32[]{:S(2)}) copy-start(bf16[1,6,256,256]{3,2,1,0:T(8,128)(2,1)} %copy-done.14) | copy-start | bytes 2359300
  50.5 4.4 %copy-start.10 = (bf16[1,6,256,256]{3,2,1,0:T(8,128)(2,1)S(1)}, bf16[1,6,256,256]{3,2,1,0:T(8,128)(2,1)}, u32[]{:S(2)}) copy-start(bf16[1,6,256,256]{3,2,1,0:T(8,128)(2,1)} %copy-done.9) | copy-start | bytes 2359300
  51.8 58.7 %copy-start = (bf16[1,6,256,256]{3,2,1,0:T(8,128)(2,1)}, bf16[1,6,256,256]{3,2,1,0:T(8,128)(2,1)S(1)}, u32[]{:S(2)}) copy-start(bf16[1,6,256,256]{3,2,1,0:T(8,128)(2,1)S(1)} %broadcast_select_fusion.1.refs_4_) | copy-start | bytes 2359300
  51.8 23.6 %collective-permute-start.11 = (bf16[1,6,256,256]{3,2,1,0:T(8,128)(2,1)S(1)}, bf16[1,6,256,256]{3,2,1,0:T(8,128)(2,1)S(1)}, u32[]{:S(2)}, u32[]{:S(2)}) collective-permute-start(bf16[1,6,256,256]{3,2,1,0:T(8,128)(2,1)S(1)} %broadcast_select_fusion.1.refs_4_), channel_id=1, source_target_pairs={{0,16},{4,20},{8,24},{12,28},{16,0},{20,4},{24,8},{28,12},{1,17},{... | collective-permute-start | bytes 2359304 | tf_op jit(solution)/shard_map/ppermute | solution.py:272
  53.4 22.0 %collective-permute-start.10 = (bf16[1,6,256,256]{3,2,1,0:T(8,128)(2,1)S(1)}, bf16[1,6,256,256]{3,2,1,0:T(8,128)(2,1)S(1)}, u32[]{:S(2)}, u32[]{:S(2)}) collective-permute-start(bf16[1,6,256,256]{3,2,1,0:T(8,128)(2,1)S(1)} %copy-done.15), channel_id=1, source_target_pairs={{0,8},{4,12},{8,0},{12,4},{16,24},{20,28},{24,16},{28,20},{1,9},{5... | collective-permute-start | bytes 2359304 | tf_op jit(solution)/shard_map/ppermute | solution.py:272
  54.9 20.6 %collective-permute-start.12 = (bf16[1,6,256,256]{3,2,1,0:T(8,128)(2,1)S(1)}, bf16[1,6,256,256]{3,2,1,0:T(8,128)(2,1)S(1)}, u32[]{:S(2)}, u32[]{:S(2)}) collective-permute-start(bf16[1,6,256,256]{3,2,1,0:T(8,128)(2,1)S(1)} %copy-done.10), channel_id=1, source_target_pairs={{1,0},{2,3},{5,4},{6,7},{9,8},{10,11},{13,12},{14,15},{17,16},{18,... | collective-permute-start | bytes 2359304 | tf_op jit(solution)/shard_map/ppermute | solution.py:277
  56.2 19.2 %collective-permute-start.13 = (s32[4,7]{1,0:T(4,128)S(1)}, s32[4,7]{1,0:T(4,128)S(1)}, u32[]{:S(2)}, u32[]{:S(2)}) collective-permute-start(s32[4,7]{1,0:T(4,128)S(1)} %pad_add_fusion.2), channel_id=1, source_target_pairs={{0,1},{1,0},{2,3},{3,2},{4,5},{5,4},{6,7},{7,6},{8,9},{9,8},{10,11... | collective-permute-start | bytes 344 | tf_op jit(solution)/shard_map/ppermute | solution.py:277
  75.4 0.9 copy-start.5
  75.5 25.6 %copy-start.18 = (bf16[1,6,256,256]{3,2,1,0:T(8,128)(2,1)}, bf16[1,6,256,256]{3,2,1,0:T(8,128)(2,1)S(1)}, u32[]{:S(2)}) copy-start(bf16[1,6,256,256]{3,2,1,0:T(8,128)(2,1)S(1)} %collective-permute-done.10.refs_10_) | copy-start | bytes 2359300
  76.4 34.1 %copy-start.1 = (bf16[1,6,256,256]{3,2,1,0:T(8,128)(2,1)}, bf16[1,6,256,256]{3,2,1,0:T(8,128)(2,1)S(1)}, u32[]{:S(2)}) copy-start(bf16[1,6,256,256]{3,2,1,0:T(8,128)(2,1)S(1)} %broadcast_select_fusion.refs_8_) | copy-start | bytes 2359300
  76.4 21.5 %collective-permute-start.15 = (bf16[1,6,256,256]{3,2,1,0:T(8,128)(2,1)S(1)}, bf16[1,6,256,256]{3,2,1,0:T(8,128)(2,1)S(1)}, u32[]{:S(2)}, u32[]{:S(2)}) collective-permute-start(bf16[1,6,256,256]{3,2,1,0:T(8,128)(2,1)S(1)} %broadcast_select_fusion.refs_8_), channel_id=1, source_target_pairs={{0,8},{4,12},{8,0},{12,4},{16,24},{20,28},{24,16},{28,20},{1,9},{5... | collective-permute-start | bytes 2359304 | tf_op jit(solution)/shard_map/ppermute | solution.py:272
  77.0 20.9 %collective-permute-start.16 = (bf16[1,6,256,256]{3,2,1,0:T(8,128)(2,1)S(1)}, bf16[1,6,256,256]{3,2,1,0:T(8,128)(2,1)S(1)}, u32[]{:S(2)}, u32[]{:S(2)}) collective-permute-start(bf16[1,6,256,256]{3,2,1,0:T(8,128)(2,1)S(1)} %broadcast_select_fusion.refs_8_), channel_id=1, source_target_pairs={{0,16},{4,20},{8,24},{12,28},{16,0},{20,4},{24,8},{28,12},{1,17},{... | collective-permute-start | bytes 2359304 | tf_op jit(solution)/shard_map/ppermute | solution.py:272
  77.5 20.4 %collective-permute-start.17 = (bf16[1,6,256,256]{3,2,1,0:T(8,128)(2,1)S(1)}, bf16[1,6,256,256]{3,2,1,0:T(8,128)(2,1)S(1)}, u32[]{:S(2)}, u32[]{:S(2)}) collective-permute-start(bf16[1,6,256,256]{3,2,1,0:T(8,128)(2,1)S(1)} %collective-permute-done.10.refs_10_), channel_id=1, source_target_pairs={{0,1},{1,0},{2,3},{3,2},{4,5},{5,4},{6,7},{7,6},{8,9},{9,8},{10,11... | collective-permute-start | bytes 2359304 | tf_op jit(solution)/shard_map/ppermute | solution.py:277
  77.5 20.4 %collective-permute-start.18 = (bf16[1,6,256,256]{3,2,1,0:T(8,128)(2,1)S(1)}, bf16[1,6,256,256]{3,2,1,0:T(8,128)(2,1)S(1)}, u32[]{:S(2)}, u32[]{:S(2)}) collective-permute-start(bf16[1,6,256,256]{3,2,1,0:T(8,128)(2,1)S(1)} %collective-permute-done.10.refs_10_), channel_id=1, source_target_pairs={{1,2},{2,1},{5,6},{6,5},{9,10},{10,9},{13,14},{14,13},{17,18},{18,... | collective-permute-start | bytes 2359304 | tf_op jit(solution)/shard_map/ppermute | solution.py:277
  78.3 19.6 %collective-permute-start.19 = (s32[8,7]{1,0:T(8,128)S(1)}, s32[8,7]{1,0:T(8,128)S(1)}, u32[]{:S(2)}, u32[]{:S(2)}) collective-permute-start(s32[8,7]{1,0:T(8,128)S(1)} %pad_add_fusion.1), channel_id=1, source_target_pairs={{0,2},{1,3},{2,0},{3,1},{4,6},{5,7},{6,4},{7,5},{8,10},{9,11},{10,... | collective-permute-start | bytes 680 | tf_op jit(solution)/shard_map/ppermute | solution.py:277
  97.9 12.6 %copy-start.2 = (bf16[1,6,256,256]{3,2,1,0:T(8,128)(2,1)}, bf16[1,6,256,256]{3,2,1,0:T(8,128)(2,1)S(1)}, u32[]{:S(2)}) copy-start(bf16[1,6,256,256]{3,2,1,0:T(8,128)(2,1)S(1)} %collective-permute-done.15.refs_4_) | copy-start | bytes 2359300
  97.9 1.6 %copy-start.6 = (bf16[1,6,256,256]{3,2,1,0:T(8,128)(2,1)}, bf16[1,6,256,256]{3,2,1,0:T(8,128)(2,1)S(1)}, u32[]{:S(2)}) copy-start(bf16[1,6,256,256]{3,2,1,0:T(8,128)(2,1)S(1)} %collective-permute-done.16.refs_9_) | copy-start | bytes 2359300
  97.9 3.1 %copy-start.7 = (bf16[1,6,256,256]{3,2,1,0:T(8,128)(2,1)}, bf16[1,6,256,256]{3,2,1,0:T(8,128)(2,1)S(1)}, u32[]{:S(2)}) copy-start(bf16[1,6,256,256]{3,2,1,0:T(8,128)(2,1)S(1)} %collective-permute-done.17.refs_7_) | copy-start | bytes 2359300
  98.0 12.6 %copy-start.3 = (bf16[1,6,256,256]{3,2,1,0:T(8,128)(2,1)}, bf16[1,6,256,256]{3,2,1,0:T(8,128)(2,1)S(1)}, u32[]{:S(2)}) copy-start(bf16[1,6,256,256]{3,2,1,0:T(8,128)(2,1)S(1)} %collective-permute-done.18.refs_7_) | copy-start | bytes 2359300
  98.0 18.4 %collective-permute-start.20 = (bf16[1,6,256,256]{3,2,1,0:T(8,128)(2,1)S(1)}, bf16[1,6,256,256]{3,2,1,0:T(8,128)(2,1)}, u32[]{:S(2)}, u32[]{:S(2)}) collective-permute-start(bf16[1,6,256,256]{3,2,1,0:T(8,128)(2,1)S(1)} %collective-permute-done.15.refs_4_), channel_id=1, source_target_pairs={{0,16},{4,20},{8,24},{12,28},{16,0},{20,4},{24,8},{28,12},{1,17},{... | collective-permute-start | bytes 2359304 | tf_op jit(solution)/shard_map/ppermute | solution.py:272
  99.6 16.8 %collective-permute-start.21 = (bf16[1,6,256,256]{3,2,1,0:T(8,128)(2,1)S(1)}, bf16[1,6,256,256]{3,2,1,0:T(8,128)(2,1)}, u32[]{:S(2)}, u32[]{:S(2)}) collective-permute-start(bf16[1,6,256,256]{3,2,1,0:T(8,128)(2,1)S(1)} %broadcast_select_fusion.1.refs_4_), channel_id=1, source_target_pairs={{0,8},{4,12},{8,0},{12,4},{16,24},{20,28},{24,16},{28,20},{1,9},{5... | collective-permute-start | bytes 2359304 | tf_op jit(solution)/shard_map/ppermute | solution.py:272
  101.1 17.0 %collective-permute-start.22 = (bf16[1,6,256,256]{3,2,1,0:T(8,128)(2,1)S(1)}, bf16[1,6,256,256]{3,2,1,0:T(8,128)(2,1)}, u32[]{:S(2)}, u32[]{:S(2)}) collective-permute-start(bf16[1,6,256,256]{3,2,1,0:T(8,128)(2,1)S(1)} %collective-permute-done.18.refs_7_), channel_id=1, source_target_pairs={{1,0},{2,3},{5,4},{6,7},{9,8},{10,11},{13,12},{14,15},{17,16},{18,... | collective-permute-start | bytes 2359304 | tf_op jit(solution)/shard_map/ppermute | solution.py:277
  122.3 4.6 %collective-permute-start.24 = (bf16[128,4096]{1,0:T(8,128)(2,1)S(1)}, bf16[128,4096]{1,0:T(8,128)(2,1)S(1)}, u32[]{:S(2)}, u32[]{:S(2)}) collective-permute-start(bf16[128,4096]{1,0:T(8,128)(2,1)S(1)} %get-tuple-element.77), channel_id=1, source_target_pairs={{0,4},{4,0},{8,12},{12,8},{16,20},{20,16},{24,28},{28,24},{1,5},{5... | collective-permute-start | bytes 3145736 | tf_op jit(solution)/shard_map/ppermute | solution.py:272
  122.3 5.7 %collective-permute-start.23 = (bf16[128,4096]{1,0:T(8,128)(2,1)S(1)}, bf16[128,4096]{1,0:T(8,128)(2,1)S(1)}, u32[]{:S(2)}, u32[]{:S(2)}) collective-permute-start(bf16[128,4096]{1,0:T(8,128)(2,1)S(1)} %get-tuple-element.75), channel_id=1, source_target_pairs={{0,4},{4,0},{8,12},{12,8},{16,20},{20,16},{24,28},{28,24},{1,5},{5... | collective-permute-start | bytes 3145736 | tf_op jit(solution)/shard_map/ppermute | solution.py:272

commit v2 on v1

--- a/solution.py
+++ b/solution.py
@@ -10,6 +10,8 @@
 ROOT_2_OVER_PI = 0.7978845608028654
 CUBIC = 0.044715
 BOTH = ("wide", "narrow")
+LABEL_ROWS = 16
+MOST_BLOCKS, MOST_SLOTS = 16, 6
 VMEM_LIMIT = 32 * 1024 * 1024
 PAIRS_VMEM_LIMIT = 16 * 1024 * 1024
 
@@ -38,20 +40,21 @@
     return pl.ds(pl.multiple_of(index * width, width), width)
 
 
-def run_panel(meta, row1, row2, slots, width, toks, cots, w1, w2, out_accs, grad_accs):
-    count1, count2 = meta[row1, slots], meta[row2, slots]
-
-    def kept(parts, row, count, j):
-        at = lanes(meta[row, j], width)
+def run_panel(first, second, width, toks, cots, w1, w2, out_accs, grad_accs):
+    (index1, count1), (index2, count2) = first, second
+    slots = len(index1)
+
+    def kept(parts, index, count, j):
+        at = lanes(index[j], width)
         value = jnp.concatenate([part[:, at] for part in parts], axis=0)
         return value if j == 0 else jnp.where(j < count, value, jnp.zeros_like(value))
 
-    pre = dot_plain(kept(toks, row1, count1, 0), w1(0))
-    gact = dot_turned(kept(cots, row2, count2, 0), w2(0))
+    pre = dot_plain(kept(toks, index1, count1, 0), w1(0))
+    gact = dot_turned(kept(cots, index2, count2, 0), w2(0))
     for j in range(1, slots):
-        pre = pre + dot_plain(kept(toks, row1, count1, j), w1(j))
+        pre = pre + dot_plain(kept(toks, index1, count1, j), w1(j))
     for j in range(1, slots):
-        gact = gact + dot_turned(kept(cots, row2, count2, j), w2(j))
+        gact = gact + dot_turned(kept(cots, index2, count2, j), w2(j))
     act, slope = gelu_and_slope(pre)
     act = act.astype(jnp.bfloat16)
     gpre = (gact * slope).astype(jnp.bfloat16)
@@ -65,9 +68,29 @@
             at += rows
 
     for j in range(slots):
-        add(out_accs, meta[row2, j], dot_plain(jnp.where(j < count2, act, zero), w2(j)))
+        add(out_accs, index2[j], dot_plain(jnp.where(j < count2, act, zero), w2(j)))
     for j in range(slots):
-        add(grad_accs, meta[row1, j], dot_turned(jnp.where(j < count1, gpre, zero), w1(j)))
+        add(grad_accs, index1[j], dot_turned(jnp.where(j < count1, gpre, zero), w1(j)))
+
+
+def with_labels(weights, block_index, block_counts):
+    _, slots, width, _ = weights.shape
+    labels = jnp.concatenate([block_index, block_counts[:, None]], axis=1).astype(weights.dtype)
+    labels = jnp.pad(labels, ((0, LABEL_ROWS - 1), (0, width - labels.shape[1])))
+    return jnp.concatenate([weights.reshape(slots * width, width), labels], axis=0)
+
+
+def read_labels(labels, slots):
+    values = labels.astype(jnp.float32)
+    row = lax.broadcasted_iota(jnp.int32, values.shape, 0)
+    lane = lax.broadcasted_iota(jnp.int32, values.shape, 1)
+    scale = jnp.zeros_like(values)
+    for j in range(slots):
+        scale = jnp.where((row == 0) & (lane == j), float(MOST_BLOCKS**j), scale)
+    packed = jnp.sum(values * scale).astype(jnp.int32)
+    count = jnp.sum(jnp.where((row == 0) & (lane == slots), values, 0.0)).astype(jnp.int32)
+    index = [lax.shift_right_logical(packed, 4 * j) & (MOST_BLOCKS - 1) for j in range(slots)]
+    return index, count
 
 
 def pairs_kernel(plan, *refs):
@@ -82,9 +105,9 @@
         del refs[:count]
         return taken
 
-    pos, meta = take(2)
+    (pos,) = take(1)
     fed = take(3 if starts else 2)
-    held = [[take(k) for k in counts] for _, _, counts in pairs]
+    held = [[take(k) for k in counts] for counts in pairs]
     if starts:
         tok, cot = take(2)
     else:
@@ -92,9 +115,34 @@
         take(2 * parts)
     sums = take(2 * parts)
     rounded = take(2 * parts if rounds else 0)
-    blocks, block_sem = take(2)
     low, z = pos[0], pos[1]
     middle = (z == 1) | (z == 2)
+    if plan["direct"]:
+        toks = [tok.at[pl.ds(at, size)] for at, size in spans]
+        cots = [cot.at[pl.ds(at, size)] for at, size in spans]
+        below = pl.ds(slots * width, LABEL_ROWS)
+
+        def reader(choice):
+            if len(choice) == 1:
+                return lambda at: choice[0][at, :]
+            return lambda at: jnp.where(middle, choice[0][at, :], choice[1][at, :])
+
+        def panels(first):
+            for both in held:
+                read1, read2 = reader(both[first]), reader(both[1 - first])
+                run_panel(
+                    read_labels(read1(below), slots), read_labels(read2(below), slots), width, toks, cots,
+                    lambda j, read1=read1: read1(pl.ds(j * width, width)),
+                    lambda j, read2=read2: read2(pl.ds(j * width, width)),
+                    sums[:parts], sums[parts:],
+                )
+
+        pl.when(low == 1)(lambda: panels(0))
+        pl.when(low == 0)(lambda: panels(1))
+        for total, out in zip(sums, rounded):
+            out[...] = total[...].astype(out.dtype)
+        return
+    blocks, block_sem = take(2)
 
     feeding = []
     if starts:
@@ -112,7 +160,7 @@
         copy.start()
 
     def block_copy(k, side, source):
-        return pltpu.make_async_copy(source.at[0], blocks.at[k, side], block_sem.at[k, side])
+        return pltpu.make_async_copy(source, blocks.at[k, side], block_sem.at[k, side])
 
     def begin(k, side):
         for which in range(2):
@@ -134,33 +182,29 @@
         copy.wait()
     toks = [tok.at[pl.ds(at, size)] for at, size in spans]
     cots = [cot.at[pl.ds(at, size)] for at, size in spans]
-    for k, (flip, kind, _) in enumerate(pairs):
-        there = {
-            "own": z,
-            "near": z ^ 1,
-            "third": jnp.where(z < 2, 2, 1),
-            "last": jnp.where(z < 2, 3, 0),
-        }[kind]
+    for k in range(n):
+        rows = []
         for side in range(2):
             block_copy(k, side, held[k][side][0]).wait()
-        at = (z ^ there) * 4 + 2 * flip
+            rows.append(read_labels(blocks[k, side, pl.ds(slots * width, LABEL_ROWS), :], slots))
         run_panel(
-            meta, at + 1 - low, at + low, slots, width, toks, cots,
-            lambda j, k=k: blocks[k, 0, j], lambda j, k=k: blocks[k, 1, j],
+            rows[0], rows[1], width, toks, cots,
+            lambda j, k=k: blocks[k, 0, pl.ds(j * width, width), :],
+            lambda j, k=k: blocks[k, 1, pl.ds(j * width, width), :],
             sums[:parts], sums[parts:],
         )
     for total, out in zip(sums, rounded):
         out[...] = total[...].astype(out.dtype)
 
 
-def run_pairs(pos, meta, fed, items, spans, accs, rounds, sizes):
+def run_pairs(pos, fed, items, spans, accs, rounds, sizes, direct=False):
     slots, width = sizes
     parts, n = len(spans), len(items)
     starts = accs is None
     model = fed[0].shape[1]
     plan = dict(
-        pairs=[(flip, kind, (len(first), len(second))) for flip, kind, first, second in items],
-        spans=spans, starts=starts, rounds=rounds, slots=slots, width=width,
+        pairs=[(len(first), len(second)) for first, second in items],
+        spans=spans, starts=starts, rounds=rounds, slots=slots, width=width, direct=direct,
     )
     smem = pl.BlockSpec(memory_space=pltpu.SMEM)
     vmem = pl.BlockSpec(memory_space=pltpu.VMEM)
@@ -169,23 +213,25 @@
     def off_chip(value):
         return pltpu.with_memory_space_constraint(value, pltpu.HBM)
 
-    blocks = [off_chip(a) for item in items for choice in item[2:] for a in choice]
+    blocks = [a if direct else off_chip(a) for item in items for choice in item for a in choice]
     if starts:
         fed = [off_chip(value) for value in fed]
-    operands = [pos, meta, *fed, *blocks, *(accs or [])]
+    operands = [pos, *fed, *blocks, *(accs or [])]
     first_acc = len(operands) - 2 * parts
     out_shape = [jax.ShapeDtypeStruct((size, model), jnp.float32) for _, size in spans] * 2
     if rounds:
         out_shape += [jax.ShapeDtypeStruct((size, model), jnp.bfloat16) for _, size in spans] * 2
     rows = sum(size for _, size in spans)
-    scratch = [pltpu.VMEM((n, 2, slots, width, width), jnp.bfloat16), pltpu.SemaphoreType.DMA((n, 2))]
+    scratch = [pltpu.VMEM((n, 2, slots * width + LABEL_ROWS, width), jnp.bfloat16), pltpu.SemaphoreType.DMA((n, 2))]
+    if direct:
+        scratch = []
     if starts:
         out_shape = [jax.ShapeDtypeStruct((rows, model), jnp.bfloat16)] * 2 + out_shape
         scratch += [pltpu.SemaphoreType.DMA((4,))]
     outs = pl.pallas_call(
         functools.partial(pairs_kernel, plan),
         out_shape=out_shape,
-        in_specs=[smem, smem] + [hbm if starts else vmem] * len(fed) + [hbm] * len(blocks) + [vmem] * len(accs or []),
+        in_specs=[smem] + [hbm if starts else vmem] * len(fed) + [vmem if direct else hbm] * len(blocks) + [vmem] * len(accs or []),
         out_specs=[vmem] * len(out_shape),
         scratch_shapes=scratch,
         input_output_aliases={} if starts else {first_acc + i: i for i in range(2 * parts)},
@@ -206,6 +252,9 @@
             pltpu.make_async_copy(held.at[half + p], blocks.at[buf, 1], sem.at[buf, 1]),
         ]
 
+    def row_of(r):
+        return [meta[r, j] for j in range(slots)], meta[r, slots]
+
     out_acc[...] = jnp.zeros_like(out_acc)
     grad_acc[...] = jnp.zeros_like(grad_acc)
     for copy in copies(0, 0):
@@ -222,7 +271,7 @@
         for copy in copies(p, buf):
             copy.wait()
         run_panel(
-            meta, p, half + p, slots, width, [tok], [cot],
+            row_of(p), row_of(half + p), width, [tok], [cot],
             lambda j: blocks[buf, 0, j], lambda j: blocks[buf, 1, j], [out_acc], [grad_acc],
         )
         return 0
@@ -255,15 +304,19 @@
     return lax.optimization_barrier(values)
 
 
-def exchange_plan(wide, narrow):
-    return wide == 8 and narrow == 4
+def after(value, *others):
+    return together(value, *others)[0]
+
+
+def exchange_plan(wide, narrow, slots, blocks):
+    return wide == 8 and narrow == 4 and slots <= MOST_SLOTS and blocks <= MOST_BLOCKS
 
 
 def body(tokens, cotangent, weights, block_index, block_counts):
     wide, narrow = lax.axis_size("wide"), lax.axis_size("narrow")
     slots, width = weights.shape[1], weights.shape[2]
-    own_meta = jnp.concatenate([block_index, block_counts[:, None]], axis=1)
-    if not exchange_plan(wide, narrow):
+    if not exchange_plan(wide, narrow, slots, tokens.shape[1] // width):
+        own_meta = jnp.concatenate([block_index, block_counts[:, None]], axis=1)
         meta = lax.all_gather(own_meta, BOTH, axis=0, tiled=True)
         gathered = lax.all_gather(weights, BOTH, axis=0, tiled=True)
         return tuple(run_all(meta, tokens, cotangent, gathered))
@@ -280,45 +333,37 @@
     pos = jnp.stack([(w < wide // 2).astype(jnp.int32), z.astype(jnp.int32)])
     mid = (z == 1) | (z == 2)
     run = functools.partial(run_pairs, sizes=(slots, width))
-
-    def doubled(table, moved):
-        return jnp.concatenate([table, moved], axis=0)
-
-    own = weights
-    x_own, y_own, near, beyond = x(own), y(own), line(own, ENDS), line(own, MIDDLE)
-    meta = doubled(own_meta, y(own_meta))
-    both = jnp.concatenate([tokens, cotangent], axis=0)
-
-    x_own, y_own, near, beyond, meta, both = together(x_own, y_own, near, beyond, meta, both)
-    x_near, y_near, out1, in1 = x(near), y(near), line(beyond, OUTWARD), line(near, MIDDLE)
-    meta = doubled(meta, x(meta))
-
-    x_near, y_near, out1, in1, y_own, meta, both = together(x_near, y_near, out1, in1, y_own, meta, both)
-    third = jnp.where(mid, beyond, out1)
-    xy_own, y_third, out2 = x(y_own), y(third), line(in1, OUTWARD)
-    meta = doubled(meta, line(meta, ENDS))
-    both_other = core(both)
-
-    xy_own, y_third, out2, meta, both_other = together(xy_own, y_third, out2, meta, both_other)
-    last = jnp.where(mid, in1, out2)
-    x_last, y_last, xy_near, xy_beyond = x(last), y(last), line(xy_own, ENDS), line(xy_own, MIDDLE)
-    meta = doubled(meta, line(meta, [(i, i ^ 2) for i in range(narrow)]))
-
-    x_last, y_last, xy_near, xy_beyond, third, meta = together(x_last, y_last, xy_near, xy_beyond, third, meta)
-    x_third, xy_last, out3 = x(third), y(x_last), line(xy_beyond, OUTWARD)
     rows = tokens.shape[0]
     mine, others = (0, rows), (rows, rows)
-    fed, accs = run(pos, meta, [tokens, cotangent, both_other], [
-        (0, "own", [own], [y_own]), (0, "near", [near], [y_near]), (1, "own", [x_own], [xy_own]),
+
+    own = with_labels(weights, block_index, block_counts)
+    x_own, y_own, near, beyond = x(own), y(own), line(own, ENDS), line(own, MIDDLE)
+    x_own, y_own, near, beyond = together(x_own, y_own, near, beyond)
+    both = jnp.concatenate([tokens, cotangent], axis=0)
+
+    out1, in1 = line(beyond, OUTWARD), line(near, MIDDLE)
+    y_near, xy_own = y(after(near, y_own)), x(after(y_own, x_own))
+    both_other = core(after(both, x_own))
+
+    out2, xy_beyond = line(after(in1, out1), OUTWARD), line(after(xy_own, in1), MIDDLE)
+    third = jnp.where(mid, beyond, out1)
+    y_third, x_near = y(after(third, y_near)), x(after(near, xy_own))
+
+    last = jnp.where(mid, in1, out2)
+    x_last, xy_near, y_last = x(after(last, x_near)), line(after(xy_own, out2), ENDS), y(after(last, y_third))
+    fed, accs = run(pos, [tokens, cotangent, both_other], [
+        ([own], [y_own]), ([near], [y_near]), ([x_own], [xy_own]),
     ], [mine, others], None, False)
-    fed, accs = run(pos, meta, fed, [
-        (0, "third", [third], [y_third]), (1, "near", [x_near], [xy_near]), (0, "last", [last], [y_last]),
+
+    x_third, out3, xy_last = x(after(third, x_last)), line(after(xy_beyond, xy_near), OUTWARD), y(after(x_last, y_last))
+    fed, accs = run(pos, fed, [
+        ([third], [y_third]), ([x_near], [xy_near]), ([last], [y_last]),
     ], [mine, others], accs, False)
 
-    ending = [(1, "last", [x_last], [xy_last]), (1, "third", [x_third], [xy_beyond, out3])]
-    _, sent = run(pos, meta, fed, ending, [others], [accs[1], accs[3]], True)
+    ending = [([x_last], [xy_last]), ([x_third], [xy_beyond, out3])]
+    _, sent = run(pos, fed, ending, [others], [accs[1], accs[3]], True, direct=True)
     got = [core(part) for part in sent]
-    _, kept = run(pos, meta, fed, ending, [mine], [accs[0], accs[2]], False)
+    _, kept = run(pos, fed, ending, [mine], [accs[0], accs[2]], False, direct=True)
     return tuple(
         (total + other.astype(jnp.float32)).astype(jnp.bfloat16) for total, other in zip(kept, got)
     )

time: 129 us -> 116 us (0.90)
  starting transfers between devices: 30.7 us -> 19.2 us
  other arithmetic: 6.36 us -> 9.38 us
  waiting for transfers between devices: 66.8 us -> 64.1 us
  Pallas kernels: 21.9 us -> 20.1 us
    ppermute x15 -> x13, waiting for transfers between devices: 25.4 us -> 15.3 us  [across(): return lax.ppermute(value, 'wide', [(i, i ^ bit) for i in range(wide)])]
    ppermute x10 -> x8, waiting for transfers between devices: 41.5 us -> 48.8 us  [line(): return lax.ppermute(value, 'narrow', pairs)]
    ppermute x10 -> x8, starting transfers between devices: 15.2 us -> 9.34 us  [line(): return lax.ppermute(value, 'narrow', pairs)]
    ppermute x15 -> x13, starting transfers between devices: 15.5 us -> 9.85 us  [across(): return lax.ppermute(value, 'wide', [(i, i ^ bit) for i in range(wide)])]
    pallas_call x4, Pallas kernels: 21.9 us -> 20.1 us  [run_pairs(): pl.pallas_call(functools.partial(pairs_kernel, plan), out_shape=out_shape...]
  transfers between devices with their start and end apart: 25 -> 21, of which waited for: 8 -> 8; matrix products, arithmetic and copies ran while one was open for 4% -> 5% of each run, Pallas kernels for 14% -> 14%
where the time goes in v2:
time: 116 us; the launch traced here: 115 us
  waiting for transfers between devices  64.1 us (55%)
  Pallas kernels  20.1 us (17%)
  starting transfers between devices  19.2 us (17%)
  other arithmetic  9.38 us (8%)
  between operations  1.58 us (1%)
    ppermute x8, waiting for transfers between devices, line(): return lax.ppermute(value, 'narrow', pairs)  48.8 us
    pallas_call x4, Pallas kernels, run_pairs(): pl.pallas_call(functools.partial(pairs_kernel, plan), out_shape=out_shape...  20.1 us
    ppermute x13, waiting for transfers between devices, across(): return lax.ppermute(value, 'wide', [(i, i ^ bit) for i in range(wide)])  15.3 us
    ppermute x13, starting transfers between devices, across(): return lax.ppermute(value, 'wide', [(i, i ^ bit) for i in range(wide)])  9.85 us
    ppermute x8, starting transfers between devices, line(): return lax.ppermute(value, 'narrow', pairs)  9.34 us
    concatenate x1, other arithmetic, body(): both = jnp.concatenate([tokens, cotangent], axis=0)  2.74 us
    convert_element_type x2, other arithmetic, body(): (total + other.astype(jnp.float32)).astype(jnp.bfloat16)  2.43 us
  transfers between devices with their start and end apart: 21, of which 8 were waited for; matrix products, arithmetic and copies ran while one was open for 5% of the time, Pallas kernels for 14%

profile of v2, /device:TPU:0, one launch (start us, length us, event | category | flops | bytes accessed | tf_op | source)
XLA Modules:
  0.0 115.3 jit_solution(18188340392264992105)
XLA Ops:
  0.6 0.0 copy-start
  1.4 0.7 convert.8
  2.0 0.1 fusion.5
  2.1 1.2 %pad_maximum_fusion.1.refs_4_ = bf16[1552,256]{1,0:T(8,128)(2,1)S(1)} fusion(bf16[16,256]{1,0:T(8,128)(2,1)S(1)} %fusion.5, bf16[1536,256]{1,0:T(8,128)(2,1)} %bitcast.4), kind=kLoop, calls=%fused_computation.3 | loop fusion | flops 1589248 | bytes 1589248 | tf_op jit(solution)/shard_map/concatenate | solution.py:80
  3.3 0.0 copy-start.1
  3.3 3.0 %collective-permute-start = (bf16[1552,256]{1,0:T(8,128)(2,1)S(1)}, bf16[1552,256]{1,0:T(8,128)(2,1)S(1)}, u32[]{:S(2)}, u32[]{:S(2)}) collective-permute-start(bf16[1552,256]{1,0:T(8,128)(2,1)S(1)} %pad_maximum_fusion.1.refs_4_), channel_id=1, source_target_pairs={{0,8},{4,12},{8,0},{12,4},{16,24},{20,28},{24,16},{28,20},{1,9},{5... | collective-permute-start | bytes 2383880 | tf_op jit(solution)/shard_map/ppermute | solution.py:325
  6.3 1.5 %collective-permute-start.1 = (bf16[1552,256]{1,0:T(8,128)(2,1)S(1)}, bf16[1552,256]{1,0:T(8,128)(2,1)S(1)}, u32[]{:S(2)}, u32[]{:S(2)}) collective-permute-start(bf16[1552,256]{1,0:T(8,128)(2,1)S(1)} %pad_maximum_fusion.1.refs_4_), channel_id=1, source_target_pairs={{0,16},{4,20},{8,24},{12,28},{16,0},{20,4},{24,8},{28,12},{1,17},{... | collective-permute-start | bytes 2383880 | tf_op jit(solution)/shard_map/ppermute | solution.py:325
  7.8 1.6 %collective-permute-start.2 = (bf16[1552,256]{1,0:T(8,128)(2,1)S(1)}, bf16[1552,256]{1,0:T(8,128)(2,1)S(1)}, u32[]{:S(2)}, u32[]{:S(2)}) collective-permute-start(bf16[1552,256]{1,0:T(8,128)(2,1)S(1)} %pad_maximum_fusion.1.refs_4_), channel_id=1, source_target_pairs={{0,1},{1,0},{2,3},{3,2},{4,5},{5,4},{6,7},{7,6},{8,9},{9,8},{10,11... | collective-permute-start | bytes 2383880 | tf_op jit(solution)/shard_map/ppermute | solution.py:330
  9.4 1.6 %collective-permute-start.3 = (bf16[1552,256]{1,0:T(8,128)(2,1)S(1)}, bf16[1552,256]{1,0:T(8,128)(2,1)}, u32[]{:S(2)}, u32[]{:S(2)}) collective-permute-start(bf16[1552,256]{1,0:T(8,128)(2,1)S(1)} %pad_maximum_fusion.1.refs_4_), channel_id=1, source_target_pairs={{1,2},{2,1},{5,6},{6,5},{9,10},{10,9},{13,14},{14,13},{17,18},{18,... | collective-permute-start | bytes 2383880 | tf_op jit(solution)/shard_map/ppermute | solution.py:330
  11.1 13.0 %collective-permute-done.refs_8_ = bf16[1552,256]{1,0:T(8,128)(2,1)S(1)} collective-permute-done((bf16[1552,256]{1,0:T(8,128)(2,1)S(1)}, bf16[1552,256]{1,0:T(8,128)(2,1)S(1)}, u32[]{:S(2)}, u32[]{:S(2)}) %collective-permute-start) | collective-permute-done | bytes 794656 | tf_op jit(solution)/shard_map/ppermute | solution.py:325
  24.0 1.5 %collective-permute-done.1.refs_5_ = bf16[1552,256]{1,0:T(8,128)(2,1)S(1)} collective-permute-done((bf16[1552,256]{1,0:T(8,128)(2,1)S(1)}, bf16[1552,256]{1,0:T(8,128)(2,1)S(1)}, u32[]{:S(2)}, u32[]{:S(2)}) %collective-permute-start.1) | collective-permute-done | bytes 794656 | tf_op jit(solution)/shard_map/ppermute | solution.py:325
  25.5 1.2 %collective-permute-done.2.refs_6_ = bf16[1552,256]{1,0:T(8,128)(2,1)S(1)} collective-permute-done((bf16[1552,256]{1,0:T(8,128)(2,1)S(1)}, bf16[1552,256]{1,0:T(8,128)(2,1)S(1)}, u32[]{:S(2)}, u32[]{:S(2)}) %collective-permute-start.2) | collective-permute-done | bytes 794656 | tf_op jit(solution)/shard_map/ppermute | solution.py:330
  26.7 0.0 collective-permute-done.3
  26.8 1.3 %collective-permute-start.8 = (bf16[1552,256]{1,0:T(8,128)(2,1)}, bf16[1552,256]{1,0:T(8,128)(2,1)}, u32[]{:S(2)}, u32[]{:S(2)}) collective-permute-start(bf16[1552,256]{1,0:T(8,128)(2,1)} %collective-permute-done.3), channel_id=1, source_target_pairs={{1,0},{2,3},{5,4},{6,7},{9,8},{10,11},{13,12},{14,15},{17,16},{18,... | collective-permute-start | bytes 2383880 | tf_op jit(solution)/shard_map/ppermute | solution.py:330
  28.1 1.6 %collective-permute-start.7 = (bf16[1552,256]{1,0:T(8,128)(2,1)S(1)}, bf16[1552,256]{1,0:T(8,128)(2,1)}, u32[]{:S(2)}, u32[]{:S(2)}) collective-permute-start(bf16[1552,256]{1,0:T(8,128)(2,1)S(1)} %collective-permute-done.2.refs_6_), channel_id=1, source_target_pairs={{1,2},{2,1},{5,6},{6,5},{9,10},{10,9},{13,14},{14,13},{17,18},{18,... | collective-permute-start | bytes 2383880 | tf_op jit(solution)/shard_map/ppermute | solution.py:330
  29.6 0.5 collective-permute-start.6
  30.2 0.9 collective-permute-start.5
  31.1 2.7 %pad_maximum_fusion = bf16[256,4096]{1,0:T(8,128)(2,1)} fusion(bf16[128,4096]{1,0:T(8,128)(2,1)} %refs_2_.1, bf16[128,4096]{1,0:T(8,128)(2,1)S(1)} %copy-done), kind=kLoop, calls=%fused_computation | loop fusion | flops 4194304 | bytes 4194304 | tf_op jit(solution)/shard_map/concatenate | solution.py:342
  33.8 15.5 %collective-permute-done.8 = bf16[1552,256]{1,0:T(8,128)(2,1)} collective-permute-done((bf16[1552,256]{1,0:T(8,128)(2,1)}, bf16[1552,256]{1,0:T(8,128)(2,1)}, u32[]{:S(2)}, u32[]{:S(2)}) %collective-permute-start.8) | collective-permute-done | bytes 794656 | tf_op jit(solution)/shard_map/ppermute | solution.py:330
  49.3 0.0 collective-permute-done.7
  49.3 1.3 %collective-permute-start.9 = (bf16[1552,256]{1,0:T(8,128)(2,1)}, bf16[1552,256]{1,0:T(8,128)(2,1)S(1)}, u32[]{:S(2)}, u32[]{:S(2)}) collective-permute-start(bf16[1552,256]{1,0:T(8,128)(2,1)} %collective-permute-done.7), channel_id=1, source_target_pairs={{1,0},{2,3},{5,4},{6,7},{9,8},{10,11},{13,12},{14,15},{17,16},{18,... | collective-permute-start | bytes 2383880 | tf_op jit(solution)/shard_map/ppermute | solution.py:330
  50.6 0.6 collective-permute-start.10
  51.2 2.1 %broadcast_select_fusion.refs_3_ = bf16[1552,256]{1,0:T(8,128)(2,1)} fusion(bf16[1552,256]{1,0:T(8,128)(2,1)} %collective-permute-done.3, bf16[1552,256]{1,0:T(8,128)(2,1)} %collective-permute-done.8, pred[]{:T(512)S(6)} %or.3), kind=kLoop, calls=%fused_computation.4 | loop fusion | flops 397312 | bytes 2383873 | tf_op jit(solution)/shard_map/jit(_where)/select_n | solution.py:349
  53.3 0.5 collective-permute-start.12
  53.8 0.7 collective-permute-start.16
  54.5 16.3 %collective-permute-done.9 = bf16[1552,256]{1,0:T(8,128)(2,1)S(1)} collective-permute-done((bf16[1552,256]{1,0:T(8,128)(2,1)}, bf16[1552,256]{1,0:T(8,128)(2,1)S(1)}, u32[]{:S(2)}, u32[]{:S(2)}) %collective-permute-start.9) | collective-permute-done | bytes 794656 | tf_op jit(solution)/shard_map/ppermute | solution.py:330
  70.8 0.1 broadcast_select_fusion.1.refs_7_
  71.0 0.6 collective-permute-start.11
  71.6 0.0 collective-permute-done.12.refs_4_
  71.6 0.5 collective-permute-start.13
  72.1 0.0 collective-permute-done.16.refs_6_
  72.1 15.3 %collective-permute-done.17.refs_6_ = bf16[1552,256]{1,0:T(8,128)(2,1)S(1)} collective-permute-done((bf16[1552,256]{1,0:T(8,128)(2,1)S(1)}, bf16[1552,256]{1,0:T(8,128)(2,1)S(1)}, u32[]{:S(2)}, u32[]{:S(2)}) %collective-permute-start.17) | collective-permute-done | bytes 794656 | tf_op jit(solution)/shard_map/ppermute | solution.py:330
  87.4 1.3 %collective-permute-start.18 = (bf16[1552,256]{1,0:T(8,128)(2,1)S(1)}, bf16[1552,256]{1,0:T(8,128)(2,1)S(1)}, u32[]{:S(2)}, u32[]{:S(2)}) collective-permute-start(bf16[1552,256]{1,0:T(8,128)(2,1)S(1)} %collective-permute-done.16.refs_6_), channel_id=1, source_target_pairs={{1,0},{2,3},{5,4},{6,7},{9,8},{10,11},{13,12},{14,15},{17,16},{18,... | collective-permute-start | bytes 2383880 | tf_op jit(solution)/shard_map/ppermute | solution.py:330
  88.7 0.6 collective-permute-start.15
  89.3 0.9 copy-done.10
  90.3 0.5 collective-permute-start.14
  90.8 0.1 pad_add_fusion.refs_0_
  90.9 0.0 collective-permute-done.4.refs_3_
  90.9 7.8 %shard_map.68 = (bf16[256,4096]{1,0:T(8,128)(2,1)S(1)}, bf16[256,4096]{1,0:T(8,128)(2,1)S(1)}, f32[128,4096]{1,0:T(8,128)S(1)}, f32[128,4096]{1,0:T(8,128)S(1)},...) custom-call(s32[2]{0:T(128)S(1)} %pad_add_fusion.refs_0_, bf16[128,4096]{1,0:T(8,128)(2,1)} %refs_1_.1, ...), custom_call_target="tpu_custom_call" | custom-call | flops 2415919104 | bytes 4718592 | tf_op jit(solution)/shard_map/pallas_call | solution.py:231
  98.7 5.7 %shard_map.69 = (f32[128,4096]{1,0:T(8,128)S(1)}, f32[128,4096]{1,0:T(8,128)S(1)}, f32[128,4096]{1,0:T(8,128)S(1)}, f32[128,4096]{1,0:T(8,128)S(1)}) custom-call(s32[2]{0:T(128)S(1)} %pad_add_fusion.refs_0_, bf16[256,4096]{1,0:T(8,128)(2,1)S(1)} %get-tuple-element.39.refs_1_, ...), custom_call_target="tpu_custom_call", output_to_operand_aliasing={{0}: (9, {}), {1}: (10, {}), {2}: (11, {}), {3}: (12, {})} | custom-call | flops 2415919104 | bytes 4718592 | tf_op jit(solution)/shard_map/pallas_call | solution.py:231
  104.5 0.5 collective-permute-done.18.refs_7_
  105.0 0.8 collective-permute-done.14.refs_4_
  105.8 3.5 %shard_map.71 = (f32[128,4096]{1,0:T(8,128)S(1)}, f32[128,4096]{1,0:T(8,128)S(1)}, bf16[128,4096]{1,0:T(8,128)(2,1)S(1)}, bf16[128,4096]{1,0:T(8,128)(2,1)S(1)}) custom-call(s32[2]{0:T(128)S(1)} %pad_add_fusion.refs_0_, bf16[256,4096]{1,0:T(8,128)(2,1)S(1)} %get-tuple-element.39.refs_1_, ...), custom_call_target="tpu_custom_call", output_to_operand_aliasing={{0}: (8, {}), {1}: (9, {})} | custom-call | flops 805306368 | bytes 3145728 | tf_op jit(solution)/shard_map/pallas_call | solution.py:231
  109.2 0.1 collective-permute-start.20
  109.3 0.5 collective-permute-start.19
  109.8 3.1 %shard_map.70 = (f32[128,4096]{1,0:T(8,128)S(1)}, f32[128,4096]{1,0:T(8,128)S(1)}) custom-call(s32[2]{0:T(128)S(1)} %pad_add_fusion.refs_0_, bf16[256,4096]{1,0:T(8,128)(2,1)S(1)} %get-tuple-element.39.refs_1_, bf16[256,4096]{1,0:T(8,128)(2,1)S(1)} %get-tuple-element.40.refs_2_, ...), custom_call_target="tpu_custom_call", output_to_operand_aliasing={{0}: (8, {}), {1}: (9, {})} | custom-call | flops 805306368 | bytes 3145728 | tf_op jit(solution)/shard_map/pallas_call | solution.py:231
  112.9 1.2 %add_convert_fusion = bf16[128,4096]{1,0:T(8,128)(2,1)} fusion(f32[128,4096]{1,0:T(8,128)S(1)} %get-tuple-element.62, bf16[128,4096]{1,0:T(8,128)(2,1)S(1)} %collective-permute-done.20), kind=kLoop, calls=%fused_computation.1 | loop fusion | flops 1572864 | bytes 4194304 | tf_op jit(solution)/shard_map/convert_element_type | solution.py:368
  114.1 1.2 %add_convert_fusion.1 = bf16[128,4096]{1,0:T(8,128)(2,1)} fusion(f32[128,4096]{1,0:T(8,128)S(1)} %get-tuple-element.58, bf16[128,4096]{1,0:T(8,128)(2,1)S(1)} %collective-permute-done.19), kind=kLoop, calls=%fused_computation.2 | loop fusion | flops 1572864 | bytes 4194304 | tf_op jit(solution)/shard_map/convert_element_type | solution.py:368
  (29 shorter events, 0.1 us)
Async XLA Ops:
  0.6 30.4 %copy-start = (bf16[128,4096]{1,0:T(8,128)(2,1)S(1)}, bf16[128,4096]{1,0:T(8,128)(2,1)}, u32[]{:S(2)}) copy-start(bf16[128,4096]{1,0:T(8,128)(2,1)} %refs_1_.1) | copy-start | bytes 3145732
  3.3 6.1 %copy-start.1 = (bf16[1552,256]{1,0:T(8,128)(2,1)}, bf16[1552,256]{1,0:T(8,128)(2,1)S(1)}, u32[]{:S(2)}) copy-start(bf16[1552,256]{1,0:T(8,128)(2,1)S(1)} %pad_maximum_fusion.1.refs_4_) | copy-start | bytes 2383876
  3.3 20.7 %collective-permute-start = (bf16[1552,256]{1,0:T(8,128)(2,1)S(1)}, bf16[1552,256]{1,0:T(8,128)(2,1)S(1)}, u32[]{:S(2)}, u32[]{:S(2)}) collective-permute-start(bf16[1552,256]{1,0:T(8,128)(2,1)S(1)} %pad_maximum_fusion.1.refs_4_), channel_id=1, source_target_pairs={{0,8},{4,12},{8,0},{12,4},{16,24},{20,28},{24,16},{28,20},{1,9},{5... | collective-permute-start | bytes 2383880 | tf_op jit(solution)/shard_map/ppermute | solution.py:325
  6.3 19.2 %collective-permute-start.1 = (bf16[1552,256]{1,0:T(8,128)(2,1)S(1)}, bf16[1552,256]{1,0:T(8,128)(2,1)S(1)}, u32[]{:S(2)}, u32[]{:S(2)}) collective-permute-start(bf16[1552,256]{1,0:T(8,128)(2,1)S(1)} %pad_maximum_fusion.1.refs_4_), channel_id=1, source_target_pairs={{0,16},{4,20},{8,24},{12,28},{16,0},{20,4},{24,8},{28,12},{1,17},{... | collective-permute-start | bytes 2383880 | tf_op jit(solution)/shard_map/ppermute | solution.py:325
  7.8 18.9 %collective-permute-start.2 = (bf16[1552,256]{1,0:T(8,128)(2,1)S(1)}, bf16[1552,256]{1,0:T(8,128)(2,1)S(1)}, u32[]{:S(2)}, u32[]{:S(2)}) collective-permute-start(bf16[1552,256]{1,0:T(8,128)(2,1)S(1)} %pad_maximum_fusion.1.refs_4_), channel_id=1, source_target_pairs={{0,1},{1,0},{2,3},{3,2},{4,5},{5,4},{6,7},{7,6},{8,9},{9,8},{10,11... | collective-permute-start | bytes 2383880 | tf_op jit(solution)/shard_map/ppermute | solution.py:330
  9.4 17.3 %collective-permute-start.3 = (bf16[1552,256]{1,0:T(8,128)(2,1)S(1)}, bf16[1552,256]{1,0:T(8,128)(2,1)}, u32[]{:S(2)}, u32[]{:S(2)}) collective-permute-start(bf16[1552,256]{1,0:T(8,128)(2,1)S(1)} %pad_maximum_fusion.1.refs_4_), channel_id=1, source_target_pairs={{1,2},{2,1},{5,6},{6,5},{9,10},{10,9},{13,14},{14,13},{17,18},{18,... | collective-permute-start | bytes 2383880 | tf_op jit(solution)/shard_map/ppermute | solution.py:330
  24.0 2.7 %copy-start.3 = (bf16[1552,256]{1,0:T(8,128)(2,1)}, bf16[1552,256]{1,0:T(8,128)(2,1)S(1)}, u32[]{:S(2)}) copy-start(bf16[1552,256]{1,0:T(8,128)(2,1)S(1)} %collective-permute-done.refs_8_) | copy-start | bytes 2383876
  25.5 8.3 %copy-start.4 = (bf16[1552,256]{1,0:T(8,128)(2,1)}, bf16[1552,256]{1,0:T(8,128)(2,1)S(1)}, u32[]{:S(2)}) copy-start(bf16[1552,256]{1,0:T(8,128)(2,1)S(1)} %collective-permute-done.1.refs_5_) | copy-start | bytes 2383876
  26.7 23.8 %copy-start.5 = (bf16[1552,256]{1,0:T(8,128)(2,1)}, bf16[1552,256]{1,0:T(8,128)(2,1)S(1)}, u32[]{:S(2)}) copy-start(bf16[1552,256]{1,0:T(8,128)(2,1)S(1)} %collective-permute-done.2.refs_6_) | copy-start | bytes 2383876
  26.8 22.5 %collective-permute-start.8 = (bf16[1552,256]{1,0:T(8,128)(2,1)}, bf16[1552,256]{1,0:T(8,128)(2,1)}, u32[]{:S(2)}, u32[]{:S(2)}) collective-permute-start(bf16[1552,256]{1,0:T(8,128)(2,1)} %collective-permute-done.3), channel_id=1, source_target_pairs={{1,0},{2,3},{5,4},{6,7},{9,8},{10,11},{13,12},{14,15},{17,16},{18,... | collective-permute-start | bytes 2383880 | tf_op jit(solution)/shard_map/ppermute | solution.py:330
  28.1 21.2 %collective-permute-start.7 = (bf16[1552,256]{1,0:T(8,128)(2,1)S(1)}, bf16[1552,256]{1,0:T(8,128)(2,1)}, u32[]{:S(2)}, u32[]{:S(2)}) collective-permute-start(bf16[1552,256]{1,0:T(8,128)(2,1)S(1)} %collective-permute-done.2.refs_6_), channel_id=1, source_target_pairs={{1,2},{2,1},{5,6},{6,5},{9,10},{10,9},{13,14},{14,13},{17,18},{18,... | collective-permute-start | bytes 2383880 | tf_op jit(solution)/shard_map/ppermute | solution.py:330
  29.6 20.9 %collective-permute-start.6 = (bf16[1552,256]{1,0:T(8,128)(2,1)S(1)}, bf16[1552,256]{1,0:T(8,128)(2,1)S(1)}, u32[]{:S(2)}, u32[]{:S(2)}) collective-permute-start(bf16[1552,256]{1,0:T(8,128)(2,1)S(1)} %collective-permute-done.1.refs_5_), channel_id=1, source_target_pairs={{0,8},{4,12},{8,0},{12,4},{16,24},{20,28},{24,16},{28,20},{1,9},{5... | collective-permute-start | bytes 2383880 | tf_op jit(solution)/shard_map/ppermute | solution.py:325
  30.2 23.1 %collective-permute-start.5 = (bf16[1552,256]{1,0:T(8,128)(2,1)S(1)}, bf16[1552,256]{1,0:T(8,128)(2,1)S(1)}, u32[]{:S(2)}, u32[]{:S(2)}) collective-permute-start(bf16[1552,256]{1,0:T(8,128)(2,1)S(1)} %collective-permute-done.2.refs_6_), channel_id=1, source_target_pairs={{0,16},{4,20},{8,24},{12,28},{16,0},{20,4},{24,8},{28,12},{1,17},{... | collective-permute-start | bytes 2383880 | tf_op jit(solution)/shard_map/ppermute | solution.py:325
  33.8 57.1 %collective-permute-start.4 = (bf16[256,4096]{1,0:T(8,128)(2,1)}, bf16[256,4096]{1,0:T(8,128)(2,1)}, u32[]{:S(2)}, u32[]{:S(2)}) collective-permute-start(bf16[256,4096]{1,0:T(8,128)(2,1)} %pad_maximum_fusion), channel_id=1, source_target_pairs={{0,4},{4,0},{8,12},{12,8},{16,20},{20,16},{24,28},{28,24},{1,5},{5... | collective-permute-start | bytes 6291464 | tf_op jit(solution)/shard_map/ppermute | solution.py:325
  49.3 21.6 %collective-permute-start.9 = (bf16[1552,256]{1,0:T(8,128)(2,1)}, bf16[1552,256]{1,0:T(8,128)(2,1)S(1)}, u32[]{:S(2)}, u32[]{:S(2)}) collective-permute-start(bf16[1552,256]{1,0:T(8,128)(2,1)} %collective-permute-done.7), channel_id=1, source_target_pairs={{1,0},{2,3},{5,4},{6,7},{9,8},{10,11},{13,12},{14,15},{17,16},{18,... | collective-permute-start | bytes 2383880 | tf_op jit(solution)/shard_map/ppermute | solution.py:330
  50.6 20.4 %copy-start.6 = (bf16[1552,256]{1,0:T(8,128)(2,1)}, bf16[1552,256]{1,0:T(8,128)(2,1)S(1)}, u32[]{:S(2)}) copy-start(bf16[1552,256]{1,0:T(8,128)(2,1)S(1)} %collective-permute-done.6.refs_9_) | copy-start | bytes 2383876
  50.6 20.4 %collective-permute-start.10 = (bf16[1552,256]{1,0:T(8,128)(2,1)S(1)}, bf16[1552,256]{1,0:T(8,128)(2,1)}, u32[]{:S(2)}, u32[]{:S(2)}) collective-permute-start(bf16[1552,256]{1,0:T(8,128)(2,1)S(1)} %collective-permute-done.2.refs_6_), channel_id=1, source_target_pairs={{0,8},{4,12},{8,0},{12,4},{16,24},{20,28},{24,16},{28,20},{1,9},{5... | collective-permute-start | bytes 2383880 | tf_op jit(solution)/shard_map/ppermute | solution.py:325
  53.3 36.0 %copy-start.7 = (bf16[1552,256]{1,0:T(8,128)(2,1)}, bf16[1552,256]{1,0:T(8,128)(2,1)S(1)}, u32[]{:S(2)}) copy-start(bf16[1552,256]{1,0:T(8,128)(2,1)S(1)} %collective-permute-done.5.refs_7_) | copy-start | bytes 2383876
  53.3 18.3 %collective-permute-start.12 = (bf16[1552,256]{1,0:T(8,128)(2,1)}, bf16[1552,256]{1,0:T(8,128)(2,1)S(1)}, u32[]{:S(2)}, u32[]{:S(2)}) collective-permute-start(bf16[1552,256]{1,0:T(8,128)(2,1)} %broadcast_select_fusion.refs_3_), channel_id=1, source_target_pairs={{0,16},{4,20},{8,24},{12,28},{16,0},{20,4},{24,8},{28,12},{1,17},{... | collective-permute-start | bytes 2383880 | tf_op jit(solution)/shard_map/ppermute | solution.py:325
  53.8 18.3 %collective-permute-start.16 = (bf16[1552,256]{1,0:T(8,128)(2,1)S(1)}, bf16[1552,256]{1,0:T(8,128)(2,1)S(1)}, u32[]{:S(2)}, u32[]{:S(2)}) collective-permute-start(bf16[1552,256]{1,0:T(8,128)(2,1)S(1)} %collective-permute-done.6.refs_9_), channel_id=1, source_target_pairs={{1,2},{2,1},{5,6},{6,5},{9,10},{10,9},{13,14},{14,13},{17,18},{18,... | collective-permute-start | bytes 2383880 | tf_op jit(solution)/shard_map/ppermute | solution.py:330
  70.8 16.6 %collective-permute-start.17 = (bf16[1552,256]{1,0:T(8,128)(2,1)S(1)}, bf16[1552,256]{1,0:T(8,128)(2,1)S(1)}, u32[]{:S(2)}, u32[]{:S(2)}) collective-permute-start(bf16[1552,256]{1,0:T(8,128)(2,1)S(1)} %collective-permute-done.6.refs_9_), channel_id=1, source_target_pairs={{0,1},{1,0},{2,3},{3,2},{4,5},{5,4},{6,7},{7,6},{8,9},{9,8},{10,11... | collective-permute-start | bytes 2383880 | tf_op jit(solution)/shard_map/ppermute | solution.py:330
  71.0 18.4 %copy-start.2 = (bf16[1552,256]{1,0:T(8,128)(2,1)}, bf16[1552,256]{1,0:T(8,128)(2,1)S(1)}, u32[]{:S(2)}) copy-start(bf16[1552,256]{1,0:T(8,128)(2,1)S(1)} %broadcast_select_fusion.1.refs_7_) | copy-start | bytes 2383876
  71.0 17.7 %collective-permute-start.11 = (bf16[1552,256]{1,0:T(8,128)(2,1)S(1)}, bf16[1552,256]{1,0:T(8,128)(2,1)S(1)}, u32[]{:S(2)}, u32[]{:S(2)}) collective-permute-start(bf16[1552,256]{1,0:T(8,128)(2,1)S(1)} %broadcast_select_fusion.1.refs_7_), channel_id=1, source_target_pairs={{0,8},{4,12},{8,0},{12,4},{16,24},{20,28},{24,16},{28,20},{1,9},{5... | collective-permute-start | bytes 2383880 | tf_op jit(solution)/shard_map/ppermute | solution.py:325
  71.6 17.7 %copy-start.8 = (bf16[1552,256]{1,0:T(8,128)(2,1)}, bf16[1552,256]{1,0:T(8,128)(2,1)S(1)}, u32[]{:S(2)}) copy-start(bf16[1552,256]{1,0:T(8,128)(2,1)S(1)} %collective-permute-done.12.refs_4_) | copy-start | bytes 2383876
  71.6 17.7 %collective-permute-start.13 = (bf16[1552,256]{1,0:T(8,128)(2,1)S(1)}, bf16[1552,256]{1,0:T(8,128)(2,1)S(1)}, u32[]{:S(2)}, u32[]{:S(2)}) collective-permute-start(bf16[1552,256]{1,0:T(8,128)(2,1)S(1)} %broadcast_select_fusion.1.refs_7_), channel_id=1, source_target_pairs={{0,16},{4,20},{8,24},{12,28},{16,0},{20,4},{24,8},{28,12},{1,17},{... | collective-permute-start | bytes 2383880 | tf_op jit(solution)/shard_map/ppermute | solution.py:325
  87.4 1.9 %copy-start.9 = (bf16[1552,256]{1,0:T(8,128)(2,1)}, bf16[1552,256]{1,0:T(8,128)(2,1)S(1)}, u32[]{:S(2)}) copy-start(bf16[1552,256]{1,0:T(8,128)(2,1)S(1)} %collective-permute-done.17.refs_6_) | copy-start | bytes 2383876
  87.4 17.5 %collective-permute-start.18 = (bf16[1552,256]{1,0:T(8,128)(2,1)S(1)}, bf16[1552,256]{1,0:T(8,128)(2,1)S(1)}, u32[]{:S(2)}, u32[]{:S(2)}) collective-permute-start(bf16[1552,256]{1,0:T(8,128)(2,1)S(1)} %collective-permute-done.16.refs_6_), channel_id=1, source_target_pairs={{1,0},{2,3},{5,4},{6,7},{9,8},{10,11},{13,12},{14,15},{17,16},{18,... | collective-permute-start | bytes 2383880 | tf_op jit(solution)/shard_map/ppermute | solution.py:330
  88.7 16.2 %collective-permute-start.15 = (bf16[1552,256]{1,0:T(8,128)(2,1)}, bf16[1552,256]{1,0:T(8,128)(2,1)S(1)}, u32[]{:S(2)}, u32[]{:S(2)}) collective-permute-start(bf16[1552,256]{1,0:T(8,128)(2,1)} %broadcast_select_fusion.refs_3_), channel_id=1, source_target_pairs={{0,8},{4,12},{8,0},{12,4},{16,24},{20,28},{24,16},{28,20},{1,9},{5... | collective-permute-start | bytes 2383880 | tf_op jit(solution)/shard_map/ppermute | solution.py:325
  89.3 0.9 copy-start.10
  90.3 15.5 %collective-permute-start.14 = (bf16[1552,256]{1,0:T(8,128)(2,1)S(1)}, bf16[1552,256]{1,0:T(8,128)(2,1)}, u32[]{:S(2)}, u32[]{:S(2)}) collective-permute-start(bf16[1552,256]{1,0:T(8,128)(2,1)S(1)} %collective-permute-done.11.refs_3_), channel_id=1, source_target_pairs={{0,16},{4,20},{8,24},{12,28},{16,0},{20,4},{24,8},{28,12},{1,17},{... | collective-permute-start | bytes 2383880 | tf_op jit(solution)/shard_map/ppermute | solution.py:325
  109.2 3.7 %collective-permute-start.20 = (bf16[128,4096]{1,0:T(8,128)(2,1)S(1)}, bf16[128,4096]{1,0:T(8,128)(2,1)S(1)}, u32[]{:S(2)}, u32[]{:S(2)}) collective-permute-start(bf16[128,4096]{1,0:T(8,128)(2,1)S(1)} %get-tuple-element.63), channel_id=1, source_target_pairs={{0,4},{4,0},{8,12},{12,8},{16,20},{20,16},{24,28},{28,24},{1,5},{5... | collective-permute-start | bytes 3145736 | tf_op jit(solution)/shard_map/ppermute | solution.py:325
  109.3 4.8 %collective-permute-start.19 = (bf16[128,4096]{1,0:T(8,128)(2,1)S(1)}, bf16[128,4096]{1,0:T(8,128)(2,1)S(1)}, u32[]{:S(2)}, u32[]{:S(2)}) collective-permute-start(bf16[128,4096]{1,0:T(8,128)(2,1)S(1)} %get-tuple-element.61), channel_id=1, source_target_pairs={{0,4},{4,0},{8,12},{12,8},{16,20},{20,16},{24,28},{28,24},{1,5},{5... | collective-permute-start | bytes 3145736 | tf_op jit(solution)/shard_map/ppermute | solution.py:325

commit v3 on v2

--- a/solution.py
+++ b/solution.py
@@ -355,9 +355,9 @@
         ([own], [y_own]), ([near], [y_near]), ([x_own], [xy_own]),
     ], [mine, others], None, False)
 
-    x_third, out3, xy_last = x(after(third, x_last)), line(after(xy_beyond, xy_near), OUTWARD), y(after(x_last, y_last))
+    xy_last, x_third, out3 = y(after(x_last, y_last)), x(after(third, x_last)), line(after(xy_beyond, xy_near), OUTWARD)
     fed, accs = run(pos, fed, [
-        ([third], [y_third]), ([x_near], [xy_near]), ([last], [y_last]),
+        ([beyond, out1], [y_third]), ([x_near], [xy_near]), ([in1, out2], [y_last]),
     ], [mine, others], accs, False)
 
     ending = [([x_last], [xy_last]), ([x_third], [xy_beyond, out3])]

time: 116 us -> 115 us (level)
  waiting for transfers between devices: 64.1 us -> 66 us
  starting transfers between devices: 19.2 us -> 17.4 us
    ppermute x8, starting transfers between devices: 9.34 us -> 7.55 us  [line(): return lax.ppermute(value, 'narrow', pairs)]
  transfers between devices with their start and end apart: 21 -> 21, of which waited for: 8 -> 8; matrix products, arithmetic and copies ran while one was open for 5% -> 4% of each run, Pallas kernels for 14% -> 15%
where the time goes in v3:
time: 115 us; the launch traced here: 114 us
  waiting for transfers between devices  66 us (57%)
  Pallas kernels  20.1 us (17%)
  starting transfers between devices  17.4 us (15%)
  other arithmetic  8.25 us (7%)
  between operations  1.6 us (1%)
    ppermute x8, waiting for transfers between devices, line(): return lax.ppermute(value, 'narrow', pairs)  49.7 us
    pallas_call x4, Pallas kernels, run_pairs(): pl.pallas_call(functools.partial(pairs_kernel, plan), out_shape=out_shape...  20.1 us
    ppermute x13, waiting for transfers between devices, across(): return lax.ppermute(value, 'wide', [(i, i ^ bit) for i in range(wide)])  16.3 us
    ppermute x13, starting transfers between devices, across(): return lax.ppermute(value, 'wide', [(i, i ^ bit) for i in range(wide)])  9.88 us
    ppermute x8, starting transfers between devices, line(): return lax.ppermute(value, 'narrow', pairs)  7.55 us
    concatenate x1, other arithmetic, body(): both = jnp.concatenate([tokens, cotangent], axis=0)  2.73 us
    convert_element_type x2, other arithmetic, body(): (total + other.astype(jnp.float32)).astype(jnp.bfloat16)  2.43 us
  transfers between devices with their start and end apart: 21, of which 8 were waited for; matrix products, arithmetic and copies ran while one was open for 4% of the time, Pallas kernels for 15%

profile of v3, /device:TPU:0, one launch (start us, length us, event | category | flops | bytes accessed | tf_op | source)
XLA Modules:
  0.0 114.4 jit_solution(15789809841122553441)
XLA Ops:
  0.6 0.0 copy-start
  1.4 0.7 convert.8
  2.0 0.1 fusion.5
  2.1 1.2 %pad_maximum_fusion.1.refs_4_ = bf16[1552,256]{1,0:T(8,128)(2,1)S(1)} fusion(bf16[16,256]{1,0:T(8,128)(2,1)S(1)} %fusion.5, bf16[1536,256]{1,0:T(8,128)(2,1)} %bitcast.4), kind=kLoop, calls=%fused_computation.3 | loop fusion | flops 1589248 | bytes 1589248 | tf_op jit(solution)/shard_map/concatenate | solution.py:80
  3.3 0.0 copy-start.1
  3.3 3.0 %collective-permute-start = (bf16[1552,256]{1,0:T(8,128)(2,1)S(1)}, bf16[1552,256]{1,0:T(8,128)(2,1)S(1)}, u32[]{:S(2)}, u32[]{:S(2)}) collective-permute-start(bf16[1552,256]{1,0:T(8,128)(2,1)S(1)} %pad_maximum_fusion.1.refs_4_), channel_id=1, source_target_pairs={{0,8},{4,12},{8,0},{12,4},{16,24},{20,28},{24,16},{28,20},{1,9},{5... | collective-permute-start | bytes 2383880 | tf_op jit(solution)/shard_map/ppermute | solution.py:325
  6.3 1.5 %collective-permute-start.1 = (bf16[1552,256]{1,0:T(8,128)(2,1)S(1)}, bf16[1552,256]{1,0:T(8,128)(2,1)}, u32[]{:S(2)}, u32[]{:S(2)}) collective-permute-start(bf16[1552,256]{1,0:T(8,128)(2,1)S(1)} %pad_maximum_fusion.1.refs_4_), channel_id=1, source_target_pairs={{0,16},{4,20},{8,24},{12,28},{16,0},{20,4},{24,8},{28,12},{1,17},{... | collective-permute-start | bytes 2383880 | tf_op jit(solution)/shard_map/ppermute | solution.py:325
  7.8 1.6 %collective-permute-start.2 = (bf16[1552,256]{1,0:T(8,128)(2,1)S(1)}, bf16[1552,256]{1,0:T(8,128)(2,1)}, u32[]{:S(2)}, u32[]{:S(2)}) collective-permute-start(bf16[1552,256]{1,0:T(8,128)(2,1)S(1)} %pad_maximum_fusion.1.refs_4_), channel_id=1, source_target_pairs={{0,1},{1,0},{2,3},{3,2},{4,5},{5,4},{6,7},{7,6},{8,9},{9,8},{10,11... | collective-permute-start | bytes 2383880 | tf_op jit(solution)/shard_map/ppermute | solution.py:330
  9.4 0.7 collective-permute-start.3
  10.1 13.9 %collective-permute-done.refs_8_ = bf16[1552,256]{1,0:T(8,128)(2,1)S(1)} collective-permute-done((bf16[1552,256]{1,0:T(8,128)(2,1)S(1)}, bf16[1552,256]{1,0:T(8,128)(2,1)S(1)}, u32[]{:S(2)}, u32[]{:S(2)}) %collective-permute-start) | collective-permute-done | bytes 794656 | tf_op jit(solution)/shard_map/ppermute | solution.py:325
  24.0 1.6 %collective-permute-done.1.refs_5_ = bf16[1552,256]{1,0:T(8,128)(2,1)} collective-permute-done((bf16[1552,256]{1,0:T(8,128)(2,1)S(1)}, bf16[1552,256]{1,0:T(8,128)(2,1)}, u32[]{:S(2)}, u32[]{:S(2)}) %collective-permute-start.1) | collective-permute-done | bytes 794656 | tf_op jit(solution)/shard_map/ppermute | solution.py:325
  25.6 1.2 %collective-permute-done.2.refs_6_ = bf16[1552,256]{1,0:T(8,128)(2,1)} collective-permute-done((bf16[1552,256]{1,0:T(8,128)(2,1)S(1)}, bf16[1552,256]{1,0:T(8,128)(2,1)}, u32[]{:S(2)}, u32[]{:S(2)}) %collective-permute-start.2) | collective-permute-done | bytes 794656 | tf_op jit(solution)/shard_map/ppermute | solution.py:330
  26.8 0.0 collective-permute-done.3.refs_3_
  26.9 1.3 %collective-permute-start.8 = (bf16[1552,256]{1,0:T(8,128)(2,1)S(1)}, bf16[1552,256]{1,0:T(8,128)(2,1)S(1)}, u32[]{:S(2)}, u32[]{:S(2)}) collective-permute-start(bf16[1552,256]{1,0:T(8,128)(2,1)S(1)} %collective-permute-done.3.refs_3_), channel_id=1, source_target_pairs={{1,0},{2,3},{5,4},{6,7},{9,8},{10,11},{13,12},{14,15},{17,16},{18,... | collective-permute-start | bytes 2383880 | tf_op jit(solution)/shard_map/ppermute | solution.py:330
  28.2 0.7 collective-permute-start.7
  28.9 0.6 collective-permute-start.6
  29.5 0.9 collective-permute-start.5
  30.3 2.7 %pad_maximum_fusion = bf16[256,4096]{1,0:T(8,128)(2,1)} fusion(bf16[128,4096]{1,0:T(8,128)(2,1)} %refs_2_.1, bf16[128,4096]{1,0:T(8,128)(2,1)S(1)} %copy-done), kind=kLoop, calls=%fused_computation | loop fusion | flops 4194304 | bytes 4194304 | tf_op jit(solution)/shard_map/concatenate | solution.py:342
  33.1 15.8 %collective-permute-done.8.refs_4_ = bf16[1552,256]{1,0:T(8,128)(2,1)S(1)} collective-permute-done((bf16[1552,256]{1,0:T(8,128)(2,1)S(1)}, bf16[1552,256]{1,0:T(8,128)(2,1)S(1)}, u32[]{:S(2)}, u32[]{:S(2)}) %collective-permute-start.8) | collective-permute-done | bytes 794656 | tf_op jit(solution)/shard_map/ppermute | solution.py:330
  48.8 0.0 collective-permute-done.7.refs_8_
  48.8 1.3 %collective-permute-start.9 = (bf16[1552,256]{1,0:T(8,128)(2,1)S(1)}, bf16[1552,256]{1,0:T(8,128)(2,1)S(1)}, u32[]{:S(2)}, u32[]{:S(2)}) collective-permute-start(bf16[1552,256]{1,0:T(8,128)(2,1)S(1)} %collective-permute-done.7.refs_8_), channel_id=1, source_target_pairs={{1,0},{2,3},{5,4},{6,7},{9,8},{10,11},{13,12},{14,15},{17,16},{18,... | collective-permute-start | bytes 2383880 | tf_op jit(solution)/shard_map/ppermute | solution.py:330
  50.1 0.0 collective-permute-done.6.refs_9_
  50.2 0.6 collective-permute-start.10
  50.8 1.0 broadcast_select_fusion
  51.8 0.5 collective-permute-start.12
  52.3 0.7 collective-permute-start.16
  53.0 16.7 %collective-permute-done.9.refs_9_ = bf16[1552,256]{1,0:T(8,128)(2,1)S(1)} collective-permute-done((bf16[1552,256]{1,0:T(8,128)(2,1)S(1)}, bf16[1552,256]{1,0:T(8,128)(2,1)S(1)}, u32[]{:S(2)}, u32[]{:S(2)}) %collective-permute-start.9) | collective-permute-done | bytes 794656 | tf_op jit(solution)/shard_map/ppermute | solution.py:330
  69.7 0.1 broadcast_select_fusion.1
  69.8 0.0 collective-permute-done.10.refs_6_
  69.8 0.6 collective-permute-start.11
  70.4 0.5 collective-permute-start.13
  70.9 0.0 collective-permute-done.16.refs_6_
  70.9 15.5 %collective-permute-done.17.refs_7_ = bf16[1552,256]{1,0:T(8,128)(2,1)S(1)} collective-permute-done((bf16[1552,256]{1,0:T(8,128)(2,1)}, bf16[1552,256]{1,0:T(8,128)(2,1)S(1)}, u32[]{:S(2)}, u32[]{:S(2)}) %collective-permute-start.17) | collective-permute-done | bytes 794656 | tf_op jit(solution)/shard_map/ppermute | solution.py:330
  86.5 1.3 %collective-permute-start.18 = (bf16[1552,256]{1,0:T(8,128)(2,1)S(1)}, bf16[1552,256]{1,0:T(8,128)(2,1)S(1)}, u32[]{:S(2)}, u32[]{:S(2)}) collective-permute-start(bf16[1552,256]{1,0:T(8,128)(2,1)S(1)} %collective-permute-done.16.refs_6_), channel_id=1, source_target_pairs={{1,0},{2,3},{5,4},{6,7},{9,8},{10,11},{13,12},{14,15},{17,16},{18,... | collective-permute-start | bytes 2383880 | tf_op jit(solution)/shard_map/ppermute | solution.py:330
  87.8 0.6 collective-permute-start.15
  88.4 0.9 copy-done.11
  89.3 0.5 collective-permute-start.14
  89.8 0.1 pad_add_fusion.refs_0_
  89.9 7.9 %shard_map.68 = (bf16[256,4096]{1,0:T(8,128)(2,1)S(1)}, bf16[256,4096]{1,0:T(8,128)(2,1)S(1)}, f32[128,4096]{1,0:T(8,128)S(1)}, f32[128,4096]{1,0:T(8,128)S(1)},...) custom-call(s32[2]{0:T(128)S(1)} %pad_add_fusion.refs_0_, bf16[128,4096]{1,0:T(8,128)(2,1)} %refs_1_.1, ...), custom_call_target="tpu_custom_call" | custom-call | flops 2415919104 | bytes 4718592 | tf_op jit(solution)/shard_map/pallas_call | solution.py:231
  97.8 5.7 %shard_map.69 = (f32[128,4096]{1,0:T(8,128)S(1)}, f32[128,4096]{1,0:T(8,128)S(1)}, f32[128,4096]{1,0:T(8,128)S(1)}, f32[128,4096]{1,0:T(8,128)S(1)}) custom-call(s32[2]{0:T(128)S(1)} %pad_add_fusion.refs_0_, bf16[256,4096]{1,0:T(8,128)(2,1)S(1)} %get-tuple-element.39.refs_1_, ...), custom_call_target="tpu_custom_call", output_to_operand_aliasing={{0}: (11, {}), {1}: (12, {}), {2}: (13, {}), {3}: (14, {})} | custom-call | flops 2415919104 | bytes 4718592 | tf_op jit(solution)/shard_map/pallas_call | solution.py:231
  103.5 0.5 collective-permute-done.18.refs_7_
  104.0 0.8 collective-permute-done.14.refs_4_
  104.8 3.5 %shard_map.71 = (f32[128,4096]{1,0:T(8,128)S(1)}, f32[128,4096]{1,0:T(8,128)S(1)}, bf16[128,4096]{1,0:T(8,128)(2,1)S(1)}, bf16[128,4096]{1,0:T(8,128)(2,1)S(1)}) custom-call(s32[2]{0:T(128)S(1)} %pad_add_fusion.refs_0_, bf16[256,4096]{1,0:T(8,128)(2,1)S(1)} %get-tuple-element.39.refs_1_, ...), custom_call_target="tpu_custom_call", output_to_operand_aliasing={{0}: (8, {}), {1}: (9, {})} | custom-call | flops 805306368 | bytes 3145728 | tf_op jit(solution)/shard_map/pallas_call | solution.py:231
  108.3 0.1 collective-permute-start.20
  108.3 0.5 collective-permute-start.19
  108.8 3.1 %shard_map.70 = (f32[128,4096]{1,0:T(8,128)S(1)}, f32[128,4096]{1,0:T(8,128)S(1)}) custom-call(s32[2]{0:T(128)S(1)} %pad_add_fusion.refs_0_, bf16[256,4096]{1,0:T(8,128)(2,1)S(1)} %get-tuple-element.39.refs_1_, bf16[256,4096]{1,0:T(8,128)(2,1)S(1)} %get-tuple-element.40.refs_2_, ...), custom_call_target="tpu_custom_call", output_to_operand_aliasing={{0}: (8, {}), {1}: (9, {})} | custom-call | flops 805306368 | bytes 3145728 | tf_op jit(solution)/shard_map/pallas_call | solution.py:231
  111.9 1.2 %add_convert_fusion = bf16[128,4096]{1,0:T(8,128)(2,1)} fusion(f32[128,4096]{1,0:T(8,128)S(1)} %get-tuple-element.62, bf16[128,4096]{1,0:T(8,128)(2,1)S(1)} %collective-permute-done.20), kind=kLoop, calls=%fused_computation.1 | loop fusion | flops 1572864 | bytes 4194304 | tf_op jit(solution)/shard_map/convert_element_type | solution.py:368
  113.2 1.2 %add_convert_fusion.1 = bf16[128,4096]{1,0:T(8,128)(2,1)} fusion(f32[128,4096]{1,0:T(8,128)S(1)} %get-tuple-element.58, bf16[128,4096]{1,0:T(8,128)(2,1)S(1)} %collective-permute-done.19), kind=kLoop, calls=%fused_computation.2 | loop fusion | flops 1572864 | bytes 4194304 | tf_op jit(solution)/shard_map/convert_element_type | solution.py:368
  (31 shorter events, 0.1 us)
Async XLA Ops:
  0.6 29.7 %copy-start = (bf16[128,4096]{1,0:T(8,128)(2,1)S(1)}, bf16[128,4096]{1,0:T(8,128)(2,1)}, u32[]{:S(2)}) copy-start(bf16[128,4096]{1,0:T(8,128)(2,1)} %refs_1_.1) | copy-start | bytes 3145732
  3.3 6.1 %copy-start.1 = (bf16[1552,256]{1,0:T(8,128)(2,1)}, bf16[1552,256]{1,0:T(8,128)(2,1)S(1)}, u32[]{:S(2)}) copy-start(bf16[1552,256]{1,0:T(8,128)(2,1)S(1)} %pad_maximum_fusion.1.refs_4_) | copy-start | bytes 2383876
  3.3 20.7 %collective-permute-start = (bf16[1552,256]{1,0:T(8,128)(2,1)S(1)}, bf16[1552,256]{1,0:T(8,128)(2,1)S(1)}, u32[]{:S(2)}, u32[]{:S(2)}) collective-permute-start(bf16[1552,256]{1,0:T(8,128)(2,1)S(1)} %pad_maximum_fusion.1.refs_4_), channel_id=1, source_target_pairs={{0,8},{4,12},{8,0},{12,4},{16,24},{20,28},{24,16},{28,20},{1,9},{5... | collective-permute-start | bytes 2383880 | tf_op jit(solution)/shard_map/ppermute | solution.py:325
  6.3 19.3 %collective-permute-start.1 = (bf16[1552,256]{1,0:T(8,128)(2,1)S(1)}, bf16[1552,256]{1,0:T(8,128)(2,1)}, u32[]{:S(2)}, u32[]{:S(2)}) collective-permute-start(bf16[1552,256]{1,0:T(8,128)(2,1)S(1)} %pad_maximum_fusion.1.refs_4_), channel_id=1, source_target_pairs={{0,16},{4,20},{8,24},{12,28},{16,0},{20,4},{24,8},{28,12},{1,17},{... | collective-permute-start | bytes 2383880 | tf_op jit(solution)/shard_map/ppermute | solution.py:325
  7.8 19.0 %collective-permute-start.2 = (bf16[1552,256]{1,0:T(8,128)(2,1)S(1)}, bf16[1552,256]{1,0:T(8,128)(2,1)}, u32[]{:S(2)}, u32[]{:S(2)}) collective-permute-start(bf16[1552,256]{1,0:T(8,128)(2,1)S(1)} %pad_maximum_fusion.1.refs_4_), channel_id=1, source_target_pairs={{0,1},{1,0},{2,3},{3,2},{4,5},{5,4},{6,7},{7,6},{8,9},{9,8},{10,11... | collective-permute-start | bytes 2383880 | tf_op jit(solution)/shard_map/ppermute | solution.py:330
  9.4 17.4 %collective-permute-start.3 = (bf16[1552,256]{1,0:T(8,128)(2,1)S(1)}, bf16[1552,256]{1,0:T(8,128)(2,1)S(1)}, u32[]{:S(2)}, u32[]{:S(2)}) collective-permute-start(bf16[1552,256]{1,0:T(8,128)(2,1)S(1)} %pad_maximum_fusion.1.refs_4_), channel_id=1, source_target_pairs={{1,2},{2,1},{5,6},{6,5},{9,10},{10,9},{13,14},{14,13},{17,18},{18,... | collective-permute-start | bytes 2383880 | tf_op jit(solution)/shard_map/ppermute | solution.py:330
  24.0 2.8 %copy-start.6 = (bf16[1552,256]{1,0:T(8,128)(2,1)}, bf16[1552,256]{1,0:T(8,128)(2,1)S(1)}, u32[]{:S(2)}) copy-start(bf16[1552,256]{1,0:T(8,128)(2,1)S(1)} %collective-permute-done.refs_8_) | copy-start | bytes 2383876
  26.9 23.9 %copy-start.2 = (bf16[1552,256]{1,0:T(8,128)(2,1)}, bf16[1552,256]{1,0:T(8,128)(2,1)S(1)}, u32[]{:S(2)}) copy-start(bf16[1552,256]{1,0:T(8,128)(2,1)S(1)} %collective-permute-done.3.refs_3_) | copy-start | bytes 2383876
  26.9 22.0 %collective-permute-start.8 = (bf16[1552,256]{1,0:T(8,128)(2,1)S(1)}, bf16[1552,256]{1,0:T(8,128)(2,1)S(1)}, u32[]{:S(2)}, u32[]{:S(2)}) collective-permute-start(bf16[1552,256]{1,0:T(8,128)(2,1)S(1)} %collective-permute-done.3.refs_3_), channel_id=1, source_target_pairs={{1,0},{2,3},{5,4},{6,7},{9,8},{10,11},{13,12},{14,15},{17,16},{18,... | collective-permute-start | bytes 2383880 | tf_op jit(solution)/shard_map/ppermute | solution.py:330
  28.2 20.7 %collective-permute-start.7 = (bf16[1552,256]{1,0:T(8,128)(2,1)}, bf16[1552,256]{1,0:T(8,128)(2,1)S(1)}, u32[]{:S(2)}, u32[]{:S(2)}) collective-permute-start(bf16[1552,256]{1,0:T(8,128)(2,1)} %collective-permute-done.2.refs_6_), channel_id=1, source_target_pairs={{1,2},{2,1},{5,6},{6,5},{9,10},{10,9},{13,14},{14,13},{17,18},{18,... | collective-permute-start | bytes 2383880 | tf_op jit(solution)/shard_map/ppermute | solution.py:330
  28.9 21.3 %collective-permute-start.6 = (bf16[1552,256]{1,0:T(8,128)(2,1)}, bf16[1552,256]{1,0:T(8,128)(2,1)}, u32[]{:S(2)}, u32[]{:S(2)}) collective-permute-start(bf16[1552,256]{1,0:T(8,128)(2,1)} %collective-permute-done.1.refs_5_), channel_id=1, source_target_pairs={{0,8},{4,12},{8,0},{12,4},{16,24},{20,28},{24,16},{28,20},{1,9},{5... | collective-permute-start | bytes 2383880 | tf_op jit(solution)/shard_map/ppermute | solution.py:325
  29.5 22.3 %collective-permute-start.5 = (bf16[1552,256]{1,0:T(8,128)(2,1)}, bf16[1552,256]{1,0:T(8,128)(2,1)S(1)}, u32[]{:S(2)}, u32[]{:S(2)}) collective-permute-start(bf16[1552,256]{1,0:T(8,128)(2,1)} %collective-permute-done.2.refs_6_), channel_id=1, source_target_pairs={{0,16},{4,20},{8,24},{12,28},{16,0},{20,4},{24,8},{28,12},{1,17},{... | collective-permute-start | bytes 2383880 | tf_op jit(solution)/shard_map/ppermute | solution.py:325
  33.1 56.8 %collective-permute-start.4 = (bf16[256,4096]{1,0:T(8,128)(2,1)}, bf16[256,4096]{1,0:T(8,128)(2,1)}, u32[]{:S(2)}, u32[]{:S(2)}) collective-permute-start(bf16[256,4096]{1,0:T(8,128)(2,1)} %pad_maximum_fusion), channel_id=1, source_target_pairs={{0,4},{4,0},{8,12},{12,8},{16,20},{20,16},{24,28},{28,24},{1,5},{5... | collective-permute-start | bytes 6291464 | tf_op jit(solution)/shard_map/ppermute | solution.py:325
  48.8 20.9 %copy-start.3 = (bf16[1552,256]{1,0:T(8,128)(2,1)}, bf16[1552,256]{1,0:T(8,128)(2,1)S(1)}, u32[]{:S(2)}) copy-start(bf16[1552,256]{1,0:T(8,128)(2,1)S(1)} %collective-permute-done.8.refs_4_) | copy-start | bytes 2383876
  48.8 20.9 %copy-start.4 = (bf16[1552,256]{1,0:T(8,128)(2,1)}, bf16[1552,256]{1,0:T(8,128)(2,1)S(1)}, u32[]{:S(2)}) copy-start(bf16[1552,256]{1,0:T(8,128)(2,1)S(1)} %collective-permute-done.7.refs_8_) | copy-start | bytes 2383876
  48.8 20.8 %collective-permute-start.9 = (bf16[1552,256]{1,0:T(8,128)(2,1)S(1)}, bf16[1552,256]{1,0:T(8,128)(2,1)S(1)}, u32[]{:S(2)}, u32[]{:S(2)}) collective-permute-start(bf16[1552,256]{1,0:T(8,128)(2,1)S(1)} %collective-permute-done.7.refs_8_), channel_id=1, source_target_pairs={{1,0},{2,3},{5,4},{6,7},{9,8},{10,11},{13,12},{14,15},{17,16},{18,... | collective-permute-start | bytes 2383880 | tf_op jit(solution)/shard_map/ppermute | solution.py:330
  50.2 19.6 %collective-permute-start.10 = (bf16[1552,256]{1,0:T(8,128)(2,1)}, bf16[1552,256]{1,0:T(8,128)(2,1)S(1)}, u32[]{:S(2)}, u32[]{:S(2)}) collective-permute-start(bf16[1552,256]{1,0:T(8,128)(2,1)} %collective-permute-done.2.refs_6_), channel_id=1, source_target_pairs={{0,8},{4,12},{8,0},{12,4},{16,24},{20,28},{24,16},{28,20},{1,9},{5... | collective-permute-start | bytes 2383880 | tf_op jit(solution)/shard_map/ppermute | solution.py:325
  51.8 36.6 %copy-start.7 = (bf16[1552,256]{1,0:T(8,128)(2,1)}, bf16[1552,256]{1,0:T(8,128)(2,1)S(1)}, u32[]{:S(2)}) copy-start(bf16[1552,256]{1,0:T(8,128)(2,1)S(1)} %collective-permute-done.5.refs_7_) | copy-start | bytes 2383876
  51.8 18.6 %collective-permute-start.12 = (bf16[1552,256]{1,0:T(8,128)(2,1)}, bf16[1552,256]{1,0:T(8,128)(2,1)S(1)}, u32[]{:S(2)}, u32[]{:S(2)}) collective-permute-start(bf16[1552,256]{1,0:T(8,128)(2,1)} %broadcast_select_fusion), channel_id=1, source_target_pairs={{0,16},{4,20},{8,24},{12,28},{16,0},{20,4},{24,8},{28,12},{1,17},{... | collective-permute-start | bytes 2383880 | tf_op jit(solution)/shard_map/ppermute | solution.py:325
  52.3 18.6 %collective-permute-start.16 = (bf16[1552,256]{1,0:T(8,128)(2,1)}, bf16[1552,256]{1,0:T(8,128)(2,1)S(1)}, u32[]{:S(2)}, u32[]{:S(2)}) collective-permute-start(bf16[1552,256]{1,0:T(8,128)(2,1)} %collective-permute-done.6.refs_9_), channel_id=1, source_target_pairs={{1,2},{2,1},{5,6},{6,5},{9,10},{10,9},{13,14},{14,13},{17,18},{18,... | collective-permute-start | bytes 2383880 | tf_op jit(solution)/shard_map/ppermute | solution.py:330
  69.7 18.7 %copy-start.5 = (bf16[1552,256]{1,0:T(8,128)(2,1)}, bf16[1552,256]{1,0:T(8,128)(2,1)S(1)}, u32[]{:S(2)}) copy-start(bf16[1552,256]{1,0:T(8,128)(2,1)S(1)} %collective-permute-done.9.refs_9_) | copy-start | bytes 2383876
  69.7 16.8 %collective-permute-start.17 = (bf16[1552,256]{1,0:T(8,128)(2,1)}, bf16[1552,256]{1,0:T(8,128)(2,1)S(1)}, u32[]{:S(2)}, u32[]{:S(2)}) collective-permute-start(bf16[1552,256]{1,0:T(8,128)(2,1)} %collective-permute-done.6.refs_9_), channel_id=1, source_target_pairs={{0,1},{1,0},{2,3},{3,2},{4,5},{5,4},{6,7},{7,6},{8,9},{9,8},{10,11... | collective-permute-start | bytes 2383880 | tf_op jit(solution)/shard_map/ppermute | solution.py:330
  69.8 18.6 %copy-start.8 = (bf16[1552,256]{1,0:T(8,128)(2,1)}, bf16[1552,256]{1,0:T(8,128)(2,1)S(1)}, u32[]{:S(2)}) copy-start(bf16[1552,256]{1,0:T(8,128)(2,1)S(1)} %collective-permute-done.10.refs_6_) | copy-start | bytes 2383876
  69.8 18.0 %collective-permute-start.11 = (bf16[1552,256]{1,0:T(8,128)(2,1)S(1)}, bf16[1552,256]{1,0:T(8,128)(2,1)S(1)}, u32[]{:S(2)}, u32[]{:S(2)}) collective-permute-start(bf16[1552,256]{1,0:T(8,128)(2,1)S(1)} %broadcast_select_fusion.1), channel_id=1, source_target_pairs={{0,8},{4,12},{8,0},{12,4},{16,24},{20,28},{24,16},{28,20},{1,9},{5... | collective-permute-start | bytes 2383880 | tf_op jit(solution)/shard_map/ppermute | solution.py:325
  70.4 18.0 %copy-start.9 = (bf16[1552,256]{1,0:T(8,128)(2,1)}, bf16[1552,256]{1,0:T(8,128)(2,1)S(1)}, u32[]{:S(2)}) copy-start(bf16[1552,256]{1,0:T(8,128)(2,1)S(1)} %collective-permute-done.12.refs_5_) | copy-start | bytes 2383876
  70.4 18.0 %collective-permute-start.13 = (bf16[1552,256]{1,0:T(8,128)(2,1)S(1)}, bf16[1552,256]{1,0:T(8,128)(2,1)S(1)}, u32[]{:S(2)}, u32[]{:S(2)}) collective-permute-start(bf16[1552,256]{1,0:T(8,128)(2,1)S(1)} %broadcast_select_fusion.1), channel_id=1, source_target_pairs={{0,16},{4,20},{8,24},{12,28},{16,0},{20,4},{24,8},{28,12},{1,17},{... | collective-permute-start | bytes 2383880 | tf_op jit(solution)/shard_map/ppermute | solution.py:325
  86.5 1.9 %copy-start.10 = (bf16[1552,256]{1,0:T(8,128)(2,1)}, bf16[1552,256]{1,0:T(8,128)(2,1)S(1)}, u32[]{:S(2)}) copy-start(bf16[1552,256]{1,0:T(8,128)(2,1)S(1)} %collective-permute-done.17.refs_7_) | copy-start | bytes 2383876
  86.5 17.5 %collective-permute-start.18 = (bf16[1552,256]{1,0:T(8,128)(2,1)S(1)}, bf16[1552,256]{1,0:T(8,128)(2,1)S(1)}, u32[]{:S(2)}, u32[]{:S(2)}) collective-permute-start(bf16[1552,256]{1,0:T(8,128)(2,1)S(1)} %collective-permute-done.16.refs_6_), channel_id=1, source_target_pairs={{1,0},{2,3},{5,4},{6,7},{9,8},{10,11},{13,12},{14,15},{17,16},{18,... | collective-permute-start | bytes 2383880 | tf_op jit(solution)/shard_map/ppermute | solution.py:330
  87.8 16.2 %collective-permute-start.15 = (bf16[1552,256]{1,0:T(8,128)(2,1)}, bf16[1552,256]{1,0:T(8,128)(2,1)S(1)}, u32[]{:S(2)}, u32[]{:S(2)}) collective-permute-start(bf16[1552,256]{1,0:T(8,128)(2,1)} %broadcast_select_fusion), channel_id=1, source_target_pairs={{0,8},{4,12},{8,0},{12,4},{16,24},{20,28},{24,16},{28,20},{1,9},{5... | collective-permute-start | bytes 2383880 | tf_op jit(solution)/shard_map/ppermute | solution.py:325
  88.4 0.9 copy-start.11
  89.3 15.5 %collective-permute-start.14 = (bf16[1552,256]{1,0:T(8,128)(2,1)S(1)}, bf16[1552,256]{1,0:T(8,128)(2,1)}, u32[]{:S(2)}, u32[]{:S(2)}) collective-permute-start(bf16[1552,256]{1,0:T(8,128)(2,1)S(1)} %collective-permute-done.11.refs_3_), channel_id=1, source_target_pairs={{0,16},{4,20},{8,24},{12,28},{16,0},{20,4},{24,8},{28,12},{1,17},{... | collective-permute-start | bytes 2383880 | tf_op jit(solution)/shard_map/ppermute | solution.py:325
  108.3 3.7 %collective-permute-start.20 = (bf16[128,4096]{1,0:T(8,128)(2,1)S(1)}, bf16[128,4096]{1,0:T(8,128)(2,1)S(1)}, u32[]{:S(2)}, u32[]{:S(2)}) collective-permute-start(bf16[128,4096]{1,0:T(8,128)(2,1)S(1)} %get-tuple-element.63), channel_id=1, source_target_pairs={{0,4},{4,0},{8,12},{12,8},{16,20},{20,16},{24,28},{28,24},{1,5},{5... | collective-permute-start | bytes 3145736 | tf_op jit(solution)/shard_map/ppermute | solution.py:325
  108.3 4.8 %collective-permute-start.19 = (bf16[128,4096]{1,0:T(8,128)(2,1)S(1)}, bf16[128,4096]{1,0:T(8,128)(2,1)S(1)}, u32[]{:S(2)}, u32[]{:S(2)}) collective-permute-start(bf16[128,4096]{1,0:T(8,128)(2,1)S(1)} %get-tuple-element.61), channel_id=1, source_target_pairs={{0,4},{4,0},{8,12},{12,8},{16,20},{20,16},{24,28},{28,24},{1,5},{5... | collective-permute-start | bytes 3145736 | tf_op jit(solution)/shard_map/ppermute | solution.py:325

commit v4 on v3

--- a/solution.py
+++ b/solution.py
@@ -11,6 +11,7 @@
 CUBIC = 0.044715
 BOTH = ("wide", "narrow")
 LABEL_ROWS = 16
+ADD_STEPS = 4
 MOST_BLOCKS, MOST_SLOTS = 16, 6
 VMEM_LIMIT = 32 * 1024 * 1024
 PAIRS_VMEM_LIMIT = 16 * 1024 * 1024
@@ -75,9 +76,42 @@
 
 def with_labels(weights, block_index, block_counts):
     _, slots, width, _ = weights.shape
-    labels = jnp.concatenate([block_index, block_counts[:, None]], axis=1).astype(weights.dtype)
-    labels = jnp.pad(labels, ((0, LABEL_ROWS - 1), (0, width - labels.shape[1])))
+    row = lax.broadcasted_iota(jnp.int32, (LABEL_ROWS, width), 0)
+    lane = lax.broadcasted_iota(jnp.int32, (LABEL_ROWS, width), 1)
+    count = jnp.where((row == 0) & (lane == slots), lax.reshape(block_counts, ()), 0)
+    labels = jnp.pad(block_index, ((0, LABEL_ROWS - 1), (0, width - slots))) + count
+    labels = labels.astype(weights.dtype)
     return jnp.concatenate([weights.reshape(slots * width, width), labels], axis=0)
+
+
+def add_kernel(*refs):
+    n = (len(refs) - 2) // 3
+    totals, others, outs = refs[:n], refs[n : 2 * n], refs[2 * n : 3 * n]
+    staged, sem = refs[3 * n :]
+    step = totals[0].shape[0] // ADD_STEPS
+    copies = []
+    for k in range(n):
+        for i in range(ADD_STEPS):
+            at = pl.ds(i * step, step)
+            staged[k, at, :] = (totals[k][at, :] + others[k][at, :].astype(jnp.float32)).astype(staged.dtype)
+            copies.append(pltpu.make_async_copy(staged.at[k, at], outs[k].at[at], sem.at[k, i]))
+            copies[-1].start()
+    for copy in copies:
+        copy.wait()
+
+
+def add_rounded(totals, others):
+    n = len(totals)
+    vmem, hbm = pl.BlockSpec(memory_space=pltpu.VMEM), pl.BlockSpec(memory_space=pl.ANY)
+    shape = jax.ShapeDtypeStruct(totals[0].shape, jnp.bfloat16)
+    return pl.pallas_call(
+        add_kernel,
+        out_shape=[shape] * n,
+        in_specs=[vmem] * (2 * n),
+        out_specs=[hbm] * n,
+        scratch_shapes=[pltpu.VMEM((n,) + shape.shape, shape.dtype), pltpu.SemaphoreType.DMA((n, ADD_STEPS))],
+        compiler_params=pltpu.CompilerParams(vmem_limit_bytes=PAIRS_VMEM_LIMIT),
+    )(*totals, *others)
 
 
 def read_labels(labels, slots):
@@ -213,7 +247,10 @@
     def off_chip(value):
         return pltpu.with_memory_space_constraint(value, pltpu.HBM)
 
-    blocks = [a if direct else off_chip(a) for item in items for choice in item for a in choice]
+    def on_chip(value):
+        return pltpu.with_memory_space_constraint(value, pltpu.VMEM)
+
+    blocks = [on_chip(a) if direct else off_chip(a) for item in items for choice in item for a in choice]
     if starts:
         fed = [off_chip(value) for value in fed]
     operands = [pos, *fed, *blocks, *(accs or [])]
@@ -364,9 +401,7 @@
     _, sent = run(pos, fed, ending, [others], [accs[1], accs[3]], True, direct=True)
     got = [core(part) for part in sent]
     _, kept = run(pos, fed, ending, [mine], [accs[0], accs[2]], False, direct=True)
-    return tuple(
-        (total + other.astype(jnp.float32)).astype(jnp.bfloat16) for total, other in zip(kept, got)
-    )
+    return tuple(add_rounded(kept, got))
 
 
 def solution(mesh):

time: 115 us -> 115 us (level)
  other arithmetic: 8.25 us -> 5.83 us
  Pallas kernels: 20.1 us -> 21.5 us
    convert_element_type x2 -> x1, other arithmetic: 2.43 us -> 0.73 us  [with_labels(): labels = labels.astype(weights.dtype)]
    pallas_call x0 -> x1, Pallas kernels: none -> 1.44 us  [add_rounded(): pl.pallas_call(add_kernel, out_shape=[shape] * n, in_specs=[vmem] * (2 *...]
  transfers between devices with their start and end apart: 21 -> 21, of which waited for: 8 -> 9; matrix products, arithmetic and copies ran while one was open for 4% -> 3% of each run, Pallas kernels for 15% -> 15%
where the time goes in v4:
time: 115 us; the launch traced here: 114 us
  waiting for transfers between devices  66.6 us (58%)
  Pallas kernels  21.5 us (19%)
  starting transfers between devices  17.4 us (15%)
  other arithmetic  5.83 us (5%)
  between operations  1.76 us (2%)
    ppermute x8, waiting for transfers between devices, line(): return lax.ppermute(value, 'narrow', pairs)  49.8 us
    pallas_call x4, Pallas kernels, run_pairs(): pl.pallas_call(functools.partial(pairs_kernel, plan), out_shape=out_shape...  20.1 us
    ppermute x13, waiting for transfers between devices, across(): return lax.ppermute(value, 'wide', [(i, i ^ bit) for i in range(wide)])  16.8 us
    ppermute x13, starting transfers between devices, across(): return lax.ppermute(value, 'wide', [(i, i ^ bit) for i in range(wide)])  9.88 us
    ppermute x8, starting transfers between devices, line(): return lax.ppermute(value, 'narrow', pairs)  7.55 us
    concatenate x1, other arithmetic, body(): both = jnp.concatenate([tokens, cotangent], axis=0)  2.73 us
  transfers between devices with their start and end apart: 21, of which 9 were waited for; matrix products, arithmetic and copies ran while one was open for 3% of the time, Pallas kernels for 15%

profile of v4, /device:TPU:0, one launch (start us, length us, event | category | flops | bytes accessed | tf_op | source)
XLA Modules:
  0.0 114.1 jit_solution(14921270817078322060)
XLA Ops:
  0.6 0.0 copy-start
  1.4 0.7 add_convert_fusion
  2.1 1.2 %pad_maximum_fusion.1.refs_4_ = bf16[1552,256]{1,0:T(8,128)(2,1)S(1)} fusion(bf16[16,256]{1,0:T(8,128)(2,1)S(1)} %add_convert_fusion, bf16[1536,256]{1,0:T(8,128)(2,1)} %bitcast.5), kind=kLoop, calls=%fused_computation.1 | loop fusion | flops 1589248 | bytes 1589248 | tf_op jit(solution)/shard_map/concatenate | solution.py:84
  3.3 0.0 copy-start.1
  3.3 3.0 %collective-permute-start = (bf16[1552,256]{1,0:T(8,128)(2,1)S(1)}, bf16[1552,256]{1,0:T(8,128)(2,1)S(1)}, u32[]{:S(2)}, u32[]{:S(2)}) collective-permute-start(bf16[1552,256]{1,0:T(8,128)(2,1)S(1)} %pad_maximum_fusion.1.refs_4_), channel_id=1, source_target_pairs={{0,8},{4,12},{8,0},{12,4},{16,24},{20,28},{24,16},{28,20},{1,9},{5... | collective-permute-start | bytes 2383880 | tf_op jit(solution)/shard_map/ppermute | solution.py:362
  6.3 1.5 %collective-permute-start.1 = (bf16[1552,256]{1,0:T(8,128)(2,1)S(1)}, bf16[1552,256]{1,0:T(8,128)(2,1)}, u32[]{:S(2)}, u32[]{:S(2)}) collective-permute-start(bf16[1552,256]{1,0:T(8,128)(2,1)S(1)} %pad_maximum_fusion.1.refs_4_), channel_id=1, source_target_pairs={{0,16},{4,20},{8,24},{12,28},{16,0},{20,4},{24,8},{28,12},{1,17},{... | collective-permute-start | bytes 2383880 | tf_op jit(solution)/shard_map/ppermute | solution.py:362
  7.9 1.6 %collective-permute-start.2 = (bf16[1552,256]{1,0:T(8,128)(2,1)S(1)}, bf16[1552,256]{1,0:T(8,128)(2,1)}, u32[]{:S(2)}, u32[]{:S(2)}) collective-permute-start(bf16[1552,256]{1,0:T(8,128)(2,1)S(1)} %pad_maximum_fusion.1.refs_4_), channel_id=1, source_target_pairs={{0,1},{1,0},{2,3},{3,2},{4,5},{5,4},{6,7},{7,6},{8,9},{9,8},{10,11... | collective-permute-start | bytes 2383880 | tf_op jit(solution)/shard_map/ppermute | solution.py:367
  9.4 0.7 collective-permute-start.3
  10.1 13.9 %collective-permute-done.refs_8_ = bf16[1552,256]{1,0:T(8,128)(2,1)S(1)} collective-permute-done((bf16[1552,256]{1,0:T(8,128)(2,1)S(1)}, bf16[1552,256]{1,0:T(8,128)(2,1)S(1)}, u32[]{:S(2)}, u32[]{:S(2)}) %collective-permute-start) | collective-permute-done | bytes 794656 | tf_op jit(solution)/shard_map/ppermute | solution.py:362
  24.1 1.6 %collective-permute-done.1.refs_5_ = bf16[1552,256]{1,0:T(8,128)(2,1)} collective-permute-done((bf16[1552,256]{1,0:T(8,128)(2,1)S(1)}, bf16[1552,256]{1,0:T(8,128)(2,1)}, u32[]{:S(2)}, u32[]{:S(2)}) %collective-permute-start.1) | collective-permute-done | bytes 794656 | tf_op jit(solution)/shard_map/ppermute | solution.py:362
  25.6 1.2 %collective-permute-done.2.refs_6_ = bf16[1552,256]{1,0:T(8,128)(2,1)} collective-permute-done((bf16[1552,256]{1,0:T(8,128)(2,1)S(1)}, bf16[1552,256]{1,0:T(8,128)(2,1)}, u32[]{:S(2)}, u32[]{:S(2)}) %collective-permute-start.2) | collective-permute-done | bytes 794656 | tf_op jit(solution)/shard_map/ppermute | solution.py:367
  26.9 1.3 %collective-permute-start.8 = (bf16[1552,256]{1,0:T(8,128)(2,1)S(1)}, bf16[1552,256]{1,0:T(8,128)(2,1)S(1)}, u32[]{:S(2)}, u32[]{:S(2)}) collective-permute-start(bf16[1552,256]{1,0:T(8,128)(2,1)S(1)} %collective-permute-done.3.refs_3_), channel_id=1, source_target_pairs={{1,0},{2,3},{5,4},{6,7},{9,8},{10,11},{13,12},{14,15},{17,16},{18,... | collective-permute-start | bytes 2383880 | tf_op jit(solution)/shard_map/ppermute | solution.py:367
  28.2 0.7 collective-permute-start.7
  28.9 0.6 collective-permute-start.6
  29.5 0.9 collective-permute-start.5
  30.4 2.7 %pad_maximum_fusion = bf16[256,4096]{1,0:T(8,128)(2,1)} fusion(bf16[128,4096]{1,0:T(8,128)(2,1)} %refs_2_.1, bf16[128,4096]{1,0:T(8,128)(2,1)S(1)} %copy-done), kind=kLoop, calls=%fused_computation | loop fusion | flops 4194304 | bytes 4194304 | tf_op jit(solution)/shard_map/concatenate | solution.py:379
  33.1 0.0 collective-permute-start.4
  33.1 15.8 %collective-permute-done.8.refs_4_ = bf16[1552,256]{1,0:T(8,128)(2,1)S(1)} collective-permute-done((bf16[1552,256]{1,0:T(8,128)(2,1)S(1)}, bf16[1552,256]{1,0:T(8,128)(2,1)S(1)}, u32[]{:S(2)}, u32[]{:S(2)}) %collective-permute-start.8) | collective-permute-done | bytes 794656 | tf_op jit(solution)/shard_map/ppermute | solution.py:367
  48.9 0.0 collective-permute-done.7.refs_8_
  48.9 1.3 %collective-permute-start.9 = (bf16[1552,256]{1,0:T(8,128)(2,1)S(1)}, bf16[1552,256]{1,0:T(8,128)(2,1)S(1)}, u32[]{:S(2)}, u32[]{:S(2)}) collective-permute-start(bf16[1552,256]{1,0:T(8,128)(2,1)S(1)} %collective-permute-done.7.refs_8_), channel_id=1, source_target_pairs={{1,0},{2,3},{5,4},{6,7},{9,8},{10,11},{13,12},{14,15},{17,16},{18,... | collective-permute-start | bytes 2383880 | tf_op jit(solution)/shard_map/ppermute | solution.py:367
  50.2 0.6 collective-permute-start.10
  50.8 1.0 broadcast_select_fusion
  51.8 0.0 collective-permute-done.5.refs_7_
  51.8 0.5 collective-permute-start.12
  52.3 0.7 collective-permute-start.16
  53.0 16.7 %collective-permute-done.9.refs_9_ = bf16[1552,256]{1,0:T(8,128)(2,1)S(1)} collective-permute-done((bf16[1552,256]{1,0:T(8,128)(2,1)S(1)}, bf16[1552,256]{1,0:T(8,128)(2,1)S(1)}, u32[]{:S(2)}, u32[]{:S(2)}) %collective-permute-start.9) | collective-permute-done | bytes 794656 | tf_op jit(solution)/shard_map/ppermute | solution.py:367
  69.7 0.0 collective-permute-start.17
  69.7 0.1 broadcast_select_fusion.1
  69.8 0.6 collective-permute-start.11
  70.4 0.0 collective-permute-done.12.refs_5_
  70.4 0.5 collective-permute-start.13
  70.9 15.5 %collective-permute-done.17.refs_7_ = bf16[1552,256]{1,0:T(8,128)(2,1)S(1)} collective-permute-done((bf16[1552,256]{1,0:T(8,128)(2,1)}, bf16[1552,256]{1,0:T(8,128)(2,1)S(1)}, u32[]{:S(2)}, u32[]{:S(2)}) %collective-permute-start.17) | collective-permute-done | bytes 794656 | tf_op jit(solution)/shard_map/ppermute | solution.py:367
  86.5 1.3 %collective-permute-start.18 = (bf16[1552,256]{1,0:T(8,128)(2,1)S(1)}, bf16[1552,256]{1,0:T(8,128)(2,1)S(1)}, u32[]{:S(2)}, u32[]{:S(2)}) collective-permute-start(bf16[1552,256]{1,0:T(8,128)(2,1)S(1)} %collective-permute-done.16.refs_6_), channel_id=1, source_target_pairs={{1,0},{2,3},{5,4},{6,7},{9,8},{10,11},{13,12},{14,15},{17,16},{18,... | collective-permute-start | bytes 2383880 | tf_op jit(solution)/shard_map/ppermute | solution.py:367
  87.8 0.6 collective-permute-start.15
  88.4 0.9 copy-done.11
  89.3 0.5 collective-permute-start.14
  89.8 0.1 pad_add_fusion.refs_0_
  89.9 0.0 collective-permute-done.4.refs_3_
  89.9 7.8 %shard_map.68 = (bf16[256,4096]{1,0:T(8,128)(2,1)S(1)}, bf16[256,4096]{1,0:T(8,128)(2,1)S(1)}, f32[128,4096]{1,0:T(8,128)S(1)}, f32[128,4096]{1,0:T(8,128)S(1)},...) custom-call(s32[2]{0:T(128)S(1)} %pad_add_fusion.refs_0_, bf16[128,4096]{1,0:T(8,128)(2,1)} %refs_1_.1, ...), custom_call_target="tpu_custom_call" | custom-call | flops 2415919104 | bytes 4718592 | tf_op jit(solution)/shard_map/pallas_call | solution.py:268
  97.8 5.7 %shard_map.69 = (f32[128,4096]{1,0:T(8,128)S(1)}, f32[128,4096]{1,0:T(8,128)S(1)}, f32[128,4096]{1,0:T(8,128)S(1)}, f32[128,4096]{1,0:T(8,128)S(1)}) custom-call(s32[2]{0:T(128)S(1)} %pad_add_fusion.refs_0_, bf16[256,4096]{1,0:T(8,128)(2,1)S(1)} %get-tuple-element.39.refs_1_, ...), custom_call_target="tpu_custom_call", output_to_operand_aliasing={{0}: (11, {}), {1}: (12, {}), {2}: (13, {}), {3}: (14, {})} | custom-call | flops 2415919104 | bytes 4718592 | tf_op jit(solution)/shard_map/pallas_call | solution.py:268
  103.5 0.5 collective-permute-done.18.refs_7_
  104.0 0.8 collective-permute-done.14.refs_4_
  104.8 3.5 %shard_map.71 = (f32[128,4096]{1,0:T(8,128)S(1)}, f32[128,4096]{1,0:T(8,128)S(1)}, bf16[128,4096]{1,0:T(8,128)(2,1)S(1)}, bf16[128,4096]{1,0:T(8,128)(2,1)S(1)}) custom-call(s32[2]{0:T(128)S(1)} %pad_add_fusion.refs_0_, bf16[256,4096]{1,0:T(8,128)(2,1)S(1)} %get-tuple-element.39.refs_1_, ...), custom_call_target="tpu_custom_call", output_to_operand_aliasing={{0}: (8, {}), {1}: (9, {})} | custom-call | flops 805306368 | bytes 3145728 | tf_op jit(solution)/shard_map/pallas_call | solution.py:268
  108.3 0.1 collective-permute-start.19
  108.4 0.5 collective-permute-start.20
  108.9 3.1 %shard_map.70 = (f32[128,4096]{1,0:T(8,128)S(1)}, f32[128,4096]{1,0:T(8,128)S(1)}) custom-call(s32[2]{0:T(128)S(1)} %pad_add_fusion.refs_0_, bf16[256,4096]{1,0:T(8,128)(2,1)S(1)} %get-tuple-element.39.refs_1_, bf16[256,4096]{1,0:T(8,128)(2,1)S(1)} %get-tuple-element.40.refs_2_, ...), custom_call_target="tpu_custom_call", output_to_operand_aliasing={{0}: (8, {}), {1}: (9, {})} | custom-call | flops 805306368 | bytes 3145728 | tf_op jit(solution)/shard_map/pallas_call | solution.py:268
  111.9 0.6 collective-permute-done.20.refs_3_
  112.5 1.4 %shard_map.72 = (bf16[128,4096]{1,0:T(8,128)(2,1)}, bf16[128,4096]{1,0:T(8,128)(2,1)}) custom-call(f32[128,4096]{1,0:T(8,128)S(1)} %get-tuple-element.58.refs_0_, f32[128,4096]{1,0:T(8,128)S(1)} %get-tuple-element.59.refs_1_, bf16[128,4096]{1,0:T(8,128)(2,1)S(1)} %collective-permute-done.19.refs_2_, bf16[128,4096]{1,0:T(8,128)(2,1)S(1)} %collective-permute-done.20.refs_3_), custom_call_target="tpu_custom_call" | custom-call | tf_op jit(solution)/shard_map/pallas_call | solution.py:107
  (31 shorter events, 0.1 us)
Async XLA Ops:
  0.6 29.7 %copy-start = (bf16[128,4096]{1,0:T(8,128)(2,1)S(1)}, bf16[128,4096]{1,0:T(8,128)(2,1)}, u32[]{:S(2)}) copy-start(bf16[128,4096]{1,0:T(8,128)(2,1)} %refs_1_.1) | copy-start | bytes 3145732
  3.3 6.1 %copy-start.1 = (bf16[1552,256]{1,0:T(8,128)(2,1)}, bf16[1552,256]{1,0:T(8,128)(2,1)S(1)}, u32[]{:S(2)}) copy-start(bf16[1552,256]{1,0:T(8,128)(2,1)S(1)} %pad_maximum_fusion.1.refs_4_) | copy-start | bytes 2383876
  3.3 20.7 %collective-permute-start = (bf16[1552,256]{1,0:T(8,128)(2,1)S(1)}, bf16[1552,256]{1,0:T(8,128)(2,1)S(1)}, u32[]{:S(2)}, u32[]{:S(2)}) collective-permute-start(bf16[1552,256]{1,0:T(8,128)(2,1)S(1)} %pad_maximum_fusion.1.refs_4_), channel_id=1, source_target_pairs={{0,8},{4,12},{8,0},{12,4},{16,24},{20,28},{24,16},{28,20},{1,9},{5... | collective-permute-start | bytes 2383880 | tf_op jit(solution)/shard_map/ppermute | solution.py:362
  6.3 19.3 %collective-permute-start.1 = (bf16[1552,256]{1,0:T(8,128)(2,1)S(1)}, bf16[1552,256]{1,0:T(8,128)(2,1)}, u32[]{:S(2)}, u32[]{:S(2)}) collective-permute-start(bf16[1552,256]{1,0:T(8,128)(2,1)S(1)} %pad_maximum_fusion.1.refs_4_), channel_id=1, source_target_pairs={{0,16},{4,20},{8,24},{12,28},{16,0},{20,4},{24,8},{28,12},{1,17},{... | collective-permute-start | bytes 2383880 | tf_op jit(solution)/shard_map/ppermute | solution.py:362
  7.9 19.0 %collective-permute-start.2 = (bf16[1552,256]{1,0:T(8,128)(2,1)S(1)}, bf16[1552,256]{1,0:T(8,128)(2,1)}, u32[]{:S(2)}, u32[]{:S(2)}) collective-permute-start(bf16[1552,256]{1,0:T(8,128)(2,1)S(1)} %pad_maximum_fusion.1.refs_4_), channel_id=1, source_target_pairs={{0,1},{1,0},{2,3},{3,2},{4,5},{5,4},{6,7},{7,6},{8,9},{9,8},{10,11... | collective-permute-start | bytes 2383880 | tf_op jit(solution)/shard_map/ppermute | solution.py:367
  9.4 17.4 %collective-permute-start.3 = (bf16[1552,256]{1,0:T(8,128)(2,1)S(1)}, bf16[1552,256]{1,0:T(8,128)(2,1)S(1)}, u32[]{:S(2)}, u32[]{:S(2)}) collective-permute-start(bf16[1552,256]{1,0:T(8,128)(2,1)S(1)} %pad_maximum_fusion.1.refs_4_), channel_id=1, source_target_pairs={{1,2},{2,1},{5,6},{6,5},{9,10},{10,9},{13,14},{14,13},{17,18},{18,... | collective-permute-start | bytes 2383880 | tf_op jit(solution)/shard_map/ppermute | solution.py:367
  24.0 2.8 %copy-start.6 = (bf16[1552,256]{1,0:T(8,128)(2,1)}, bf16[1552,256]{1,0:T(8,128)(2,1)S(1)}, u32[]{:S(2)}) copy-start(bf16[1552,256]{1,0:T(8,128)(2,1)S(1)} %collective-permute-done.refs_8_) | copy-start | bytes 2383876
  26.9 23.9 %copy-start.2 = (bf16[1552,256]{1,0:T(8,128)(2,1)}, bf16[1552,256]{1,0:T(8,128)(2,1)S(1)}, u32[]{:S(2)}) copy-start(bf16[1552,256]{1,0:T(8,128)(2,1)S(1)} %collective-permute-done.3.refs_3_) | copy-start | bytes 2383876
  26.9 22.0 %collective-permute-start.8 = (bf16[1552,256]{1,0:T(8,128)(2,1)S(1)}, bf16[1552,256]{1,0:T(8,128)(2,1)S(1)}, u32[]{:S(2)}, u32[]{:S(2)}) collective-permute-start(bf16[1552,256]{1,0:T(8,128)(2,1)S(1)} %collective-permute-done.3.refs_3_), channel_id=1, source_target_pairs={{1,0},{2,3},{5,4},{6,7},{9,8},{10,11},{13,12},{14,15},{17,16},{18,... | collective-permute-start | bytes 2383880 | tf_op jit(solution)/shard_map/ppermute | solution.py:367
  28.2 20.7 %collective-permute-start.7 = (bf16[1552,256]{1,0:T(8,128)(2,1)}, bf16[1552,256]{1,0:T(8,128)(2,1)S(1)}, u32[]{:S(2)}, u32[]{:S(2)}) collective-permute-start(bf16[1552,256]{1,0:T(8,128)(2,1)} %collective-permute-done.2.refs_6_), channel_id=1, source_target_pairs={{1,2},{2,1},{5,6},{6,5},{9,10},{10,9},{13,14},{14,13},{17,18},{18,... | collective-permute-start | bytes 2383880 | tf_op jit(solution)/shard_map/ppermute | solution.py:367
  28.9 21.3 %collective-permute-start.6 = (bf16[1552,256]{1,0:T(8,128)(2,1)}, bf16[1552,256]{1,0:T(8,128)(2,1)}, u32[]{:S(2)}, u32[]{:S(2)}) collective-permute-start(bf16[1552,256]{1,0:T(8,128)(2,1)} %collective-permute-done.1.refs_5_), channel_id=1, source_target_pairs={{0,8},{4,12},{8,0},{12,4},{16,24},{20,28},{24,16},{28,20},{1,9},{5... | collective-permute-start | bytes 2383880 | tf_op jit(solution)/shard_map/ppermute | solution.py:362
  29.5 22.3 %collective-permute-start.5 = (bf16[1552,256]{1,0:T(8,128)(2,1)}, bf16[1552,256]{1,0:T(8,128)(2,1)S(1)}, u32[]{:S(2)}, u32[]{:S(2)}) collective-permute-start(bf16[1552,256]{1,0:T(8,128)(2,1)} %collective-permute-done.2.refs_6_), channel_id=1, source_target_pairs={{0,16},{4,20},{8,24},{12,28},{16,0},{20,4},{24,8},{28,12},{1,17},{... | collective-permute-start | bytes 2383880 | tf_op jit(solution)/shard_map/ppermute | solution.py:362
  33.1 56.8 %collective-permute-start.4 = (bf16[256,4096]{1,0:T(8,128)(2,1)}, bf16[256,4096]{1,0:T(8,128)(2,1)}, u32[]{:S(2)}, u32[]{:S(2)}) collective-permute-start(bf16[256,4096]{1,0:T(8,128)(2,1)} %pad_maximum_fusion), channel_id=1, source_target_pairs={{0,4},{4,0},{8,12},{12,8},{16,20},{20,16},{24,28},{28,24},{1,5},{5... | collective-permute-start | bytes 6291464 | tf_op jit(solution)/shard_map/ppermute | solution.py:362
  48.8 20.9 %copy-start.3 = (bf16[1552,256]{1,0:T(8,128)(2,1)}, bf16[1552,256]{1,0:T(8,128)(2,1)S(1)}, u32[]{:S(2)}) copy-start(bf16[1552,256]{1,0:T(8,128)(2,1)S(1)} %collective-permute-done.8.refs_4_) | copy-start | bytes 2383876
  48.9 20.9 %copy-start.4 = (bf16[1552,256]{1,0:T(8,128)(2,1)}, bf16[1552,256]{1,0:T(8,128)(2,1)S(1)}, u32[]{:S(2)}) copy-start(bf16[1552,256]{1,0:T(8,128)(2,1)S(1)} %collective-permute-done.7.refs_8_) | copy-start | bytes 2383876
  48.9 20.8 %collective-permute-start.9 = (bf16[1552,256]{1,0:T(8,128)(2,1)S(1)}, bf16[1552,256]{1,0:T(8,128)(2,1)S(1)}, u32[]{:S(2)}, u32[]{:S(2)}) collective-permute-start(bf16[1552,256]{1,0:T(8,128)(2,1)S(1)} %collective-permute-done.7.refs_8_), channel_id=1, source_target_pairs={{1,0},{2,3},{5,4},{6,7},{9,8},{10,11},{13,12},{14,15},{17,16},{18,... | collective-permute-start | bytes 2383880 | tf_op jit(solution)/shard_map/ppermute | solution.py:367
  50.2 19.6 %collective-permute-start.10 = (bf16[1552,256]{1,0:T(8,128)(2,1)}, bf16[1552,256]{1,0:T(8,128)(2,1)S(1)}, u32[]{:S(2)}, u32[]{:S(2)}) collective-permute-start(bf16[1552,256]{1,0:T(8,128)(2,1)} %collective-permute-done.2.refs_6_), channel_id=1, source_target_pairs={{0,8},{4,12},{8,0},{12,4},{16,24},{20,28},{24,16},{28,20},{1,9},{5... | collective-permute-start | bytes 2383880 | tf_op jit(solution)/shard_map/ppermute | solution.py:362
  51.8 36.6 %copy-start.7 = (bf16[1552,256]{1,0:T(8,128)(2,1)}, bf16[1552,256]{1,0:T(8,128)(2,1)S(1)}, u32[]{:S(2)}) copy-start(bf16[1552,256]{1,0:T(8,128)(2,1)S(1)} %collective-permute-done.5.refs_7_) | copy-start | bytes 2383876
  51.8 18.6 %collective-permute-start.12 = (bf16[1552,256]{1,0:T(8,128)(2,1)}, bf16[1552,256]{1,0:T(8,128)(2,1)S(1)}, u32[]{:S(2)}, u32[]{:S(2)}) collective-permute-start(bf16[1552,256]{1,0:T(8,128)(2,1)} %broadcast_select_fusion), channel_id=1, source_target_pairs={{0,16},{4,20},{8,24},{12,28},{16,0},{20,4},{24,8},{28,12},{1,17},{... | collective-permute-start | bytes 2383880 | tf_op jit(solution)/shard_map/ppermute | solution.py:362
  52.3 18.6 %collective-permute-start.16 = (bf16[1552,256]{1,0:T(8,128)(2,1)}, bf16[1552,256]{1,0:T(8,128)(2,1)S(1)}, u32[]{:S(2)}, u32[]{:S(2)}) collective-permute-start(bf16[1552,256]{1,0:T(8,128)(2,1)} %collective-permute-done.6.refs_9_), channel_id=1, source_target_pairs={{1,2},{2,1},{5,6},{6,5},{9,10},{10,9},{13,14},{14,13},{17,18},{18,... | collective-permute-start | bytes 2383880 | tf_op jit(solution)/shard_map/ppermute | solution.py:367
  69.7 18.7 %copy-start.5 = (bf16[1552,256]{1,0:T(8,128)(2,1)}, bf16[1552,256]{1,0:T(8,128)(2,1)S(1)}, u32[]{:S(2)}) copy-start(bf16[1552,256]{1,0:T(8,128)(2,1)S(1)} %collective-permute-done.9.refs_9_) | copy-start | bytes 2383876
  69.7 16.8 %collective-permute-start.17 = (bf16[1552,256]{1,0:T(8,128)(2,1)}, bf16[1552,256]{1,0:T(8,128)(2,1)S(1)}, u32[]{:S(2)}, u32[]{:S(2)}) collective-permute-start(bf16[1552,256]{1,0:T(8,128)(2,1)} %collective-permute-done.6.refs_9_), channel_id=1, source_target_pairs={{0,1},{1,0},{2,3},{3,2},{4,5},{5,4},{6,7},{7,6},{8,9},{9,8},{10,11... | collective-permute-start | bytes 2383880 | tf_op jit(solution)/shard_map/ppermute | solution.py:367
  69.8 18.6 %copy-start.8 = (bf16[1552,256]{1,0:T(8,128)(2,1)}, bf16[1552,256]{1,0:T(8,128)(2,1)S(1)}, u32[]{:S(2)}) copy-start(bf16[1552,256]{1,0:T(8,128)(2,1)S(1)} %collective-permute-done.10.refs_6_) | copy-start | bytes 2383876
  69.8 18.0 %collective-permute-start.11 = (bf16[1552,256]{1,0:T(8,128)(2,1)S(1)}, bf16[1552,256]{1,0:T(8,128)(2,1)S(1)}, u32[]{:S(2)}, u32[]{:S(2)}) collective-permute-start(bf16[1552,256]{1,0:T(8,128)(2,1)S(1)} %broadcast_select_fusion.1), channel_id=1, source_target_pairs={{0,8},{4,12},{8,0},{12,4},{16,24},{20,28},{24,16},{28,20},{1,9},{5... | collective-permute-start | bytes 2383880 | tf_op jit(solution)/shard_map/ppermute | solution.py:362
  70.4 18.0 %copy-start.9 = (bf16[1552,256]{1,0:T(8,128)(2,1)}, bf16[1552,256]{1,0:T(8,128)(2,1)S(1)}, u32[]{:S(2)}) copy-start(bf16[1552,256]{1,0:T(8,128)(2,1)S(1)} %collective-permute-done.12.refs_5_) | copy-start | bytes 2383876
  70.4 18.0 %collective-permute-start.13 = (bf16[1552,256]{1,0:T(8,128)(2,1)S(1)}, bf16[1552,256]{1,0:T(8,128)(2,1)S(1)}, u32[]{:S(2)}, u32[]{:S(2)}) collective-permute-start(bf16[1552,256]{1,0:T(8,128)(2,1)S(1)} %broadcast_select_fusion.1), channel_id=1, source_target_pairs={{0,16},{4,20},{8,24},{12,28},{16,0},{20,4},{24,8},{28,12},{1,17},{... | collective-permute-start | bytes 2383880 | tf_op jit(solution)/shard_map/ppermute | solution.py:362
  86.5 1.9 %copy-start.10 = (bf16[1552,256]{1,0:T(8,128)(2,1)}, bf16[1552,256]{1,0:T(8,128)(2,1)S(1)}, u32[]{:S(2)}) copy-start(bf16[1552,256]{1,0:T(8,128)(2,1)S(1)} %collective-permute-done.17.refs_7_) | copy-start | bytes 2383876
  86.5 17.5 %collective-permute-start.18 = (bf16[1552,256]{1,0:T(8,128)(2,1)S(1)}, bf16[1552,256]{1,0:T(8,128)(2,1)S(1)}, u32[]{:S(2)}, u32[]{:S(2)}) collective-permute-start(bf16[1552,256]{1,0:T(8,128)(2,1)S(1)} %collective-permute-done.16.refs_6_), channel_id=1, source_target_pairs={{1,0},{2,3},{5,4},{6,7},{9,8},{10,11},{13,12},{14,15},{17,16},{18,... | collective-permute-start | bytes 2383880 | tf_op jit(solution)/shard_map/ppermute | solution.py:367
  87.8 16.2 %collective-permute-start.15 = (bf16[1552,256]{1,0:T(8,128)(2,1)}, bf16[1552,256]{1,0:T(8,128)(2,1)S(1)}, u32[]{:S(2)}, u32[]{:S(2)}) collective-permute-start(bf16[1552,256]{1,0:T(8,128)(2,1)} %broadcast_select_fusion), channel_id=1, source_target_pairs={{0,8},{4,12},{8,0},{12,4},{16,24},{20,28},{24,16},{28,20},{1,9},{5... | collective-permute-start | bytes 2383880 | tf_op jit(solution)/shard_map/ppermute | solution.py:362
  88.4 0.9 copy-start.11
  89.3 15.5 %collective-permute-start.14 = (bf16[1552,256]{1,0:T(8,128)(2,1)S(1)}, bf16[1552,256]{1,0:T(8,128)(2,1)}, u32[]{:S(2)}, u32[]{:S(2)}) collective-permute-start(bf16[1552,256]{1,0:T(8,128)(2,1)S(1)} %collective-permute-done.11.refs_3_), channel_id=1, source_target_pairs={{0,16},{4,20},{8,24},{12,28},{16,0},{20,4},{24,8},{28,12},{1,17},{... | collective-permute-start | bytes 2383880 | tf_op jit(solution)/shard_map/ppermute | solution.py:362
  108.3 3.7 %collective-permute-start.19 = (bf16[128,4096]{1,0:T(8,128)(2,1)S(1)}, bf16[128,4096]{1,0:T(8,128)(2,1)S(1)}, u32[]{:S(2)}, u32[]{:S(2)}) collective-permute-start(bf16[128,4096]{1,0:T(8,128)(2,1)S(1)} %get-tuple-element.62), channel_id=1, source_target_pairs={{0,4},{4,0},{8,12},{12,8},{16,20},{20,16},{24,28},{28,24},{1,5},{5... | collective-permute-start | bytes 3145736 | tf_op jit(solution)/shard_map/ppermute | solution.py:362
  108.4 4.1 %collective-permute-start.20 = (bf16[128,4096]{1,0:T(8,128)(2,1)S(1)}, bf16[128,4096]{1,0:T(8,128)(2,1)S(1)}, u32[]{:S(2)}, u32[]{:S(2)}) collective-permute-start(bf16[128,4096]{1,0:T(8,128)(2,1)S(1)} %get-tuple-element.63), channel_id=1, source_target_pairs={{0,4},{4,0},{8,12},{12,8},{16,20},{20,16},{24,28},{28,24},{1,5},{5... | collective-permute-start | bytes 3145736 | tf_op jit(solution)/shard_map/ppermute | solution.py:362

commit v5 on v4

--- a/solution.py
+++ b/solution.py
@@ -374,8 +374,8 @@
     mine, others = (0, rows), (rows, rows)
 
     own = with_labels(weights, block_index, block_counts)
-    x_own, y_own, near, beyond = x(own), y(own), line(own, ENDS), line(own, MIDDLE)
-    x_own, y_own, near, beyond = together(x_own, y_own, near, beyond)
+    near, x_own, beyond, y_own = line(own, ENDS), x(own), line(own, MIDDLE), y(own)
+    near, x_own, beyond, y_own = together(near, x_own, beyond, y_own)
     both = jnp.concatenate([tokens, cotangent], axis=0)
 
     out1, in1 = line(beyond, OUTWARD), line(near, MIDDLE)

time: 115 us -> 114 us (level)
  waiting for transfers between devices: 66.6 us -> 62.4 us
  starting transfers between devices: 17.4 us -> 21.2 us
    ppermute x13, waiting for transfers between devices: 16.8 us -> 4.03 us  [across(): return lax.ppermute(value, 'wide', [(i, i ^ bit) for i in range(wide)])]
    ppermute x8, waiting for transfers between devices: 49.8 us -> 58.4 us  [line(): return lax.ppermute(value, 'narrow', pairs)]
    ppermute x13, starting transfers between devices: 9.88 us -> 12.1 us  [across(): return lax.ppermute(value, 'wide', [(i, i ^ bit) for i in range(wide)])]
    ppermute x8, starting transfers between devices: 7.55 us -> 9.05 us  [line(): return lax.ppermute(value, 'narrow', pairs)]
  transfers between devices with their start and end apart: 21 -> 21, of which waited for: 9 -> 7; matrix products, arithmetic and copies ran while one was open for 3% -> 3% of each run, Pallas kernels for 15% -> 15%
where the time goes in v5:
time: 114 us
  waiting for transfers between devices  62.4 us (55%)
  Pallas kernels  21.6 us (19%)
  starting transfers between devices  21.2 us (19%)
  other arithmetic  5.83 us (5%)
  between operations  1.79 us (2%)
    ppermute x8, waiting for transfers between devices, line(): return lax.ppermute(value, 'narrow', pairs)  58.4 us
    pallas_call x4, Pallas kernels, run_pairs(): pl.pallas_call(functools.partial(pairs_kernel, plan), out_shape=out_shape...  20.1 us
    ppermute x13, starting transfers between devices, across(): return lax.ppermute(value, 'wide', [(i, i ^ bit) for i in range(wide)])  12.1 us
    ppermute x8, starting transfers between devices, line(): return lax.ppermute(value, 'narrow', pairs)  9.05 us
    ppermute x13, waiting for transfers between devices, across(): return lax.ppermute(value, 'wide', [(i, i ^ bit) for i in range(wide)])  4.03 us
    concatenate x1, other arithmetic, body(): both = jnp.concatenate([tokens, cotangent], axis=0)  2.73 us
  transfers between devices with their start and end apart: 21, of which 7 were waited for; matrix products, arithmetic and copies ran while one was open for 3% of the time, Pallas kernels for 15%

profile of v5, /device:TPU:0, one launch (start us, length us, event | category | flops | bytes accessed | tf_op | source)
XLA Modules:
  0.0 113.7 jit_solution(2792597670981928229)
XLA Ops:
  0.6 0.0 copy-start
  1.4 0.7 add_convert_fusion
  2.1 1.2 %pad_maximum_fusion.1.refs_4_ = bf16[1552,256]{1,0:T(8,128)(2,1)S(1)} fusion(bf16[16,256]{1,0:T(8,128)(2,1)S(1)} %add_convert_fusion, bf16[1536,256]{1,0:T(8,128)(2,1)} %bitcast.5), kind=kLoop, calls=%fused_computation.1 | loop fusion | flops 1589248 | bytes 1589248 | tf_op jit(solution)/shard_map/concatenate | solution.py:84
  3.3 0.0 copy-start.1
  3.3 3.1 %collective-permute-start = (bf16[1552,256]{1,0:T(8,128)(2,1)S(1)}, bf16[1552,256]{1,0:T(8,128)(2,1)}, u32[]{:S(2)}, u32[]{:S(2)}) collective-permute-start(bf16[1552,256]{1,0:T(8,128)(2,1)S(1)} %pad_maximum_fusion.1.refs_4_), channel_id=1, source_target_pairs={{0,1},{1,0},{2,3},{3,2},{4,5},{5,4},{6,7},{7,6},{8,9},{9,8},{10,11... | collective-permute-start | bytes 2383880 | tf_op jit(solution)/shard_map/ppermute | solution.py:367
  6.4 1.5 %collective-permute-start.1 = (bf16[1552,256]{1,0:T(8,128)(2,1)S(1)}, bf16[1552,256]{1,0:T(8,128)(2,1)S(1)}, u32[]{:S(2)}, u32[]{:S(2)}) collective-permute-start(bf16[1552,256]{1,0:T(8,128)(2,1)S(1)} %pad_maximum_fusion.1.refs_4_), channel_id=1, source_target_pairs={{0,8},{4,12},{8,0},{12,4},{16,24},{20,28},{24,16},{28,20},{1,9},{5... | collective-permute-start | bytes 2383880 | tf_op jit(solution)/shard_map/ppermute | solution.py:362
  7.9 0.7 collective-permute-start.2
  8.6 1.6 %collective-permute-start.3 = (bf16[1552,256]{1,0:T(8,128)(2,1)S(1)}, bf16[1552,256]{1,0:T(8,128)(2,1)}, u32[]{:S(2)}, u32[]{:S(2)}) collective-permute-start(bf16[1552,256]{1,0:T(8,128)(2,1)S(1)} %pad_maximum_fusion.1.refs_4_), channel_id=1, source_target_pairs={{0,16},{4,20},{8,24},{12,28},{16,0},{20,4},{24,8},{28,12},{1,17},{... | collective-permute-start | bytes 2383880 | tf_op jit(solution)/shard_map/ppermute | solution.py:362
  10.2 14.0 %collective-permute-done.refs_6_ = bf16[1552,256]{1,0:T(8,128)(2,1)} collective-permute-done((bf16[1552,256]{1,0:T(8,128)(2,1)S(1)}, bf16[1552,256]{1,0:T(8,128)(2,1)}, u32[]{:S(2)}, u32[]{:S(2)}) %collective-permute-start) | collective-permute-done | bytes 794656 | tf_op jit(solution)/shard_map/ppermute | solution.py:367
  24.2 1.4 %collective-permute-done.1.refs_8_ = bf16[1552,256]{1,0:T(8,128)(2,1)S(1)} collective-permute-done((bf16[1552,256]{1,0:T(8,128)(2,1)S(1)}, bf16[1552,256]{1,0:T(8,128)(2,1)S(1)}, u32[]{:S(2)}, u32[]{:S(2)}) %collective-permute-start.1) | collective-permute-done | bytes 794656 | tf_op jit(solution)/shard_map/ppermute | solution.py:362
  25.6 2.1 %collective-permute-done.3.refs_5_ = bf16[1552,256]{1,0:T(8,128)(2,1)} collective-permute-done((bf16[1552,256]{1,0:T(8,128)(2,1)S(1)}, bf16[1552,256]{1,0:T(8,128)(2,1)}, u32[]{:S(2)}, u32[]{:S(2)}) %collective-permute-start.3) | collective-permute-done | bytes 794656 | tf_op jit(solution)/shard_map/ppermute | solution.py:362
  27.7 1.3 %collective-permute-start.8 = (bf16[1552,256]{1,0:T(8,128)(2,1)S(1)}, bf16[1552,256]{1,0:T(8,128)(2,1)S(1)}, u32[]{:S(2)}, u32[]{:S(2)}) collective-permute-start(bf16[1552,256]{1,0:T(8,128)(2,1)S(1)} %collective-permute-done.2.refs_3_), channel_id=1, source_target_pairs={{1,0},{2,3},{5,4},{6,7},{9,8},{10,11},{13,12},{14,15},{17,16},{18,... | collective-permute-start | bytes 2383880 | tf_op jit(solution)/shard_map/ppermute | solution.py:367
  29.0 0.7 collective-permute-start.7
  29.7 0.6 collective-permute-start.6
  30.3 1.5 %collective-permute-start.5 = (bf16[1552,256]{1,0:T(8,128)(2,1)}, bf16[1552,256]{1,0:T(8,128)(2,1)S(1)}, u32[]{:S(2)}, u32[]{:S(2)}) collective-permute-start(bf16[1552,256]{1,0:T(8,128)(2,1)} %collective-permute-done.refs_6_), channel_id=1, source_target_pairs={{0,16},{4,20},{8,24},{12,28},{16,0},{20,4},{24,8},{28,12},{1,17},{... | collective-permute-start | bytes 2383880 | tf_op jit(solution)/shard_map/ppermute | solution.py:362
  31.8 2.7 %pad_maximum_fusion = bf16[256,4096]{1,0:T(8,128)(2,1)} fusion(bf16[128,4096]{1,0:T(8,128)(2,1)} %refs_2_.1, bf16[128,4096]{1,0:T(8,128)(2,1)S(1)} %copy-done), kind=kLoop, calls=%fused_computation | loop fusion | flops 4194304 | bytes 4194304 | tf_op jit(solution)/shard_map/concatenate | solution.py:379
  34.6 0.0 collective-permute-start.4
  34.6 14.4 %collective-permute-done.8.refs_4_ = bf16[1552,256]{1,0:T(8,128)(2,1)S(1)} collective-permute-done((bf16[1552,256]{1,0:T(8,128)(2,1)S(1)}, bf16[1552,256]{1,0:T(8,128)(2,1)S(1)}, u32[]{:S(2)}, u32[]{:S(2)}) %collective-permute-start.8) | collective-permute-done | bytes 794656 | tf_op jit(solution)/shard_map/ppermute | solution.py:367
  49.0 0.0 collective-permute-done.7.refs_8_
  49.0 1.3 %collective-permute-start.9 = (bf16[1552,256]{1,0:T(8,128)(2,1)S(1)}, bf16[1552,256]{1,0:T(8,128)(2,1)S(1)}, u32[]{:S(2)}, u32[]{:S(2)}) collective-permute-start(bf16[1552,256]{1,0:T(8,128)(2,1)S(1)} %collective-permute-done.7.refs_8_), channel_id=1, source_target_pairs={{1,0},{2,3},{5,4},{6,7},{9,8},{10,11},{13,12},{14,15},{17,16},{18,... | collective-permute-start | bytes 2383880 | tf_op jit(solution)/shard_map/ppermute | solution.py:367
  50.3 0.6 collective-permute-start.10
  50.9 1.0 broadcast_select_fusion
  51.9 1.5 %collective-permute-start.12 = (bf16[1552,256]{1,0:T(8,128)(2,1)}, bf16[1552,256]{1,0:T(8,128)(2,1)S(1)}, u32[]{:S(2)}, u32[]{:S(2)}) collective-permute-start(bf16[1552,256]{1,0:T(8,128)(2,1)} %broadcast_select_fusion), channel_id=1, source_target_pairs={{0,16},{4,20},{8,24},{12,28},{16,0},{20,4},{24,8},{28,12},{1,17},{... | collective-permute-start | bytes 2383880 | tf_op jit(solution)/shard_map/ppermute | solution.py:362
  53.4 0.7 collective-permute-start.16
  54.1 15.7 %collective-permute-done.9.refs_9_ = bf16[1552,256]{1,0:T(8,128)(2,1)S(1)} collective-permute-done((bf16[1552,256]{1,0:T(8,128)(2,1)S(1)}, bf16[1552,256]{1,0:T(8,128)(2,1)S(1)}, u32[]{:S(2)}, u32[]{:S(2)}) %collective-permute-start.9) | collective-permute-done | bytes 794656 | tf_op jit(solution)/shard_map/ppermute | solution.py:367
  69.8 0.0 collective-permute-start.17
  69.8 0.1 broadcast_select_fusion.1
  69.9 0.6 collective-permute-start.11
  70.5 0.0 collective-permute-done.12.refs_5_
  70.6 1.5 %collective-permute-start.13 = (bf16[1552,256]{1,0:T(8,128)(2,1)S(1)}, bf16[1552,256]{1,0:T(8,128)(2,1)S(1)}, u32[]{:S(2)}, u32[]{:S(2)}) collective-permute-start(bf16[1552,256]{1,0:T(8,128)(2,1)S(1)} %broadcast_select_fusion.1), channel_id=1, source_target_pairs={{0,16},{4,20},{8,24},{12,28},{16,0},{20,4},{24,8},{28,12},{1,17},{... | collective-permute-start | bytes 2383880 | tf_op jit(solution)/shard_map/ppermute | solution.py:362
  72.1 0.0 collective-permute-done.16.refs_6_
  72.1 14.2 %collective-permute-done.17.refs_7_ = bf16[1552,256]{1,0:T(8,128)(2,1)S(1)} collective-permute-done((bf16[1552,256]{1,0:T(8,128)(2,1)}, bf16[1552,256]{1,0:T(8,128)(2,1)S(1)}, u32[]{:S(2)}, u32[]{:S(2)}) %collective-permute-start.17) | collective-permute-done | bytes 794656 | tf_op jit(solution)/shard_map/ppermute | solution.py:367
  86.3 1.3 %collective-permute-start.18 = (bf16[1552,256]{1,0:T(8,128)(2,1)S(1)}, bf16[1552,256]{1,0:T(8,128)(2,1)S(1)}, u32[]{:S(2)}, u32[]{:S(2)}) collective-permute-start(bf16[1552,256]{1,0:T(8,128)(2,1)S(1)} %collective-permute-done.16.refs_6_), channel_id=1, source_target_pairs={{1,0},{2,3},{5,4},{6,7},{9,8},{10,11},{13,12},{14,15},{17,16},{18,... | collective-permute-start | bytes 2383880 | tf_op jit(solution)/shard_map/ppermute | solution.py:367
  87.6 0.6 collective-permute-start.15
  88.2 0.0 collective-permute-done.13.refs_10_
  88.3 0.9 copy-done.11
  89.2 1.5 %collective-permute-start.14 = (bf16[1552,256]{1,0:T(8,128)(2,1)S(1)}, bf16[1552,256]{1,0:T(8,128)(2,1)}, u32[]{:S(2)}, u32[]{:S(2)}) collective-permute-start(bf16[1552,256]{1,0:T(8,128)(2,1)S(1)} %collective-permute-done.11.refs_3_), channel_id=1, source_target_pairs={{0,16},{4,20},{8,24},{12,28},{16,0},{20,4},{24,8},{28,12},{1,17},{... | collective-permute-start | bytes 2383880 | tf_op jit(solution)/shard_map/ppermute | solution.py:362
  90.7 0.1 pad_add_fusion.refs_0_
  90.8 7.9 %shard_map.68 = (bf16[256,4096]{1,0:T(8,128)(2,1)S(1)}, bf16[256,4096]{1,0:T(8,128)(2,1)S(1)}, f32[128,4096]{1,0:T(8,128)S(1)}, f32[128,4096]{1,0:T(8,128)S(1)},...) custom-call(s32[2]{0:T(128)S(1)} %pad_add_fusion.refs_0_, bf16[128,4096]{1,0:T(8,128)(2,1)} %refs_1_.1, ...), custom_call_target="tpu_custom_call" | custom-call | flops 2415919104 | bytes 4718592 | tf_op jit(solution)/shard_map/pallas_call | solution.py:268
  98.6 5.7 %shard_map.69 = (f32[128,4096]{1,0:T(8,128)S(1)}, f32[128,4096]{1,0:T(8,128)S(1)}, f32[128,4096]{1,0:T(8,128)S(1)}, f32[128,4096]{1,0:T(8,128)S(1)}) custom-call(s32[2]{0:T(128)S(1)} %pad_add_fusion.refs_0_, bf16[256,4096]{1,0:T(8,128)(2,1)S(1)} %get-tuple-element.39.refs_1_, ...), custom_call_target="tpu_custom_call", output_to_operand_aliasing={{0}: (11, {}), {1}: (12, {}), {2}: (13, {}), {3}: (14, {})} | custom-call | flops 2415919104 | bytes 4718592 | tf_op jit(solution)/shard_map/pallas_call | solution.py:268
  104.4 0.0 collective-permute-done.18.refs_7_
  104.4 0.0 collective-permute-done.14.refs_4_
  104.4 3.5 %shard_map.71 = (f32[128,4096]{1,0:T(8,128)S(1)}, f32[128,4096]{1,0:T(8,128)S(1)}, bf16[128,4096]{1,0:T(8,128)(2,1)S(1)}, bf16[128,4096]{1,0:T(8,128)(2,1)S(1)}) custom-call(s32[2]{0:T(128)S(1)} %pad_add_fusion.refs_0_, bf16[256,4096]{1,0:T(8,128)(2,1)S(1)} %get-tuple-element.39.refs_1_, ...), custom_call_target="tpu_custom_call", output_to_operand_aliasing={{0}: (8, {}), {1}: (9, {})} | custom-call | flops 805306368 | bytes 3145728 | tf_op jit(solution)/shard_map/pallas_call | solution.py:268
  107.9 0.1 collective-permute-start.19
  108.0 0.5 collective-permute-start.20
  108.5 3.1 %shard_map.70 = (f32[128,4096]{1,0:T(8,128)S(1)}, f32[128,4096]{1,0:T(8,128)S(1)}) custom-call(s32[2]{0:T(128)S(1)} %pad_add_fusion.refs_0_, bf16[256,4096]{1,0:T(8,128)(2,1)S(1)} %get-tuple-element.39.refs_1_, bf16[256,4096]{1,0:T(8,128)(2,1)S(1)} %get-tuple-element.40.refs_2_, ...), custom_call_target="tpu_custom_call", output_to_operand_aliasing={{0}: (8, {}), {1}: (9, {})} | custom-call | flops 805306368 | bytes 3145728 | tf_op jit(solution)/shard_map/pallas_call | solution.py:268
  111.6 0.6 collective-permute-done.20.refs_3_
  112.1 1.4 %shard_map.72 = (bf16[128,4096]{1,0:T(8,128)(2,1)}, bf16[128,4096]{1,0:T(8,128)(2,1)}) custom-call(f32[128,4096]{1,0:T(8,128)S(1)} %get-tuple-element.58.refs_0_, f32[128,4096]{1,0:T(8,128)S(1)} %get-tuple-element.59.refs_1_, bf16[128,4096]{1,0:T(8,128)(2,1)S(1)} %collective-permute-done.19.refs_2_, bf16[128,4096]{1,0:T(8,128)(2,1)S(1)} %collective-permute-done.20.refs_3_), custom_call_target="tpu_custom_call" | custom-call | tf_op jit(solution)/shard_map/pallas_call | solution.py:107
  (31 shorter events, 0.1 us)
Async XLA Ops:
  0.6 31.2 %copy-start = (bf16[128,4096]{1,0:T(8,128)(2,1)S(1)}, bf16[128,4096]{1,0:T(8,128)(2,1)}, u32[]{:S(2)}) copy-start(bf16[128,4096]{1,0:T(8,128)(2,1)} %refs_1_.1) | copy-start | bytes 3145732
  3.3 5.3 %copy-start.1 = (bf16[1552,256]{1,0:T(8,128)(2,1)}, bf16[1552,256]{1,0:T(8,128)(2,1)S(1)}, u32[]{:S(2)}) copy-start(bf16[1552,256]{1,0:T(8,128)(2,1)S(1)} %pad_maximum_fusion.1.refs_4_) | copy-start | bytes 2383876
  3.3 20.9 %collective-permute-start = (bf16[1552,256]{1,0:T(8,128)(2,1)S(1)}, bf16[1552,256]{1,0:T(8,128)(2,1)}, u32[]{:S(2)}, u32[]{:S(2)}) collective-permute-start(bf16[1552,256]{1,0:T(8,128)(2,1)S(1)} %pad_maximum_fusion.1.refs_4_), channel_id=1, source_target_pairs={{0,1},{1,0},{2,3},{3,2},{4,5},{5,4},{6,7},{7,6},{8,9},{9,8},{10,11... | collective-permute-start | bytes 2383880 | tf_op jit(solution)/shard_map/ppermute | solution.py:367
  6.4 19.2 %collective-permute-start.1 = (bf16[1552,256]{1,0:T(8,128)(2,1)S(1)}, bf16[1552,256]{1,0:T(8,128)(2,1)S(1)}, u32[]{:S(2)}, u32[]{:S(2)}) collective-permute-start(bf16[1552,256]{1,0:T(8,128)(2,1)S(1)} %pad_maximum_fusion.1.refs_4_), channel_id=1, source_target_pairs={{0,8},{4,12},{8,0},{12,4},{16,24},{20,28},{24,16},{28,20},{1,9},{5... | collective-permute-start | bytes 2383880 | tf_op jit(solution)/shard_map/ppermute | solution.py:362
  7.9 17.7 %collective-permute-start.2 = (bf16[1552,256]{1,0:T(8,128)(2,1)S(1)}, bf16[1552,256]{1,0:T(8,128)(2,1)S(1)}, u32[]{:S(2)}, u32[]{:S(2)}) collective-permute-start(bf16[1552,256]{1,0:T(8,128)(2,1)S(1)} %pad_maximum_fusion.1.refs_4_), channel_id=1, source_target_pairs={{1,2},{2,1},{5,6},{6,5},{9,10},{10,9},{13,14},{14,13},{17,18},{18,... | collective-permute-start | bytes 2383880 | tf_op jit(solution)/shard_map/ppermute | solution.py:367
  8.6 19.1 %collective-permute-start.3 = (bf16[1552,256]{1,0:T(8,128)(2,1)S(1)}, bf16[1552,256]{1,0:T(8,128)(2,1)}, u32[]{:S(2)}, u32[]{:S(2)}) collective-permute-start(bf16[1552,256]{1,0:T(8,128)(2,1)S(1)} %pad_maximum_fusion.1.refs_4_), channel_id=1, source_target_pairs={{0,16},{4,20},{8,24},{12,28},{16,0},{20,4},{24,8},{28,12},{1,17},{... | collective-permute-start | bytes 2383880 | tf_op jit(solution)/shard_map/ppermute | solution.py:362
  25.6 2.1 %copy-start.6 = (bf16[1552,256]{1,0:T(8,128)(2,1)}, bf16[1552,256]{1,0:T(8,128)(2,1)S(1)}, u32[]{:S(2)}) copy-start(bf16[1552,256]{1,0:T(8,128)(2,1)S(1)} %collective-permute-done.1.refs_8_) | copy-start | bytes 2383876
  25.6 25.3 %copy-start.2 = (bf16[1552,256]{1,0:T(8,128)(2,1)}, bf16[1552,256]{1,0:T(8,128)(2,1)S(1)}, u32[]{:S(2)}) copy-start(bf16[1552,256]{1,0:T(8,128)(2,1)S(1)} %collective-permute-done.2.refs_3_) | copy-start | bytes 2383876
  27.7 21.3 %collective-permute-start.8 = (bf16[1552,256]{1,0:T(8,128)(2,1)S(1)}, bf16[1552,256]{1,0:T(8,128)(2,1)S(1)}, u32[]{:S(2)}, u32[]{:S(2)}) collective-permute-start(bf16[1552,256]{1,0:T(8,128)(2,1)S(1)} %collective-permute-done.2.refs_3_), channel_id=1, source_target_pairs={{1,0},{2,3},{5,4},{6,7},{9,8},{10,11},{13,12},{14,15},{17,16},{18,... | collective-permute-start | bytes 2383880 | tf_op jit(solution)/shard_map/ppermute | solution.py:367
  29.0 20.0 %collective-permute-start.7 = (bf16[1552,256]{1,0:T(8,128)(2,1)}, bf16[1552,256]{1,0:T(8,128)(2,1)S(1)}, u32[]{:S(2)}, u32[]{:S(2)}) collective-permute-start(bf16[1552,256]{1,0:T(8,128)(2,1)} %collective-permute-done.refs_6_), channel_id=1, source_target_pairs={{1,2},{2,1},{5,6},{6,5},{9,10},{10,9},{13,14},{14,13},{17,18},{18,... | collective-permute-start | bytes 2383880 | tf_op jit(solution)/shard_map/ppermute | solution.py:367
  29.7 20.6 %collective-permute-start.6 = (bf16[1552,256]{1,0:T(8,128)(2,1)}, bf16[1552,256]{1,0:T(8,128)(2,1)}, u32[]{:S(2)}, u32[]{:S(2)}) collective-permute-start(bf16[1552,256]{1,0:T(8,128)(2,1)} %collective-permute-done.3.refs_5_), channel_id=1, source_target_pairs={{0,8},{4,12},{8,0},{12,4},{16,24},{20,28},{24,16},{28,20},{1,9},{5... | collective-permute-start | bytes 2383880 | tf_op jit(solution)/shard_map/ppermute | solution.py:362
  30.3 21.6 %collective-permute-start.5 = (bf16[1552,256]{1,0:T(8,128)(2,1)}, bf16[1552,256]{1,0:T(8,128)(2,1)S(1)}, u32[]{:S(2)}, u32[]{:S(2)}) collective-permute-start(bf16[1552,256]{1,0:T(8,128)(2,1)} %collective-permute-done.refs_6_), channel_id=1, source_target_pairs={{0,16},{4,20},{8,24},{12,28},{16,0},{20,4},{24,8},{28,12},{1,17},{... | collective-permute-start | bytes 2383880 | tf_op jit(solution)/shard_map/ppermute | solution.py:362
  34.6 56.2 %collective-permute-start.4 = (bf16[256,4096]{1,0:T(8,128)(2,1)}, bf16[256,4096]{1,0:T(8,128)(2,1)}, u32[]{:S(2)}, u32[]{:S(2)}) collective-permute-start(bf16[256,4096]{1,0:T(8,128)(2,1)} %pad_maximum_fusion), channel_id=1, source_target_pairs={{0,4},{4,0},{8,12},{12,8},{16,20},{20,16},{24,28},{28,24},{1,5},{5... | collective-permute-start | bytes 6291464 | tf_op jit(solution)/shard_map/ppermute | solution.py:362
  49.0 20.9 %copy-start.3 = (bf16[1552,256]{1,0:T(8,128)(2,1)}, bf16[1552,256]{1,0:T(8,128)(2,1)S(1)}, u32[]{:S(2)}) copy-start(bf16[1552,256]{1,0:T(8,128)(2,1)S(1)} %collective-permute-done.8.refs_4_) | copy-start | bytes 2383876
  49.0 20.9 %copy-start.4 = (bf16[1552,256]{1,0:T(8,128)(2,1)}, bf16[1552,256]{1,0:T(8,128)(2,1)S(1)}, u32[]{:S(2)}) copy-start(bf16[1552,256]{1,0:T(8,128)(2,1)S(1)} %collective-permute-done.7.refs_8_) | copy-start | bytes 2383876
  49.0 20.8 %collective-permute-start.9 = (bf16[1552,256]{1,0:T(8,128)(2,1)S(1)}, bf16[1552,256]{1,0:T(8,128)(2,1)S(1)}, u32[]{:S(2)}, u32[]{:S(2)}) collective-permute-start(bf16[1552,256]{1,0:T(8,128)(2,1)S(1)} %collective-permute-done.7.refs_8_), channel_id=1, source_target_pairs={{1,0},{2,3},{5,4},{6,7},{9,8},{10,11},{13,12},{14,15},{17,16},{18,... | collective-permute-start | bytes 2383880 | tf_op jit(solution)/shard_map/ppermute | solution.py:367
  50.3 19.6 %collective-permute-start.10 = (bf16[1552,256]{1,0:T(8,128)(2,1)}, bf16[1552,256]{1,0:T(8,128)(2,1)S(1)}, u32[]{:S(2)}, u32[]{:S(2)}) collective-permute-start(bf16[1552,256]{1,0:T(8,128)(2,1)} %collective-permute-done.refs_6_), channel_id=1, source_target_pairs={{0,8},{4,12},{8,0},{12,4},{16,24},{20,28},{24,16},{28,20},{1,9},{5... | collective-permute-start | bytes 2383880 | tf_op jit(solution)/shard_map/ppermute | solution.py:362
  51.9 36.3 %copy-start.7 = (bf16[1552,256]{1,0:T(8,128)(2,1)}, bf16[1552,256]{1,0:T(8,128)(2,1)S(1)}, u32[]{:S(2)}) copy-start(bf16[1552,256]{1,0:T(8,128)(2,1)S(1)} %collective-permute-done.5.refs_7_) | copy-start | bytes 2383876
  51.9 18.6 %collective-permute-start.12 = (bf16[1552,256]{1,0:T(8,128)(2,1)}, bf16[1552,256]{1,0:T(8,128)(2,1)S(1)}, u32[]{:S(2)}, u32[]{:S(2)}) collective-permute-start(bf16[1552,256]{1,0:T(8,128)(2,1)} %broadcast_select_fusion), channel_id=1, source_target_pairs={{0,16},{4,20},{8,24},{12,28},{16,0},{20,4},{24,8},{28,12},{1,17},{... | collective-permute-start | bytes 2383880 | tf_op jit(solution)/shard_map/ppermute | solution.py:362
  53.4 18.6 %collective-permute-start.16 = (bf16[1552,256]{1,0:T(8,128)(2,1)}, bf16[1552,256]{1,0:T(8,128)(2,1)S(1)}, u32[]{:S(2)}, u32[]{:S(2)}) collective-permute-start(bf16[1552,256]{1,0:T(8,128)(2,1)} %collective-permute-done.6.refs_9_), channel_id=1, source_target_pairs={{1,2},{2,1},{5,6},{6,5},{9,10},{10,9},{13,14},{14,13},{17,18},{18,... | collective-permute-start | bytes 2383880 | tf_op jit(solution)/shard_map/ppermute | solution.py:367
  69.8 18.4 %copy-start.5 = (bf16[1552,256]{1,0:T(8,128)(2,1)}, bf16[1552,256]{1,0:T(8,128)(2,1)S(1)}, u32[]{:S(2)}) copy-start(bf16[1552,256]{1,0:T(8,128)(2,1)S(1)} %collective-permute-done.9.refs_9_) | copy-start | bytes 2383876
  69.8 16.5 %collective-permute-start.17 = (bf16[1552,256]{1,0:T(8,128)(2,1)}, bf16[1552,256]{1,0:T(8,128)(2,1)S(1)}, u32[]{:S(2)}, u32[]{:S(2)}) collective-permute-start(bf16[1552,256]{1,0:T(8,128)(2,1)} %collective-permute-done.6.refs_9_), channel_id=1, source_target_pairs={{0,1},{1,0},{2,3},{3,2},{4,5},{5,4},{6,7},{7,6},{8,9},{9,8},{10,11... | collective-permute-start | bytes 2383880 | tf_op jit(solution)/shard_map/ppermute | solution.py:367
  69.9 18.3 %copy-start.8 = (bf16[1552,256]{1,0:T(8,128)(2,1)}, bf16[1552,256]{1,0:T(8,128)(2,1)S(1)}, u32[]{:S(2)}) copy-start(bf16[1552,256]{1,0:T(8,128)(2,1)S(1)} %collective-permute-done.10.refs_6_) | copy-start | bytes 2383876
  69.9 17.7 %collective-permute-start.11 = (bf16[1552,256]{1,0:T(8,128)(2,1)S(1)}, bf16[1552,256]{1,0:T(8,128)(2,1)S(1)}, u32[]{:S(2)}, u32[]{:S(2)}) collective-permute-start(bf16[1552,256]{1,0:T(8,128)(2,1)S(1)} %broadcast_select_fusion.1), channel_id=1, source_target_pairs={{0,8},{4,12},{8,0},{12,4},{16,24},{20,28},{24,16},{28,20},{1,9},{5... | collective-permute-start | bytes 2383880 | tf_op jit(solution)/shard_map/ppermute | solution.py:362
  70.6 17.7 %copy-start.9 = (bf16[1552,256]{1,0:T(8,128)(2,1)}, bf16[1552,256]{1,0:T(8,128)(2,1)S(1)}, u32[]{:S(2)}) copy-start(bf16[1552,256]{1,0:T(8,128)(2,1)S(1)} %collective-permute-done.12.refs_5_) | copy-start | bytes 2383876
  70.6 17.7 %collective-permute-start.13 = (bf16[1552,256]{1,0:T(8,128)(2,1)S(1)}, bf16[1552,256]{1,0:T(8,128)(2,1)S(1)}, u32[]{:S(2)}, u32[]{:S(2)}) collective-permute-start(bf16[1552,256]{1,0:T(8,128)(2,1)S(1)} %broadcast_select_fusion.1), channel_id=1, source_target_pairs={{0,16},{4,20},{8,24},{12,28},{16,0},{20,4},{24,8},{28,12},{1,17},{... | collective-permute-start | bytes 2383880 | tf_op jit(solution)/shard_map/ppermute | solution.py:362
  86.3 1.9 %copy-start.10 = (bf16[1552,256]{1,0:T(8,128)(2,1)}, bf16[1552,256]{1,0:T(8,128)(2,1)S(1)}, u32[]{:S(2)}) copy-start(bf16[1552,256]{1,0:T(8,128)(2,1)S(1)} %collective-permute-done.17.refs_7_) | copy-start | bytes 2383876
  86.3 18.0 %collective-permute-start.18 = (bf16[1552,256]{1,0:T(8,128)(2,1)S(1)}, bf16[1552,256]{1,0:T(8,128)(2,1)S(1)}, u32[]{:S(2)}, u32[]{:S(2)}) collective-permute-start(bf16[1552,256]{1,0:T(8,128)(2,1)S(1)} %collective-permute-done.16.refs_6_), channel_id=1, source_target_pairs={{1,0},{2,3},{5,4},{6,7},{9,8},{10,11},{13,12},{14,15},{17,16},{18,... | collective-permute-start | bytes 2383880 | tf_op jit(solution)/shard_map/ppermute | solution.py:367
  87.6 16.8 %collective-permute-start.15 = (bf16[1552,256]{1,0:T(8,128)(2,1)}, bf16[1552,256]{1,0:T(8,128)(2,1)S(1)}, u32[]{:S(2)}, u32[]{:S(2)}) collective-permute-start(bf16[1552,256]{1,0:T(8,128)(2,1)} %broadcast_select_fusion), channel_id=1, source_target_pairs={{0,8},{4,12},{8,0},{12,4},{16,24},{20,28},{24,16},{28,20},{1,9},{5... | collective-permute-start | bytes 2383880 | tf_op jit(solution)/shard_map/ppermute | solution.py:362
  88.3 0.9 copy-start.11
  89.2 15.2 %collective-permute-start.14 = (bf16[1552,256]{1,0:T(8,128)(2,1)S(1)}, bf16[1552,256]{1,0:T(8,128)(2,1)}, u32[]{:S(2)}, u32[]{:S(2)}) collective-permute-start(bf16[1552,256]{1,0:T(8,128)(2,1)S(1)} %collective-permute-done.11.refs_3_), channel_id=1, source_target_pairs={{0,16},{4,20},{8,24},{12,28},{16,0},{20,4},{24,8},{28,12},{1,17},{... | collective-permute-start | bytes 2383880 | tf_op jit(solution)/shard_map/ppermute | solution.py:362
  107.9 3.7 %collective-permute-start.19 = (bf16[128,4096]{1,0:T(8,128)(2,1)S(1)}, bf16[128,4096]{1,0:T(8,128)(2,1)S(1)}, u32[]{:S(2)}, u32[]{:S(2)}) collective-permute-start(bf16[128,4096]{1,0:T(8,128)(2,1)S(1)} %get-tuple-element.62), channel_id=1, source_target_pairs={{0,4},{4,0},{8,12},{12,8},{16,20},{20,16},{24,28},{28,24},{1,5},{5... | collective-permute-start | bytes 3145736 | tf_op jit(solution)/shard_map/ppermute | solution.py:362
  108.0 4.1 %collective-permute-start.20 = (bf16[128,4096]{1,0:T(8,128)(2,1)S(1)}, bf16[128,4096]{1,0:T(8,128)(2,1)S(1)}, u32[]{:S(2)}, u32[]{:S(2)}) collective-permute-start(bf16[128,4096]{1,0:T(8,128)(2,1)S(1)} %get-tuple-element.63), channel_id=1, source_target_pairs={{0,4},{4,0},{8,12},{12,8},{16,20},{20,16},{24,28},{28,24},{1,5},{5... | collective-permute-start | bytes 3145736 | tf_op jit(solution)/shard_map/ppermute | solution.py:362
